TPU v7x, 128 devices: a whole 4x4x4 slice. The times are simulated.
128 devices in a mesh: gx: 16 (over z, x_hi, core), gy: 8 (over x_lo, y).
Axes of the slice: x: 4 (x_hi: 2, x_lo: 2; x = x_hi * 2 + x_lo), y: 4, z: 4, core: 2. Of those that a mesh axis runs over, the one named last changes fastest.
Arguments:
- grid_field: bfloat16 [1, 20, 2048, 2048], P(None, None, 'gx', 'gy'), may hold values from -8 to 8
- spectral_weight: float32 [2, 2, 20, 20, 2048], P(None, None, None, None, ('gx', 'gy')), may hold values from -1 to 1
- conv_near: bfloat16 [2, 20, 180], replicated, may hold values from -0.4375 to 0.4375
- conv_far: bfloat16 [2, 20, 500], replicated, may hold values from -0.25 to 0.25
- mix_logits: float32 [2, 3], replicated, may hold values from -1 to 1
- channel_bias: float32 [2, 20], replicated, may hold values from -3 to 3
Outputs:
- result_field: bfloat16 [1, 20, 2048, 2048], P(None, None, 'gx', 'gy')
All inputs are finite; a program needn't handle non-finite values.
Results may differ from a plain program's by a relative error of at most 0.004.
Values may be sent and summed in bfloat16 or wider, within the bound.
No kernel may reach another device: no remote copies, remote signals or barrier semaphores. Data moves between devices by JAX's collectives and lax.ppermute only.
A program may use at most 192 MiB of HBM per device.

v0:
```python
import math

import jax
import jax.numpy as jnp
from jax import lax
from jax.sharding import PartitionSpec as P

NX = 2048
NY = 2048
MX = 32
MY = 32
LAYERS = 2
KX = 64
MODES = 2048


full_turn = 2.0 * math.pi
highest = lax.Precision.HIGHEST


def padded_2(value, sides, width):
    for axis, dim in sides:
        size, length = (lax.axis_size(axis), value.shape[dim])
        up = [(i, (i + 1) % size) for i in range(size)]
        down = [(j, i) for i, j in up]
        last = lax.slice_in_dim(value, length - width, length, axis=dim)
        first = lax.slice_in_dim(value, 0, width, axis=dim)
        before = lax.ppermute(last, axis, up)
        after = lax.ppermute(first, axis, down)
        value = jnp.concatenate([before, value, after], axis=dim)
    return value


def forward_table(positions):
    col_modes = jnp.arange(MY, dtype=jnp.int32)
    phases = (positions[:, None] * col_modes[None, :] % NY).astype(jnp.float32) * (full_turn / NY)
    return jnp.concatenate([jnp.cos(phases), -jnp.sin(phases)], axis=1).astype(jnp.bfloat16)


def row_tables(positions):
    lower = jnp.arange(MX, dtype=jnp.int32)
    row_modes = jnp.concatenate([lower, lower + (NX - MX)])
    phases = (positions[:, None] * row_modes[None, :] % NX).astype(jnp.float32) * (full_turn / NX)
    return (jnp.cos(phases), jnp.sin(phases))


def inverse_table(positions):
    col_modes = jnp.arange(MY, dtype=jnp.int32)
    col_weight = jnp.where(col_modes == 0, 1.0, 2.0).astype(jnp.float32) / (NX * NY)
    phases = (col_modes[:, None] * positions[None, :] % NY).astype(jnp.float32) * (full_turn / NY)
    return jnp.concatenate(
        [jnp.cos(phases) * col_weight[:, None], -jnp.sin(phases) * col_weight[:, None]], axis=0
    )


def conv_rows(padded_plane, tap_weights, dilation, side_taps, first_row, count_rows, local_cols):
    channels = padded_plane.shape[0]
    pieces = []
    for row_tap in range(side_taps):
        for col_tap in range(side_taps):
            row_offset = 4 + (row_tap - side_taps // 2) * dilation + first_row
            col_offset = 4 + (col_tap - side_taps // 2) * dilation
            pieces.append(
                padded_plane[
                    :, row_offset : row_offset + count_rows, col_offset : col_offset + local_cols
                ]
            )
    stacked = jnp.stack(pieces, 0)
    shaped_weights = tap_weights.reshape(channels, side_taps * side_taps, channels)
    return jnp.einsum("otc,tcxy->oxy", shaped_weights, stacked, preferred_element_type=jnp.float32)


def on_device(grid_field, spectral_weight, conv_near, conv_far, mix_logits, channel_bias):
    channels = grid_field.shape[1]
    local_rows = grid_field.shape[2]
    local_cols = grid_field.shape[3]
    row_positions = lax.axis_index("gx") * local_rows + jnp.arange(local_rows, dtype=jnp.int32)
    col_positions = lax.axis_index("gy") * local_cols + jnp.arange(local_cols, dtype=jnp.int32)
    forward_cols = forward_table(col_positions)
    cosine_rows, sine_rows = row_tables(row_positions)
    inverse_cols = inverse_table(col_positions)
    share_modes = spectral_weight.shape[-1]
    owner_index = lax.axis_index("gx") * lax.axis_size("gy") + lax.axis_index("gy")
    mode_start = owner_index * share_modes
    row_blocks = max(1, local_rows // 32)
    while local_rows % row_blocks != 0:
        row_blocks = row_blocks - 1
    block_rows = local_rows // row_blocks
    planes_block = grid_field
    for layer_index in range(LAYERS):
        planes_here = planes_block.shape[0]
        line_sums = jnp.dot(
            planes_block.reshape(planes_here * channels * local_rows, local_cols),
            forward_cols,
            preferred_element_type=jnp.float32,
        )
        line_sums = line_sums.reshape(planes_here, channels, local_rows, 2 * MY)
        real_lines = line_sums[..., :MY]
        imaginary_lines = line_sums[..., MY:]

        def contract_rows(operand, lookup):
            return jnp.einsum("pcxk,xj->pcjk", operand, lookup, precision=highest)

        real_spec = contract_rows(real_lines, cosine_rows) + contract_rows(
            imaginary_lines, sine_rows
        )
        imaginary_spec = contract_rows(imaginary_lines, cosine_rows) - contract_rows(
            real_lines, sine_rows
        )
        partial_value = jnp.stack(
            [
                real_spec.reshape(planes_here, channels, MODES),
                imaginary_spec.reshape(planes_here, channels, MODES),
            ]
        )
        totals = lax.psum(partial_value, ("gx", "gy"))
        own_modes = lax.dynamic_slice_in_dim(totals, mode_start, share_modes, 3)

        def mix_modes(spectrum, weights):
            return jnp.einsum("pcm,com->pom", spectrum, weights, precision=highest)

        weight_real = spectral_weight[layer_index, 0]
        weight_imaginary = spectral_weight[layer_index, 1]
        real_mixed = mix_modes(own_modes[0], weight_real) - mix_modes(
            own_modes[1], weight_imaginary
        )
        imaginary_mixed = mix_modes(own_modes[1], weight_real) + mix_modes(
            own_modes[0], weight_imaginary
        )
        own_block = jnp.stack([real_mixed, imaginary_mixed])[None]
        gathered = lax.all_gather(own_block, ("gx", "gy"), axis=0, tiled=True)
        gathered = jnp.transpose(gathered, (1, 2, 3, 0, 4)).reshape(2, planes_here, channels, MODES)
        real_full = gathered[0].reshape(planes_here, channels, KX, MY)
        imaginary_full = gathered[1].reshape(planes_here, channels, KX, MY)

        def expand_rows(spectrum, lookup):
            return jnp.einsum("pcjk,xj->pcxk", spectrum, lookup, precision=highest)

        real_rows = expand_rows(real_full, cosine_rows) - expand_rows(imaginary_full, sine_rows)
        imaginary_rows = expand_rows(real_full, sine_rows) + expand_rows(
            imaginary_full, cosine_rows
        )
        stacked = jnp.concatenate([real_rows, imaginary_rows], axis=-1).reshape(
            planes_here * channels * local_rows, 2 * MY
        )
        spectral = jnp.dot(stacked, inverse_cols, precision=highest)
        layer_spectral = spectral.reshape(planes_here, channels, local_rows, local_cols)
        padded = padded_2(planes_block, (("gx", 2), ("gy", 3)), 4)
        exponents = jnp.exp(mix_logits[layer_index])
        mixture = exponents / jnp.sum(exponents)
        bias_column = channel_bias[layer_index][:, None, None]
        row_pieces = []
        for block_index in range(row_blocks):
            first_row = block_index * block_rows
            near_term = conv_rows(
                padded[0], conv_near[layer_index], 1, 3, first_row, block_rows, local_cols
            )
            far_term = conv_rows(
                padded[0], conv_far[layer_index], 2, 5, first_row, block_rows, local_cols
            )
            spectral_rows = layer_spectral[0, :, first_row : first_row + block_rows, :]
            summed = (
                mixture[0] * spectral_rows
                + mixture[1] * near_term
                + mixture[2] * far_term
                + bias_column
            )
            row_pieces.append(jax.nn.gelu(summed, approximate=False).astype(jnp.bfloat16))
        outputs = [jnp.concatenate(row_pieces, axis=1)]
        planes_block = jnp.stack(outputs)
    return planes_block


def solution(mesh):
    in_specs = (
        P(None, None, "gx", "gy"),
        P(None, None, None, None, ("gx", "gy")),
        P(),
        P(),
        P(),
        P(),
    )
    out_specs = P(None, None, "gx", "gy")
    return jax.shard_map(
        on_device, mesh=mesh, in_specs=in_specs, out_specs=out_specs, check_vma=False
    )
```

profile of v0, /device:TPU:0, one launch (start us, length us, event | category | flops | bytes accessed | tf_op | source)
XLA Modules:
  0.0 1025.7 jit_solution(15079216024907753427)
XLA Ops:
  8.8 6.0 collective-permute-start.1
  15.0 1.9 convolution_bitcast_fusion
  23.0 2.0 slice_bitcast_fusion.263
  27.7 2.0 broadcast_divide_fusion.1
  29.7 1.5 slice_reduce_fusion.2
  35.1 1.6 collective-permute-start.2
  37.3 2.9 collective-permute-start.3
  40.8 1.7 reshape_squeeze.9
  42.5 1.5 reshape_squeeze.8
  45.9 1.4 reshape_squeeze.10
  49.2 1.6 maximum_bitcast_fusion
  58.5 1.5 constant_dynamic-update-slice_fusion.29
  60.0 1.5 constant_dynamic-update-slice_fusion.28
  61.5 1.5 constant_dynamic-update-slice_fusion.27
  65.3 1.5 constant_dynamic-update-slice_fusion.24
  67.1 1.5 constant_dynamic-update-slice_fusion.23
  68.6 1.5 constant_dynamic-update-slice_fusion.22
  71.0 3.8 copy-done.15
  74.8 14.7 %constant_dynamic-update-slice_fusion.20 = (bf16[25,20,32,256]{3,1,2,0:T(8,128)(2,1)}, bf16[25,20,32,256]{3,1,2,0:T(8,128)(2,1)S(1)}, bf16[9,20,32,256]{3,1,2,0:...) fusion(bf16[25,20,32,256]{3,1,2,0:T(8,128)(2,1)} %get-tuple-ele, ...), kind=kLoop, calls=%fused_computation.275 | loop fusion | bytes 5505024
  89.7 1.9 constant_dynamic-update-slice_fusion.19
  91.6 1.9 constant_dynamic-update-slice_fusion.18
  93.4 1.7 constant_dynamic-update-slice_fusion.17
  95.2 1.5 constant_dynamic-update-slice_fusion.16
  96.6 1.9 constant_dynamic-update-slice_fusion.15
  98.5 1.8 constant_dynamic-update-slice_fusion.14
  100.3 1.8 constant_dynamic-update-slice_fusion.13
  102.1 1.7 constant_dynamic-update-slice_fusion.12
  104.6 2.3 convolution_bitcast_fusion.3
  106.9 2.4 convolution_bitcast_fusion.5
  109.3 6.5 convolution_bitcast_fusion.7
  115.8 2.3 convolution_bitcast_fusion.9
  118.8 1.5 convolution_bitcast_fusion.6
  120.4 1.5 convolution_bitcast_fusion.8
  123.3 1.5 convolution_bitcast_fusion.10
  124.9 39.9 %all-reduce.3.cloned.1.call-done = f32[2,1,20,2048]{3,0,2,1:T(2,128)} async-done(((f32[2,1,20,2048]{3,0,2,1:T(2,128)}), f32[2,1,20,2048]{3,0,2,1:T(2,128)}) %all-reduce.3.cloned.1.call-update) | async-done | bytes 327696 | tf_op jit(solution)/shard_map/psum | solution.py:116
  167.1 326.2 %all-gather = f32[256,1,20,16]{2,3,1,0:T(8,128)S(1)} all-gather(f32[2,1,20,16]{2,3,1,0:T(8,128)S(1)} %pad_maximum_fusion.8), channel_id=2, replica_groups=mesh['gx'=16,'gy'=8] {'gx','gy'}, dimensions={0}, use_global_device_ids=true | all-gather | bytes 330240 | tf_op jit(solution)/shard_map/all_gather | solution.py:131
  500.9 2.2 convolution_bitcast_fusion.2
  503.2 10.4 %fusion.42 = (bf16[20,32,256]{2,1,0:T(8,128)(2,1)S(1)}, bf16[20,32,256]{2,1,0:T(8,128)(2,1)S(1)}, bf16[20,32,256]{2,1,0:T(8,128)(2,1)S(1)}, bf16[20,32,256]{2,1,0:T(8,128)(2,1)S(1)}) fusion(f32[32,256,20]{1,2,0:T(8,128)} %convolution_bitcast_fusion.9, f32[32,256,20]{1,2,0:T(8,128)} %convolution_bitcast_fusion.10, ...), kind=kLoop, calls=%fused_computation.51 | loop fusion | flops 46530560 | bytes 9175132 | tf_op jit(solution)/shard_map/convert_element_type | solution.py:168
  516.9 5.3 collective-permute-start.5
  526.1 4.3 collective-permute-start.7
  532.6 1.8 maximum_bitcast_fusion.1
  548.7 3.2 copy-done.18
  552.0 2.1 constant_dynamic-update-slice_fusion.147
  554.4 2.9 constant_dynamic-update-slice_fusion.146
  557.2 2.7 constant_dynamic-update-slice_fusion.145
  560.0 2.6 constant_dynamic-update-slice_fusion.144
  562.6 2.9 constant_dynamic-update-slice_fusion.143
  565.5 2.6 constant_dynamic-update-slice_fusion.142
  568.1 2.6 constant_dynamic-update-slice_fusion.141
  570.7 2.6 constant_dynamic-update-slice_fusion.140
  573.2 2.5 constant_dynamic-update-slice_fusion.139
  576.2 2.8 copy-done.16
  579.2 4.5 fusion.25
  583.7 9.6 fusion.19
  593.3 5.3 fusion.22
  598.6 5.3 fusion.16
  603.8 2.6 fusion.28
  606.4 2.8 fusion.31
  609.2 2.6 fusion.34
  611.7 2.6 fusion.37
  614.3 58.0 %all-reduce.5.cloned.1.call-done = f32[2,1,20,2048]{3,0,2,1:T(2,128)} async-done(((f32[2,1,20,2048]{3,0,2,1:T(2,128)}), f32[2,1,20,2048]{3,0,2,1:T(2,128)}) %all-reduce.5.cloned.1.call-update) | async-done | bytes 327696 | tf_op jit(solution)/shard_map/psum | solution.py:116
  674.7 325.8 %all-gather.1 = f32[256,1,20,16]{2,3,1,0:T(8,128)S(1)} all-gather(f32[2,1,20,16]{2,3,1,0:T(8,128)S(1)} %pad_maximum_fusion.9), channel_id=3, replica_groups=mesh['gx'=16,'gy'=8] {'gx','gy'}, dimensions={0}, use_global_device_ids=true | all-gather | bytes 330240 | tf_op jit(solution)/shard_map/all_gather | solution.py:131
  1004.6 2.2 convolution_bitcast_fusion.1
  1006.8 10.5 %fusion.54 = (bf16[20,32,256]{2,1,0:T(8,128)(2,1)S(1)}, bf16[20,32,256]{2,1,0:T(8,128)(2,1)S(1)}, bf16[20,32,256]{2,1,0:T(8,128)(2,1)S(1)}, bf16[20,32,256]{2,1,0:T(8,128)(2,1)S(1)}) fusion(f32[32,256,20]{1,2,0:T(8,128)} %fusion.16, f32[32,256,20]{1,2,0:T(8,128)} %fusion.28, f32[1,20,128,256]{3,2,1,0:T(8,128)S(1)} %convolution_bitcast_fusion.1, ...), kind=kLoop, calls=%fused_computation.63 | loop fusion | flops 46530560 | bytes 9175132 | tf_op jit(solution)/shard_map/convert_element_type | solution.py:168
  (209 shorter events, 75.8 us)
Async XLA Ops:
  6.5 15.6 %copy-start.8 = (bf16[2,20,500]{2,0,1:T(2,128)(2,1)S(1)}, bf16[2,20,500]{2,0,1:T(2,128)(2,1)}, u32[]{:S(2)}) copy-start(bf16[2,20,500]{2,0,1:T(2,128)(2,1)} %param.9) | copy-start | bytes 120004
  6.5 158.2 %all-reduce.3.cloned.1.call-start = ((), (), s32[]{:S(2)}) async-start(), calls=%async_computation | async-start | bytes 655360 | tf_op jit(solution)/shard_map/psum | solution.py:116
  8.1 23.0 %collective-permute-start = (bf16[1,20,4,256]{3,1,2,0:T(8,128)(2,1)}, bf16[1,20,4,256]{3,1,2,0:T(8,128)(2,1)}, u32[]{:S(2)}, u32[]{:S(2)}) collective-permute-start(bf16[1,20,4,256]{3,1,2,0:T(8,128)(2,1)} %copy.500), channel_id=1, source_target_pairs={{0,8},{8,16},{16,24},{24,32},{32,40},{40,48},{48,56},{56,64},{64,7... | collective-permute-start | bytes 122888 | tf_op jit(solution)/shard_map/ppermute | solution.py:28
  8.8 24.0 %collective-permute-start.1 = (bf16[1,20,4,256]{3,1,2,0:T(8,128)(2,1)}, bf16[1,20,4,256]{3,1,2,0:T(8,128)(2,1)}, u32[]{:S(2)}, u32[]{:S(2)}) collective-permute-start(bf16[1,20,4,256]{3,1,2,0:T(8,128)(2,1)} %copy.501), channel_id=1, source_target_pairs={{8,0},{16,8},{24,16},{32,24},{40,32},{48,40},{56,48},{64,56},{72,6... | collective-permute-start | bytes 122888 | tf_op jit(solution)/shard_map/ppermute | solution.py:29
  15.0 7.2 copy-start.11
  15.0 7.2 copy-start.13
  15.0 10.7 %copy-start.19 = (f32[2,3]{1,0:T(2,128)S(1)}, f32[2,3]{1,0:T(2,128)}, u32[]{:S(2)}) copy-start(f32[2,3]{1,0:T(2,128)} %param.10) | copy-start | bytes 76
  15.0 17.0 %copy-start = (bf16[1,20,128,256]{3,2,1,0:T(8,128)(2,1)S(1)}, bf16[1,20,128,256]{3,2,1,0:T(8,128)(2,1)}, u32[]{:S(2)}) copy-start(bf16[1,20,128,256]{3,2,1,0:T(8,128)(2,1)} %param.6) | copy-start | bytes 3932164
  22.1 650.2 %all-reduce.5.cloned.1.call-start = ((), (), s32[]{:S(2)}) async-start(), calls=%async_computation.1 | async-start | bytes 655360 | tf_op jit(solution)/shard_map/psum | solution.py:116
  35.1 12.2 %collective-permute-start.2 = (bf16[1,20,136,4]{2,3,1,0:T(4,128)(2,1)}, bf16[1,20,136,4]{2,3,1,0:T(4,128)(2,1)S(1)}, u32[]{:S(2)}, u32[]{:S(2)}) collective-permute-start(bf16[1,20,136,4]{2,3,1,0:T(4,128)(2,1)} %copy.211), channel_id=1, source_target_pairs={{0,1},{1,2},{2,3},{3,4},{4,5},{5,6},{6,7},{7,0},{8,9},{9,10},{10,1... | collective-permute-start | bytes 65288 | tf_op jit(solution)/shard_map/ppermute | solution.py:28
  37.3 10.6 %collective-permute-start.3 = (bf16[1,20,136,4]{2,3,1,0:T(4,128)(2,1)S(1)}, bf16[1,20,136,4]{2,3,1,0:T(4,128)(2,1)}, u32[]{:S(2)}, u32[]{:S(2)}) collective-permute-start(bf16[1,20,136,4]{2,3,1,0:T(4,128)(2,1)S(1)} %copy.212), channel_id=1, source_target_pairs={{1,0},{2,1},{3,2},{4,3},{5,4},{6,5},{7,6},{0,7},{9,8},{10,9},{11,1... | collective-permute-start | bytes 65288 | tf_op jit(solution)/shard_map/ppermute | solution.py:29
  71.0 3.8 copy-start.15
  100.3 4.3 copy-start.7
  106.9 8.9 slice-start
  106.9 8.9 slice-start.1
  109.3 6.5 slice-start.2
  115.8 2.4 copy-start.5
  120.4 45.4 %copy-start.4 = (f32[20,20,16]{1,2,0:T(8,128)S(1)}, f32[20,20,16]{1,2,0:T(8,128)}, u32[]{:S(2)}) copy-start(f32[20,20,16]{1,2,0:T(8,128)} %get-tuple-element.287) | copy-start | bytes 76804
  120.4 46.1 %copy-start.3 = (f32[20,20,16]{1,2,0:T(8,128)S(1)}, f32[20,20,16]{1,2,0:T(8,128)}, u32[]{:S(2)}) copy-start(f32[20,20,16]{1,2,0:T(8,128)} %get-tuple-element.286) | copy-start | bytes 76804
  124.9 376.1 %copy-start.6 = (f32[32,256]{1,0:T(8,128)S(1)}, f32[32,256]{1,0:T(8,128)}, u32[]{:S(2)}) copy-start(f32[32,256]{1,0:T(8,128)} %get-tuple-element.296) | copy-start | bytes 98308
  167.1 336.1 %copy-start.21 = (f32[20]{0:T(128)S(1)}, f32[20]{0:T(128)}, u32[]{:S(2)}) copy-start(f32[20]{0:T(128)} %get-tuple-element.300) | copy-start | bytes 244
  494.2 9.0 copy-start.1
  500.9 12.8 %copy-start.12 = (bf16[256,32]{0,1:T(8,128)(2,1)S(1)}, bf16[256,32]{0,1:T(8,128)(2,1)}, u32[]{:S(2)}) copy-start(bf16[256,32]{0,1:T(8,128)(2,1)} %copy-done.11) | copy-start | bytes 49156
  500.9 12.8 %copy-start.14 = (bf16[256,32]{0,1:T(8,128)(2,1)S(1)}, bf16[256,32]{0,1:T(8,128)(2,1)}, u32[]{:S(2)}) copy-start(bf16[256,32]{0,1:T(8,128)(2,1)} %copy-done.13) | copy-start | bytes 49156
  516.8 7.1 collective-permute-start.4
  516.9 7.0 collective-permute-start.5
  525.6 6.2 collective-permute-start.6
  526.1 6.0 collective-permute-start.7
  548.7 3.2 copy-start.18
  568.1 11.1 %copy-start.9 = (bf16[20,25,20]{1,0,2:T(8,128)(2,1)S(1)}, bf16[20,25,20]{1,0,2:T(8,128)(2,1)}, u32[]{:S(2)}) copy-start(bf16[20,25,20]{1,0,2:T(8,128)(2,1)} %copy.257) | copy-start | bytes 60004
  575.7 3.3 copy-start.16
  583.7 9.6 copy-start.17
  598.6 5.3 copy-start.10
  606.4 66.9 %copy-start.2 = (f32[20,20,16]{1,2,0:T(8,128)S(1)}, f32[20,20,16]{1,2,0:T(8,128)}, u32[]{:S(2)}) copy-start(f32[20,20,16]{1,2,0:T(8,128)} %get-tuple-element.285) | copy-start | bytes 76804
  674.7 332.2 %copy-start.20 = (f32[20]{0:T(128)S(1)}, f32[20]{0:T(128)}, u32[]{:S(2)}) copy-start(f32[20]{0:T(128)} %get-tuple-element.299) | copy-start | bytes 244
Sparse Core Ops, SparseCore 0:
  22.2 142.4 all-reduce.2
  531.7 140.5 all-reduce.4
where the time goes:
time: 1030 us
  blocking collectives  652 us (63%)
  local copies, waits for them, and re-layouts  131 us (13%)
  waiting for transfers between devices  98.6 us (10%)
  matrix products  74.6 us (7%)
  other arithmetic  34.5 us (3%)
  starting transfers between devices  20.3 us (2%)
  between operations  14.7 us (1%)
    all_gather x2, blocking collectives, on_device(): gathered = lax.all_gather(own_block, ('gx', 'gy'), axis=0, tiled=True)  652 us
    unnamed x121, local copies, waits for them, and re-layouts  98.1 us
    psum x2, waiting for transfers between devices, on_device(): totals = lax.psum(partial_value, ('gx', 'gy'))  97.8 us
    dot_general x16, matrix products, conv_rows(): jnp.einsum('otc,tcxy->oxy', shaped_weights, stacked, preferred_element_ty...  53.9 us
    convert_element_type x2, other arithmetic, on_device(): jax.nn.gelu(summed, approximate=False).astype(jnp.bfloat16)  20.9 us
  transfers between devices with their start and end apart: 10, of which 4 were waited for; matrix products, arithmetic and copies ran while one was open for 18% of the time, Pallas kernels for 0%

commit v1 on v0

v1 whole, which is shorter than its diff:
```python
import functools
import math

import jax
import jax.numpy as jnp
import ml_dtypes
import numpy as np
from jax import lax
from jax.experimental import pallas as pl
from jax.experimental.pallas import tpu as pltpu
from jax.sharding import PartitionSpec as P

NX = 2048
NY = 2048
C = 20
LAYERS = 2
ROWS = 128
COLS = 256
GROUPS = 5
WIDE = 384
BLOCK = 8 * C

f32 = jnp.float32
bf16 = jnp.bfloat16
both = ("gx", "gy")


def wave(numbers, positions, length):
    product = numbers.astype(np.int64)[:, None] * positions.astype(np.int64)[None, :]
    scale = np.float32(2.0 * math.pi / length)
    angle = (product % length).astype(np.float32) * scale
    angle = angle.astype(np.float64)
    return np.cos(angle).astype(np.float32), np.sin(angle).astype(np.float32)


def halves(value):
    high = value.astype(ml_dtypes.bfloat16)
    low = (value - high.astype(np.float32)).astype(ml_dtypes.bfloat16)
    return high, low


ky_all = np.arange(32)
kx_all = np.concatenate([np.arange(32), np.arange(32) + NX - 32])


def forward_cols():
    cosine, sine = wave(ky_all, np.arange(NY), NY)
    cosine, sine = cosine.T.reshape(NY, 2, 1, 16), sine.T.reshape(NY, 2, 1, 16)
    first = np.stack([cosine, -sine], axis=3)
    second = np.stack([-sine, -cosine], axis=3)
    tables = [np.broadcast_to(t, (NY, 2, 4, 2, 16)).reshape(NY, 256) for t in (first, second)]
    return np.stack(tables).astype(ml_dtypes.bfloat16)


def forward_rows(before, count):
    out = np.zeros((16, 2, 64, 2 * count), ml_dtypes.bfloat16)
    for device in range(16):
        cosine, sine = wave(kx_all, np.arange(ROWS) + device * ROWS, NX)
        table = np.zeros((2, 64, count), np.float32)
        table[0, :, before : before + ROWS] = cosine
        table[1, :, before : before + ROWS] = sine
        high, low = halves(np.transpose(table, (1, 0, 2)).reshape(64, 2 * count))
        out[device, 0], out[device, 1] = high, low
    return out


def inverse_rows(before, count):
    out = np.zeros((16, 2, count, 128), ml_dtypes.bfloat16)
    for device in range(16):
        positions = (np.arange(count) - before + device * ROWS) % NX
        cosine, sine = wave(kx_all, positions, NX)
        high, low = halves(np.concatenate([cosine.T, -sine.T], axis=1))
        out[device, 0], out[device, 1] = high, low
    return out


def inverse_cols(width):
    out = np.zeros((8, 2, 64, 2 * width), ml_dtypes.bfloat16)
    weight = (np.where(ky_all == 0, 1.0, 2.0) / (NX * NY)).astype(np.float32)[:, None]
    for device in range(8):
        lanes = np.arange(width)
        lanes = np.where(lanes >= 320, lanes - WIDE, lanes)
        cosine, sine = wave(ky_all, (lanes + device * COLS) % NY, NY)
        cosine, sine = cosine * weight, sine * weight
        real = np.concatenate([cosine, sine], axis=1)
        imaginary = np.concatenate([-sine, cosine], axis=1)
        table = np.stack([real.reshape(2, 16, 2 * width), imaginary.reshape(2, 16, 2 * width)], 1)
        high, low = halves(table.reshape(64, 2 * width))
        out[device, 0], out[device, 1] = high, low
    return out


def spread(taps):
    width = 2 * taps * BLOCK
    lanes = np.arange(width) % (taps * BLOCK) // 8
    return (np.arange(taps * C)[:, None] == lanes[None, :]).astype(ml_dtypes.bfloat16)


def offsets(taps):
    width = 2 * taps * BLOCK
    lanes = np.arange(width)
    place = lanes // (taps * BLOCK) * 8 + lanes % 8
    return (place[None, :] - np.arange(8)[:, None] - 4).astype(np.int32)


def split(value):
    high = value.astype(bf16)
    return high, (value - high.astype(f32)).astype(bf16)


def mul(a, b):
    return jnp.dot(a, b, preferred_element_type=f32)


def transform(planes, cols_ref, rows_ref, out_ref):
    lane = lax.broadcasted_iota(jnp.int32, (COLS, 256), 1)
    slot = (lane >> 5) & 3
    zero = jnp.zeros((), bf16)
    placed = [[jnp.where(slot == i, cols_ref[t], zero) for i in range(4)] for t in range(2)]
    rows_high, rows_low = rows_ref[0, 0], rows_ref[0, 1]
    for group in range(GROUPS):
        members = [planes(4 * group + i) for i in range(4)]
        sums = []
        for t in range(2):
            total = mul(members[0], placed[t][0])
            for i in range(1, 4):
                total = total + mul(members[i], placed[t][i])
            sums.append(total)
        high, low = split(jnp.concatenate(sums, axis=0))
        modes = mul(rows_high, high) + mul(rows_high, low) + mul(rows_low, high)
        for half in range(2):
            out_ref[pl.ds(half, 64, stride=2), group, :] = modes[:, 128 * half : 128 * half + 128]


def forward_kernel(place_ref, grid_ref, cols_ref, rows_ref, out_ref):
    transform(lambda c: grid_ref[c], cols_ref, rows_ref, out_ref)


def mix_kernel(mixture_ref, received_ref, weights_ref, out_ref, *, layer):
    total = jnp.sum(received_ref[...], axis=0)
    lane = lax.broadcasted_iota(jnp.int32, (8, 128), 1)
    sub = lax.broadcasted_iota(jnp.int32, (8, 128), 0)
    own = (lane >> 4) == sub
    parts = []
    for group in range(GROUPS):
        row = jnp.broadcast_to(total[group : group + 1, :], (8, 128))
        row = jnp.where(own, row, 0.0)
        for shift in (64, 32, 16):
            row = row + pltpu.roll(row, shift, 1)
        parts.append(row)
    spectrum = jnp.concatenate(parts, axis=0)
    rows = [jnp.sum(weights_ref[g] * spectrum, axis=0, keepdims=True) for g in range(GROUPS)]
    mixed = jnp.concatenate(rows, axis=0) * mixture_ref[layer, 0]
    out_ref[...] = jnp.broadcast_to(mixed[None], out_ref.shape)


def edge_kernel(grid_ref, top_ref, bottom_ref, left_ref, right_ref):
    pick = lax.broadcasted_iota(jnp.int32, (8, COLS), 1) - lax.broadcasted_iota(
        jnp.int32, (8, COLS), 0
    )
    one = jnp.ones((), f32)
    zero = jnp.zeros((), f32)
    first = jnp.where(pick == 0, one, zero).astype(bf16)
    last = jnp.where(pick == COLS - 8, one, zero).astype(bf16)
    rows = jnp.concatenate(
        [
            grid_ref[...].reshape(C * ROWS, COLS),
            top_ref[...].reshape(BLOCK, COLS),
            bottom_ref[...].reshape(BLOCK, COLS),
        ],
        axis=0,
    )
    dims = (((1,), (1,)), ((), ()))
    for pattern, ref in ((first, left_ref), (last, right_ref)):
        ref[...] = lax.dot_general(pattern, rows, dims, preferred_element_type=f32).astype(bf16)


def banded(weights_ref, spread_ref, offsets_ref, steps, width):
    offset = offsets_ref[...][None]
    total = jnp.zeros((C, 8, width), f32)
    for index, step in enumerate(steps):
        taps = mul(weights_ref[index], spread_ref[...])
        total = jnp.where(offset == step, taps[:, None, :], total)
    return total.reshape(BLOCK, width).astype(bf16)


def convolve(mixture_ref, field, bands, out_ref, stacks, layer, first, count, width):
    near_band, far_band = bands
    near_stack, far_stack = stacks

    def shift(index, carry):
        block = field(first + index)
        for position, step in enumerate((-1, 0, 1)):
            moved = block if step == 0 else pltpu.roll(block, (-step) % WIDE, 1)
            start = pl.multiple_of((index * 3 + position) * BLOCK, 16)
            near_stack[pl.ds(start, BLOCK), :] = moved[:, :width].astype(bf16)
        for position, step in enumerate((-4, -2, 0, 2, 4)):
            moved = block if step == 0 else pltpu.roll(block, (-step) % WIDE, 1)
            start = pl.multiple_of((index * 5 + position) * BLOCK, 16)
            far_stack[pl.ds(start, BLOCK), :] = moved[:, :width].astype(bf16)
        return carry

    lax.fori_loop(0, count + 1, shift, 0)
    near_scale = mixture_ref[layer, 1]
    far_scale = mixture_ref[layer, 2]

    def block_sum(index, carry):
        near_rows = near_stack[pl.ds(pl.multiple_of(index * 3 * BLOCK, 16), 6 * BLOCK), :]
        far_rows = far_stack[pl.ds(pl.multiple_of(index * 5 * BLOCK, 16), 10 * BLOCK), :]
        total = near_scale * mul(near_band[...], near_rows) + far_scale * mul(
            far_band[...], far_rows
        )
        out_ref[pl.ds(pl.multiple_of(index * BLOCK, 8), BLOCK), :] = total
        return carry

    lax.fori_loop(0, count, block_sum, 0)


def first_conv_kernel(
    mixture_ref, grid_ref, top_ref, bottom_ref, left_ref, right_ref, near_ref, far_ref,
    near_spread, far_spread, near_offsets, far_offsets, order_ref, out_ref,
    field, near_band, far_band, near_stack, far_stack, *, first, count,
):
    near_band[...] = banded(near_ref, near_spread, near_offsets, (-1, 0, 1), 6 * BLOCK)
    far_band[...] = banded(far_ref, far_spread, far_offsets, (-4, -2, 0, 2, 4), 10 * BLOCK)
    lane = lax.broadcasted_iota(jnp.int32, (8, 128), 1)
    row = lax.broadcasted_iota(jnp.int32, (8, 128), 0)
    right_place = jnp.where(lane == row, 1.0, 0.0).astype(bf16)
    left_place = jnp.where(lane == row + 120, 1.0, 0.0).astype(bf16)
    dims = (((0,), (0,)), ((), ()))
    side = lax.dot_general(
        right_ref[...], right_place, dims, preferred_element_type=f32
    ) + lax.dot_general(left_ref[...], left_place, dims, preferred_element_type=f32)
    for c in range(C):
        main = grid_ref[c].astype(f32)
        for block in range(first, first + count + 1):
            if block == 0:
                value = top_ref[c].astype(f32)
                edge = side[C * ROWS + 8 * c : C * ROWS + 8 * c + 8]
            elif block == 17:
                value = bottom_ref[c].astype(f32)
                edge = side[C * ROWS + BLOCK + 8 * c : C * ROWS + BLOCK + 8 * c + 8]
            else:
                start = 8 * (block - 1)
                value = main[start : start + 8]
                edge = side[c * ROWS + start : c * ROWS + start + 8]
            place = (block - first) * BLOCK + 8 * c
            field[place : place + 8, :COLS] = value
            field[place : place + 8, COLS:] = edge
    def part(index):
        return field[pl.ds(pl.multiple_of((index - first) * BLOCK, 8), BLOCK), :]

    convolve(
        mixture_ref, part, (near_band, far_band), out_ref, (near_stack, far_stack), 0, first,
        count, WIDE,
    )


def second_conv_kernel(
    mixture_ref, field_ref, near_ref, far_ref, near_spread, far_spread, near_offsets,
    far_offsets, order_ref, out_ref, near_band, far_band, near_stack, far_stack, *, first, count,
):
    near_band[...] = banded(near_ref, near_spread, near_offsets, (-1, 0, 1), 6 * BLOCK)
    far_band[...] = banded(far_ref, far_spread, far_offsets, (-4, -2, 0, 2, 4), 10 * BLOCK)

    def part(index):
        return field_ref[pl.ds(pl.multiple_of(index * BLOCK, 8), BLOCK), :]

    convolve(
        mixture_ref, part, (near_band, far_band), out_ref, (near_stack, far_stack), 1, first,
        count, COLS,
    )


def gelu(value):
    return 0.5 * value * (1.0 + lax.erf(value * math.sqrt(0.5)))


def expand(bias_ref, gathered_ref, cols_ref, rows_ref, upper_ref, lower_ref, layer, width, blocks, emit):
    parts = []
    for group in range(GROUPS):
        pair = [gathered_ref[pl.ds(half, 64, stride=2), group, :] for half in range(2)]
        parts.append(jnp.concatenate(pair, axis=1))
    high, low = split(jnp.concatenate(parts, axis=0))
    stacked = jnp.concatenate([high, low], axis=0)
    rows_high, rows_low = rows_ref[0, 0], rows_ref[0, 1]
    rows_twice = jnp.concatenate([rows_high, rows_high], axis=1)
    upper_blocks = upper_ref.shape[0] // BLOCK
    for slot in range(4):
        placed = []
        for t in range(2):
            table = cols_ref[0, t]
            empty = jnp.zeros((32, 2 * width), bf16)
            pieces = []
            for half in range(2):
                pieces += [table[32 * half : 32 * half + 32] if i == slot else empty for i in range(4)]
            placed.append(jnp.concatenate(pieces, axis=0))
        first = mul(stacked, placed[0])
        lines = first[:320] + first[320:] + mul(high, placed[1])
        for group in range(GROUPS):
            channel = 4 * group + slot
            here = lines[64 * group : 64 * group + 64]
            line_high, line_low = split(jnp.concatenate([here[:, :width], here[:, width:]], axis=0))
            value = mul(rows_twice, jnp.concatenate([line_high, line_low], axis=0)) + mul(
                rows_low, line_high
            )
            local = []
            for block in range(blocks):
                ref, index = (
                    (upper_ref, block) if block < upper_blocks else (lower_ref, block - upper_blocks)
                )
                local.append(ref[index * BLOCK + 8 * channel : index * BLOCK + 8 * channel + 8, :])
            value = value + jnp.concatenate(local, axis=0) + bias_ref[layer, channel]
            emit(channel, gelu(value))


def middle_kernel(
    place_ref, bias_ref, gathered_ref, icols_ref, irows_ref, fcols_ref, frows_ref, upper_ref,
    lower_ref, field_ref, out_ref, planes,
):
    def emit(channel, value):
        rounded = value.astype(bf16)
        planes[channel, :136] = rounded[:, :COLS]
        planes[channel, 136:] = jnp.zeros((8, COLS), bf16)
        back = rounded.astype(f32)
        for block in range(17):
            place = block * BLOCK + 8 * channel
            field_ref[place : place + 8, :] = back[8 * block : 8 * block + 8]

    expand(bias_ref, gathered_ref, icols_ref, irows_ref, upper_ref, lower_ref, 0, WIDE, 17, emit)
    transform(lambda c: planes[c], fcols_ref, frows_ref, out_ref)


def last_kernel(
    place_ref, bias_ref, gathered_ref, icols_ref, irows_ref, upper_ref, lower_ref, out_ref
):
    def emit(channel, value):
        out_ref[channel] = value.astype(bf16)

    expand(bias_ref, gathered_ref, icols_ref, irows_ref, upper_ref, lower_ref, 1, COLS, 16, emit)


vmem = pl.BlockSpec(memory_space=pltpu.VMEM)
smem = pl.BlockSpec(memory_space=pltpu.SMEM)
anywhere = pl.BlockSpec(memory_space=pl.ANY)
limit = pltpu.CompilerParams(vmem_limit_bytes=56 * 1024 * 1024)


def call(kernel, outs, args, specs, scratch=(), flops=10**9, name=None):
    single = not isinstance(outs, (list, tuple))
    return pl.pallas_call(
        kernel,
        out_shape=outs,
        in_specs=specs,
        out_specs=vmem if single else [vmem] * len(outs),
        scratch_shapes=list(scratch),
        compiler_params=limit,
        cost_estimate=pl.CostEstimate(flops=flops, bytes_accessed=4 * 10**6, transcendentals=0),
        name=name,
    )(*args)


def whole(shape):
    zeros = (0,) * len(shape)
    return pl.BlockSpec(shape, lambda i, place: zeros)


def chosen(shape, axis, dim=0):
    def index(i, place):
        return tuple(place[axis] if d == dim else 0 for d in range(len(shape)))

    return pl.BlockSpec(shape, index)


def placed_call(kernel, outs, place, args, specs, scratch=(), flops=10**9, name=None):
    single = not isinstance(outs, (list, tuple))
    shapes = [outs] if single else list(outs)
    out_specs = [whole(s.shape) for s in shapes]
    return pl.pallas_call(
        kernel,
        out_shape=outs,
        grid_spec=pltpu.PrefetchScalarGridSpec(
            num_scalar_prefetch=1,
            grid=(1,),
            in_specs=specs,
            out_specs=out_specs[0] if single else out_specs,
            scratch_shapes=list(scratch),
        ),
        compiler_params=limit,
        cost_estimate=pl.CostEstimate(flops=flops, bytes_accessed=4 * 10**6, transcendentals=0),
        name=name,
    )(place, *args)


def shape_of(dims, kind):
    return jax.ShapeDtypeStruct(dims, kind)


def exchange(value):
    return lax.all_to_all(value, both, split_axis=0, concat_axis=0, tiled=True)


def ring(axis, step):
    size = lax.axis_size(axis)
    return [(i, (i + step) % size) for i in range(size)]


def on_device(grid_field, spectral_weight, conv_near, conv_far, mix_logits, channel_bias):
    place = jnp.stack([lax.axis_index("gx"), lax.axis_index("gy")]).astype(jnp.int32)
    grid = grid_field[0]
    top = lax.ppermute(grid[:, ROWS - 8 :], "gx", ring("gx", 1))
    bottom = lax.ppermute(grid[:, :8], "gx", ring("gx", -1))

    exponents = jnp.exp(mix_logits)
    mixture = exponents / jnp.sum(exponents, axis=1, keepdims=True)
    near = jnp.transpose(conv_near.reshape(LAYERS, C, 3, 3 * C), (0, 2, 1, 3))
    far = jnp.transpose(conv_far.reshape(LAYERS, C, 5, 5 * C), (0, 2, 1, 3))
    real, imaginary = spectral_weight[:, 0], spectral_weight[:, 1]
    from_real = jnp.stack([real, imaginary], axis=3)
    from_imaginary = jnp.stack([-imaginary, real], axis=3)
    weights = jnp.stack([from_real, from_imaginary], axis=2)
    weights = weights.reshape(LAYERS, 2 * C, GROUPS, 128)
    weights = jnp.transpose(weights, (0, 2, 1, 3))

    fcols = jnp.asarray(forward_cols())
    frows = jnp.asarray(forward_rows(0, ROWS))
    frows_wide = jnp.asarray(forward_rows(4, 144))
    irows = jnp.asarray(inverse_rows(0, ROWS))
    irows_wide = jnp.asarray(inverse_rows(4, 136))
    icols = jnp.asarray(inverse_cols(COLS))
    icols_wide = jnp.asarray(inverse_cols(WIDE))
    tables = [jnp.asarray(t) for t in (spread(3), spread(5), offsets(3), offsets(5))]

    fcols_spec = chosen((2, COLS, 256), 1, 1)
    chunk = shape_of((128, GROUPS, 128), f32)

    partial = placed_call(
        forward_kernel, chunk, place, (grid, fcols, frows),
        [whole((C, ROWS, COLS)), fcols_spec, chosen((1, 2, 64, 2 * ROWS), 0)],
        name="forward",
    )
    received = exchange(partial)
    first_cols, last_cols = call(
        edge_kernel, [shape_of((8, 18 * BLOCK), bf16)] * 2, (grid, top, bottom), [vmem] * 3,
        name="edges",
    )
    left = lax.ppermute(last_cols, "gy", ring("gy", 1))
    right = lax.ppermute(first_cols, "gy", ring("gy", -1))

    def mix(layer, received):
        return call(
            functools.partial(mix_kernel, layer=layer), chunk, (mixture, received, weights[layer]),
            [smem, vmem, vmem], flops=10**6, name="mix",
        )

    def stacks(count, width):
        return (
            pltpu.VMEM((BLOCK, 6 * BLOCK), bf16),
            pltpu.VMEM((BLOCK, 10 * BLOCK), bf16),
            pltpu.VMEM(((count + 1) * 3 * BLOCK, width), bf16),
            pltpu.VMEM(((count + 1) * 5 * BLOCK, width), bf16),
        )

    def first_conv(first, count, order):
        return call(
            functools.partial(first_conv_kernel, first=first, count=count),
            shape_of((count * BLOCK, WIDE), f32),
            (mixture, grid, top, bottom, left, right, near[0], far[0], *tables, order),
            [smem] + [vmem] * 11 + [anywhere],
            (pltpu.VMEM(((count + 1) * BLOCK, WIDE), f32), *stacks(count, WIDE)),
            name="conv_first",
        )

    def second_conv(field, first, count, order):
        return call(
            functools.partial(second_conv_kernel, first=first, count=count),
            shape_of((count * BLOCK, COLS), f32),
            (mixture, field, near[1], far[1], *tables, order),
            [smem] + [vmem] * 7 + [anywhere],
            stacks(count, COLS),
            name="conv_second",
        )

    upper = first_conv(0, 9, place)
    mixed = mix(0, received)
    gathered = exchange(mixed)
    lower = first_conv(9, 8, mixed)
    field, partial = placed_call(
        middle_kernel, [shape_of((17 * BLOCK, WIDE), f32), chunk], place,
        (channel_bias, gathered, icols_wide, irows_wide, fcols, frows_wide, upper, lower),
        [
            smem, whole((128, GROUPS, 128)), chosen((1, 2, 64, 2 * WIDE), 1),
            chosen((1, 2, 136, 128), 0), fcols_spec, chosen((1, 2, 64, 288), 0),
            whole((9 * BLOCK, WIDE)), whole((8 * BLOCK, WIDE)),
        ],
        (pltpu.VMEM((C, 144, COLS), bf16),),
        name="middle",
    )
    received = exchange(partial)
    upper = second_conv(field, 0, 8, place)
    mixed = mix(1, received)
    gathered = exchange(mixed)
    lower = second_conv(field, 8, 8, mixed)
    result = placed_call(
        last_kernel, shape_of((C, ROWS, COLS), bf16), place,
        (channel_bias, gathered, icols, irows, upper, lower),
        [
            smem, whole((128, GROUPS, 128)), chosen((1, 2, 64, 2 * COLS), 1),
            chosen((1, 2, ROWS, 128), 0), whole((8 * BLOCK, COLS)), whole((8 * BLOCK, COLS)),
        ],
        name="last",
    )
    return result[None]


def solution(mesh):
    in_specs = (
        P(None, None, "gx", "gy"),
        P(None, None, None, None, both),
        P(),
        P(),
        P(),
        P(),
    )
    out_specs = P(None, None, "gx", "gy")
    return jax.shard_map(
        on_device, mesh=mesh, in_specs=in_specs, out_specs=out_specs, check_vma=False
    )
```

time: 1030 us -> 146 us (0.14)
  blocking collectives: 652 us -> 22.9 us
  local copies, waits for them, and re-layouts: 131 us -> 12 us
  waiting for transfers between devices: 98.6 us -> 0.02 us
  Pallas kernels: 0 us -> 75.4 us
  matrix products: 74.6 us -> 0 us
  other arithmetic: 34.5 us -> 1.68 us
  between operations: 14.7 us -> 0.19 us
  starting transfers between devices: 20.3 us -> 32.8 us
    all_gather x2 -> x0, blocking collectives: 652 us -> none  [on_device(): gathered = lax.all_gather(own_block, ('gx', 'gy'), axis=0, tiled=True)]
    psum x2 -> x0, waiting for transfers between devices: 97.8 us -> none  [on_device(): totals = lax.psum(partial_value, ('gx', 'gy'))]
    unnamed x121 -> x20, local copies, waits for them, and re-layouts: 98.1 us -> 3.64 us
    pallas_call x0 -> x10, Pallas kernels: none -> 75.4 us  [the longest x7 53.6 us: call(): pl.pallas_call(kernel, out_shape=outs, in_specs=specs, out_specs=vmem if...]
    dot_general x28 -> x0, matrix products: 63.4 us -> none  [the longest x16 53.9 us: conv_rows(): jnp.einsum('otc,tcxy->oxy', shaped_weights, stacked, preferred_element_ty...]
    all_to_all x0 -> x1, blocking collectives: none -> 22.9 us  [exchange(): return lax.all_to_all(value, both, split_axis=0, concat_axis=0, tiled=True)]
    all_to_all x0 -> x3, starting transfers between devices: none -> 22.6 us  [exchange(): return lax.all_to_all(value, both, split_axis=0, concat_axis=0, tiled=True)]
    convert_element_type x2 -> x0, other arithmetic: 20.9 us -> none  [on_device(): jax.nn.gelu(summed, approximate=False).astype(jnp.bfloat16)]
  transfers between devices with their start and end apart: 10 -> 7, of which waited for: 4 -> 0; matrix products, arithmetic and copies ran while one was open for 18% -> 6% of each run, Pallas kernels for 0% -> 39%
where the time goes in v1:
time: 146 us; the launch traced here: 145 us
  Pallas kernels  75.4 us (52%)
  starting transfers between devices  32.8 us (22%)
  blocking collectives  22.9 us (16%)
  local copies, waits for them, and re-layouts  12 us (8%)
  other arithmetic  1.68 us (1%)
    pallas_call x7, Pallas kernels, call(): pl.pallas_call(kernel, out_shape=outs, in_specs=specs, out_specs=vmem if...  53.6 us
    all_to_all x1, blocking collectives, exchange(): return lax.all_to_all(value, both, split_axis=0, concat_axis=0, tiled=True)  22.9 us
    all_to_all x3, starting transfers between devices, exchange(): return lax.all_to_all(value, both, split_axis=0, concat_axis=0, tiled=True)  22.6 us
    pallas_call x3, Pallas kernels, placed_call(): pl.pallas_call(kernel, out_shape=outs, grid_spec=pltpu.PrefetchScalarGrid...  21.8 us
    ppermute x1, starting transfers between devices, on_device(): bottom = lax.ppermute(grid[:, :8], 'gx', ring('gx', -1))  6.02 us
    unnamed x20, local copies, waits for them, and re-layouts  3.64 us
    ppermute x1, starting transfers between devices, on_device(): right = lax.ppermute(first_cols, 'gy', ring('gy', -1))  3.17 us
  transfers between devices with their start and end apart: 7, of which 0 were waited for; matrix products, arithmetic and copies ran while one was open for 6% of the time, Pallas kernels for 39%

profile of v1, /device:TPU:0, one launch (start us, length us, event | category | flops | bytes accessed | tf_op | source)
XLA Modules:
  0.0 145.0 jit_solution(15356087821495407205)
XLA Ops:
  0.0 1.6 %fusion.1 = (bf16[20,8,256]{2,1,0:T(8,128)(2,1)}, bf16[20,8,256]{2,1,0:T(8,128)(2,1)}) fusion(bf16[20,128,256]{2,1,0:T(8,128)(2,1)} %bitcast.41), kind=kLoop, calls=%fused_computation.18 | loop fusion | bytes 327680 | tf_op jit(solution)/shard_map/slice | solution.py:412
  1.6 6.0 %collective-permute-start.1 = (bf16[20,8,256]{2,1,0:T(8,128)(2,1)}, bf16[20,8,256]{2,1,0:T(8,128)(2,1)S(1)}, u32[]{:S(2)}, u32[]{:S(2)}) collective-permute-start(bf16[20,8,256]{2,1,0:T(8,128)(2,1)} %get-tuple-element.13), channel_id=1, source_target_pairs={{0,120},{8,0},{16,8},{24,16},{32,24},{40,32},{48,40},{56,48},{64,5... | collective-permute-start | bytes 245768 | tf_op jit(solution)/shard_map/ppermute | solution.py:412
  7.6 0.0 collective-permute-start
  7.6 0.6 pad_add_fusion.place_ref.order_ref
  8.3 0.0 copy-start.3
  8.3 5.0 %forward.1 = f32[128,5,128]{2,1,0:T(8,128)} custom-call(s32[2]{0:T(128)} %pad_add_fusion.place_ref.order_ref, bf16[20,128,256]{2,1,0:T(8,128)(2,1)} %bitcast.42, bf16[2,2048,256]{2,1,0:T(8,128)(2,1)} %constant.33.clone.cols_ref.fcols_ref, bf16[16,2,64,256]{3,2,1,0:T(8,128)(2,1)} %constant.34.clone.rows_ref), custom_call_target="tpu_custom_call" | custom-call | flops 1000000000 | bytes 4000000 | tf_op jit(solution)/shard_map/forward/pallas_call | solution.py:379
  13.3 0.0 copy-start.7
  13.3 9.9 %all-to-all-start = ((f32[128,5,128]{2,1,0:T(8,128)}), f32[128,5,128]{2,1,0:T(8,128)S(1)}, u32[]{:S(2)}, u32[]{:S(2)}) async-start(f32[128,5,128]{2,1,0:T(8,128)} %forward.1), calls=%async_computation | async-start | bytes 1048576 | tf_op jit(solution)/shard_map/all_to_all | solution.py:400
  23.2 0.0 copy-done.3
  23.3 0.0 copy-done.7
  23.3 0.1 reshape.22
  23.5 0.6 slice_bitcast_fusion.4
  24.1 0.1 maximum_bitcast_fusion
  24.2 0.1 pad_maximum_fusion
  24.4 2.5 %copy.20 = f32[2,20,2,20,2,16]{5,4,3,2,1,0:T(2,128)S(1)} copy(f32[2,20,2,20,2,16]{3,5,1,0,4,2:T(8,128)S(1)} %pad_maximum_fusion) | data formatting | bytes 409600 | tf_op jit(solution)/shard_map/stack | solution.py:421
  26.9 0.0 copy-start.9
  26.9 0.0 copy-start.8
  26.9 2.0 %reshape.20 = f32[2,40,5,128]{3,2,1,0:T(8,128)S(1)} reshape(f32[2,20,2,20,2,16]{5,4,3,2,1,0:T(2,128)S(1)} %copy.20) | data formatting | bytes 409600 | tf_op jit(solution)/shard_map/reshape | solution.py:422
  28.9 0.7 slice_bitcast_fusion.2
  29.6 0.0 copy-done.9
  29.6 0.1 exponential_reduce_fusion
  29.7 0.7 exponential_divide_fusion.mixture_ref
  30.4 0.0 copy-done.8
  30.4 0.1 reshape.21
  30.5 0.0 collective-permute-done.1.bottom_ref
  30.5 0.0 copy-start.4
  30.5 0.0 collective-permute-done.top_ref
  30.6 0.6 copy-done.4
  31.2 2.9 %edges.1 = (bf16[8,2880]{1,0:T(8,128)(2,1)}, bf16[8,2880]{1,0:T(8,128)(2,1)}) custom-call(bf16[20,128,256]{2,1,0:T(8,128)(2,1)} %bitcast.43, bf16[20,8,256]{2,1,0:T(8,128)(2,1)} %collective-permute-done.top_ref, bf16[20,8,256]{2,1,0:T(8,128)(2,1)} %copy-done.4), custom_call_target="tpu_custom_call" | custom-call | flops 1000000000 | bytes 4000000 | tf_op jit(solution)/shard_map/edges/pallas_call | solution.py:351
  34.0 1.0 collective-permute-start.2
  35.0 3.2 %collective-permute-start.3 = (bf16[8,2880]{1,0:T(8,128)(2,1)}, bf16[8,2880]{1,0:T(8,128)(2,1)S(1)}, u32[]{:S(2)}, u32[]{:S(2)}) collective-permute-start(bf16[8,2880]{1,0:T(8,128)(2,1)} %get-tuple-element.10), channel_id=1, source_target_pairs={{0,7},{1,0},{2,1},{3,2},{4,3},{5,4},{6,5},{7,6},{8,15},{9,8},{10,9... | collective-permute-start | bytes 138248 | tf_op jit(solution)/shard_map/ppermute | solution.py:448
  38.2 0.0 all-to-all-done.received_ref
  38.2 0.0 copy-start.2
  38.2 0.8 copy-done.2
  39.0 2.3 %mix.2.order_ref = f32[128,5,128]{2,1,0:T(8,128)} custom-call(f32[2,3]{1,0:T(2,128)} %exponential_divide_fusion.mixture_ref, f32[128,5,128]{2,1,0:T(8,128)} %copy-done.2, f32[5,40,128]{2,1,0:T(8,128)} %get-tuple-element.20.weights_ref), custom_call_target="tpu_custom_call" | custom-call | flops 1000000 | bytes 4000000 | tf_op jit(solution)/shard_map/mix/pallas_call | solution.py:351
  41.2 7.8 %all-to-all-start.1 = ((f32[128,5,128]{2,1,0:T(8,128)}), f32[128,5,128]{2,1,0:T(8,128)S(1)}, u32[]{:S(2)}, u32[]{:S(2)}) async-start(f32[128,5,128]{2,1,0:T(8,128)} %mix.2.order_ref), calls=%async_computation.1 | async-start | bytes 1048576 | tf_op jit(solution)/shard_map/all_to_all | solution.py:400
  49.1 0.6 slice_bitcast_fusion.6
  49.7 0.0 collective-permute-done.2.left_ref
  49.7 0.0 copy-start.5
  49.7 0.0 collective-permute-done.3.right_ref
  49.7 0.0 copy-start.6
  49.7 0.6 copy-done.5
  50.3 0.0 copy-done.6
  50.3 13.1 %conv_first.2.upper_ref = f32[1440,384]{1,0:T(8,128)} custom-call(f32[2,3]{1,0:T(2,128)} %exponential_divide_fusion.mixture_ref, bf16[20,128,256]{2,1,0:T(8,128)(2,1)} %bitcast.44, bf16[20,8,256]{2,1,0:T(8,128)(2,1)} %collective-permute-done.top_ref, bf16[20,8,256]{2,1,0:T(8,128)(2,1)} %copy-done.4, bf16[8,2880]{1,0:T(8,128)(2,1)} %copy-done.5, ...), custom_call_target="tpu_custom_call" | custom-call | flops 1000000000 | bytes 4000000 | tf_op jit(solution)/shard_map/conv_first/pallas_call | solution.py:351
  63.5 12.1 %conv_first.3.lower_ref = f32[1280,384]{1,0:T(8,128)} custom-call(f32[2,3]{1,0:T(2,128)} %exponential_divide_fusion.mixture_ref, bf16[20,128,256]{2,1,0:T(8,128)(2,1)} %bitcast.45, bf16[20,8,256]{2,1,0:T(8,128)(2,1)} %collective-permute-done.top_ref, bf16[20,8,256]{2,1,0:T(8,128)(2,1)} %copy-done.4, bf16[8,2880]{1,0:T(8,128)(2,1)} %copy-done.5, ...), custom_call_target="tpu_custom_call" | custom-call | flops 1000000000 | bytes 4000000 | tf_op jit(solution)/shard_map/conv_first/pallas_call | solution.py:351
  75.6 0.0 all-to-all-done.1.gathered_ref
  75.6 0.0 copy-start
  75.6 0.8 copy-done
  76.4 10.8 %middle.1 = (f32[2720,384]{1,0:T(8,128)}, f32[128,5,128]{2,1,0:T(8,128)}) custom-call(s32[2]{0:T(128)} %pad_add_fusion.place_ref.order_ref, f32[2,20]{1,0:T(2,128)} %bias_ref.3, f32[128,5,128]{2,1,0:T(8,128)} %copy-done, bf16[8,2,64,768]{3,2,1,0:T(8,128)(2,1)} %constant.39.clone.icols_ref, bf16[16,2,136,128]{3,2,1,0:T(8,128)(2,1)} %constant.37.clone.irows_ref, ...), custom_call_target="tpu_custom_call" | custom-call | flops 1000000000 | bytes 4000000 | tf_op jit(solution)/shard_map/middle/pallas_call | solution.py:379
  87.2 22.9 %all_to_all.20.received_ref = f32[128,5,128]{2,1,0:T(8,128)} all-to-all(f32[128,5,128]{2,1,0:T(8,128)} %get-tuple-element.11), channel_id=1, replica_groups=mesh['gx'=16,'gy'=8] {'gx','gy'}, dimensions={0} | all-to-all | bytes 655360 | tf_op jit(solution)/shard_map/all_to_all | solution.py:400
  110.1 2.2 %mix.3.order_ref = f32[128,5,128]{2,1,0:T(8,128)} custom-call(f32[2,3]{1,0:T(2,128)} %exponential_divide_fusion.mixture_ref, f32[128,5,128]{2,1,0:T(8,128)} %all_to_all.20.received_ref, f32[5,40,128]{2,1,0:T(8,128)} %get-tuple-element.19.weights_ref), custom_call_target="tpu_custom_call" | custom-call | flops 1000000 | bytes 4000000 | tf_op jit(solution)/shard_map/mix/pallas_call | solution.py:351
  112.4 4.8 %all-to-all-start.3 = ((f32[128,5,128]{2,1,0:T(8,128)}), f32[128,5,128]{2,1,0:T(8,128)S(1)}, u32[]{:S(2)}, u32[]{:S(2)}) async-start(f32[128,5,128]{2,1,0:T(8,128)} %mix.3.order_ref), calls=%async_computation.3 | async-start | bytes 1048576 | tf_op jit(solution)/shard_map/all_to_all | solution.py:400
  117.2 10.5 %conv_second.2.upper_ref = f32[1280,256]{1,0:T(8,128)} custom-call(f32[2,3]{1,0:T(2,128)} %exponential_divide_fusion.mixture_ref, f32[2720,384]{1,0:T(8,128)} %get-tuple-element.12.field_ref, bf16[3,20,60]{2,1,0:T(8,128)(2,1)} %get-tuple-element.23.near_ref, bf16[5,20,100]{2,1,0:T(8,128)(2,1)} %get-tuple-element.21.far_ref, ...), custom_call_target="tpu_custom_call" | custom-call | flops 1000000000 | bytes 4000000 | tf_op jit(solution)/shard_map/conv_second/pallas_call | solution.py:351
  127.7 10.5 %conv_second.3.lower_ref = f32[1280,256]{1,0:T(8,128)} custom-call(f32[2,3]{1,0:T(2,128)} %exponential_divide_fusion.mixture_ref, f32[2720,384]{1,0:T(8,128)} %get-tuple-element.12.field_ref, bf16[3,20,60]{2,1,0:T(8,128)(2,1)} %get-tuple-element.23.near_ref, bf16[5,20,100]{2,1,0:T(8,128)(2,1)} %get-tuple-element.21.far_ref, ...), custom_call_target="tpu_custom_call" | custom-call | flops 1000000000 | bytes 4000000 | tf_op jit(solution)/shard_map/conv_second/pallas_call | solution.py:351
  138.2 0.0 all-to-all-done.3.gathered_ref
  138.2 0.0 copy-start.1
  138.2 0.8 copy-done.1
  139.0 6.0 %last.1 = bf16[20,128,256]{2,1,0:T(8,128)(2,1)} custom-call(s32[2]{0:T(128)} %pad_add_fusion.place_ref.order_ref, f32[2,20]{1,0:T(2,128)} %bias_ref.3, f32[128,5,128]{2,1,0:T(8,128)} %copy-done.1, bf16[8,2,64,512]{3,2,1,0:T(8,128)(2,1)} %constant.38.clone.icols_ref, bf16[16,2,128,128]{3,2,1,0:T(8,128)(2,1)} %constant.36.clone.irows_ref, ...), custom_call_target="tpu_custom_call" | custom-call | flops 1000000000 | bytes 4000000 | tf_op jit(solution)/shard_map/last/pallas_call | solution.py:379
  (5 shorter events, 0.1 us)
Async XLA Ops:
  1.6 28.9 %collective-permute-start.1 = (bf16[20,8,256]{2,1,0:T(8,128)(2,1)}, bf16[20,8,256]{2,1,0:T(8,128)(2,1)S(1)}, u32[]{:S(2)}, u32[]{:S(2)}) collective-permute-start(bf16[20,8,256]{2,1,0:T(8,128)(2,1)} %get-tuple-element.13), channel_id=1, source_target_pairs={{0,120},{8,0},{16,8},{24,16},{32,24},{40,32},{48,40},{56,48},{64,5... | collective-permute-start | bytes 245768 | tf_op jit(solution)/shard_map/ppermute | solution.py:412
  7.6 22.9 %collective-permute-start = (bf16[20,8,256]{2,1,0:T(8,128)(2,1)}, bf16[20,8,256]{2,1,0:T(8,128)(2,1)}, u32[]{:S(2)}, u32[]{:S(2)}) collective-permute-start(bf16[20,8,256]{2,1,0:T(8,128)(2,1)} %get-tuple-element.14), channel_id=1, source_target_pairs={{0,8},{8,16},{16,24},{24,32},{32,40},{40,48},{48,56},{56,64},{64,7... | collective-permute-start | bytes 245768 | tf_op jit(solution)/shard_map/ppermute | solution.py:411
  8.3 14.9 %copy-start.3 = (f32[2,2,20,20,16]{3,4,2,1,0:T(8,128)S(1)}, f32[2,2,20,20,16]{3,4,2,1,0:T(8,128)}, u32[]{:S(2)}) copy-start(f32[2,2,20,20,16]{3,4,2,1,0:T(8,128)} %param.18) | copy-start | bytes 307204
  13.3 10.0 %copy-start.7 = (bf16[2,20,500]{2,0,1:T(2,128)(2,1)S(1)}, bf16[2,20,500]{2,0,1:T(2,128)(2,1)}, u32[]{:S(2)}) copy-start(bf16[2,20,500]{2,0,1:T(2,128)(2,1)} %param.20) | copy-start | bytes 120004
  13.3 24.9 %all-to-all-start = ((f32[128,5,128]{2,1,0:T(8,128)}), f32[128,5,128]{2,1,0:T(8,128)S(1)}, u32[]{:S(2)}, u32[]{:S(2)}) async-start(f32[128,5,128]{2,1,0:T(8,128)} %forward.1), calls=%async_computation | async-start | bytes 1048576 | tf_op jit(solution)/shard_map/all_to_all | solution.py:400
  26.9 2.8 %copy-start.9 = (f32[2,3]{1,0:T(2,128)S(1)}, f32[2,3]{1,0:T(2,128)}, u32[]{:S(2)}) copy-start(f32[2,3]{1,0:T(2,128)} %param.21) | copy-start | bytes 76
  26.9 3.5 %copy-start.8 = (bf16[2,20,180]{2,0,1:T(2,128)(2,1)S(1)}, bf16[2,20,180]{2,0,1:T(2,128)(2,1)}, u32[]{:S(2)}) copy-start(bf16[2,20,180]{2,0,1:T(2,128)(2,1)} %param.19) | copy-start | bytes 43204
  30.5 0.6 copy-start.4
  34.0 15.6 %collective-permute-start.2 = (bf16[8,2880]{1,0:T(8,128)(2,1)}, bf16[8,2880]{1,0:T(8,128)(2,1)S(1)}, u32[]{:S(2)}, u32[]{:S(2)}) collective-permute-start(bf16[8,2880]{1,0:T(8,128)(2,1)} %get-tuple-element.9), channel_id=1, source_target_pairs={{0,1},{1,2},{2,3},{3,4},{4,5},{5,6},{6,7},{7,0},{8,9},{9,10},{10,1... | collective-permute-start | bytes 138248 | tf_op jit(solution)/shard_map/ppermute | solution.py:447
  35.0 14.7 %collective-permute-start.3 = (bf16[8,2880]{1,0:T(8,128)(2,1)}, bf16[8,2880]{1,0:T(8,128)(2,1)S(1)}, u32[]{:S(2)}, u32[]{:S(2)}) collective-permute-start(bf16[8,2880]{1,0:T(8,128)(2,1)} %get-tuple-element.10), channel_id=1, source_target_pairs={{0,7},{1,0},{2,1},{3,2},{4,3},{5,4},{6,5},{7,6},{8,15},{9,8},{10,9... | collective-permute-start | bytes 138248 | tf_op jit(solution)/shard_map/ppermute | solution.py:448
  38.2 0.8 copy-start.2
  41.2 34.4 %all-to-all-start.1 = ((f32[128,5,128]{2,1,0:T(8,128)}), f32[128,5,128]{2,1,0:T(8,128)S(1)}, u32[]{:S(2)}, u32[]{:S(2)}) async-start(f32[128,5,128]{2,1,0:T(8,128)} %mix.2.order_ref), calls=%async_computation.1 | async-start | bytes 1048576 | tf_op jit(solution)/shard_map/all_to_all | solution.py:400
  49.7 0.6 copy-start.5
  49.7 0.6 copy-start.6
  75.6 0.8 copy-start
  112.4 25.8 %all-to-all-start.3 = ((f32[128,5,128]{2,1,0:T(8,128)}), f32[128,5,128]{2,1,0:T(8,128)S(1)}, u32[]{:S(2)}, u32[]{:S(2)}) async-start(f32[128,5,128]{2,1,0:T(8,128)} %mix.3.order_ref), calls=%async_computation.3 | async-start | bytes 1048576 | tf_op jit(solution)/shard_map/all_to_all | solution.py:400
  138.2 0.8 copy-start.1

commit v2 on v1

v2 whole, which is shorter than its diff:
```python
import functools
import math

import jax
import jax.numpy as jnp
import ml_dtypes
import numpy as np
from jax import lax
from jax.experimental import pallas as pl
from jax.experimental.pallas import tpu as pltpu
from jax.sharding import PartitionSpec as P

NX = 2048
NY = 2048
C = 20
LAYERS = 2
ROWS = 128
COLS = 256
GROUPS = 5
WIDE = 384
BLOCK = 8 * C

f32 = jnp.float32
bf16 = jnp.bfloat16
both = ("gx", "gy")
WIRES = (jnp.float32, jnp.bfloat16)


def wave(numbers, positions, length):
    product = numbers.astype(np.int64)[:, None] * positions.astype(np.int64)[None, :]
    scale = np.float32(2.0 * math.pi / length)
    angle = (product % length).astype(np.float32) * scale
    angle = angle.astype(np.float64)
    return np.cos(angle).astype(np.float32), np.sin(angle).astype(np.float32)


def halves(value):
    high = value.astype(ml_dtypes.bfloat16)
    low = (value - high.astype(np.float32)).astype(ml_dtypes.bfloat16)
    return high, low


ky_all = np.arange(32)
kx_all = np.concatenate([np.arange(32), np.arange(32) + NX - 32])


def forward_cols():
    cosine, sine = wave(ky_all, np.arange(NY), NY)
    cosine, sine = cosine.T.reshape(NY, 2, 1, 16), sine.T.reshape(NY, 2, 1, 16)
    first = np.stack([cosine, -sine], axis=3)
    second = np.stack([-sine, -cosine], axis=3)
    tables = [np.broadcast_to(t, (NY, 2, 4, 2, 16)).reshape(NY, 256) for t in (first, second)]
    return np.stack(tables).astype(ml_dtypes.bfloat16)


def forward_rows(before, count):
    out = np.zeros((16, 2, 64, 2 * count), ml_dtypes.bfloat16)
    for device in range(16):
        cosine, sine = wave(kx_all, np.arange(ROWS) + device * ROWS, NX)
        table = np.zeros((2, 64, count), np.float32)
        table[0, :, before : before + ROWS] = cosine
        table[1, :, before : before + ROWS] = sine
        high, low = halves(np.transpose(table, (1, 0, 2)).reshape(64, 2 * count))
        out[device, 0], out[device, 1] = high, low
    return out


def inverse_rows(before, count):
    out = np.zeros((16, 2, count, 128), ml_dtypes.bfloat16)
    for device in range(16):
        positions = (np.arange(count) - before + device * ROWS) % NX
        cosine, sine = wave(kx_all, positions, NX)
        high, low = halves(np.concatenate([cosine.T, -sine.T], axis=1))
        out[device, 0], out[device, 1] = high, low
    return out


def inverse_cols():
    width = COLS
    out = np.zeros((8, 2, 64, 2 * width), ml_dtypes.bfloat16)
    weight = (np.where(ky_all == 0, 1.0, 2.0) / (NX * NY)).astype(np.float32)[:, None]
    for device in range(8):
        cosine, sine = wave(ky_all, np.arange(width) + device * COLS, NY)
        cosine, sine = cosine * weight, sine * weight
        real = np.concatenate([cosine, sine], axis=1)
        imaginary = np.concatenate([-sine, cosine], axis=1)
        table = np.stack([real.reshape(2, 16, 2 * width), imaginary.reshape(2, 16, 2 * width)], 1)
        high, low = halves(table.reshape(64, 2 * width))
        out[device, 0], out[device, 1] = high, low
    return out


def spread(taps, slots_first):
    width = 2 * taps * BLOCK
    lanes = np.arange(width) % (taps * BLOCK) // 8
    step, channel = lanes // C, lanes % C
    if slots_first:
        channel = channel % GROUPS * 4 + channel // GROUPS
    columns = step * C + channel
    return (np.arange(taps * C)[:, None] == columns[None, :]).astype(ml_dtypes.bfloat16)


def offsets(taps):
    width = 2 * taps * BLOCK
    lanes = np.arange(width)
    place = lanes // (taps * BLOCK) * 8 + lanes % 8
    return (place[None, :] - np.arange(8)[:, None] - 4).astype(np.int32)


def split(value):
    high = value.astype(bf16)
    return high, (value - high.astype(f32)).astype(bf16)


def mul(a, b):
    return jnp.dot(a, b, preferred_element_type=f32)


def fetch(pairs):
    copies = [pltpu.make_async_copy(source, target, sem) for source, target, sem in pairs]
    for copy in copies:
        copy.start()
    return copies


def transform(planes, cols_ref, rows_ref, write):
    lane = lax.broadcasted_iota(jnp.int32, (COLS, 256), 1)
    slot = (lane >> 5) & 3
    zero = jnp.zeros((), bf16)
    placed = [[jnp.where(slot == i, cols_ref[t], zero) for i in range(4)] for t in range(2)]
    rows_high, rows_low = rows_ref[0], rows_ref[1]
    for group in range(GROUPS):
        members = [planes(4 * group + i) for i in range(4)]
        sums = []
        for t in range(2):
            total = mul(members[0], placed[t][0])
            for i in range(1, 4):
                total = total + mul(members[i], placed[t][i])
            sums.append(total)
        high, low = split(jnp.concatenate(sums, axis=0))
        modes = mul(rows_high, high) + mul(rows_high, low) + mul(rows_low, high)
        for half in range(2):
            write(half, group, modes[:, 128 * half : 128 * half + 128])


def indices():
    return lax.axis_index("gx"), lax.axis_index("gy")


def forward_kernel(
    grid_all, cols_all, rows_all, out_ref, first_ref, last_ref, grid_buffer, cols, rows, sems
):
    gx, gy = indices()
    start = pl.multiple_of(gy * COLS, COLS)
    copies = fetch(
        [
            (cols_all.at[:, pl.ds(start, COLS), :], cols, sems.at[0]),
            (rows_all.at[0, gx, :, :, pl.ds(0, 2 * ROWS)], rows, sems.at[1]),
        ]
        + [
            (grid_all.at[pl.ds(4 * g, 4)], grid_buffer.at[pl.ds(4 * g, 4)], sems.at[2 + g])
            for g in range(GROUPS)
        ]
    )
    copies[0].wait()
    copies[1].wait()

    def plane(c):
        if c % 4 == 0:
            copies[2 + c // 4].wait()
        return grid_buffer[c]

    def write(half, group, value):
        out_ref[pl.ds(half, 64, stride=2), group, :] = value

    transform(plane, cols, rows, write)
    edges(grid_buffer[...].reshape(C * ROWS, COLS), first_ref, last_ref)


def mixture_of(logits_ref, layer):
    exponents = jnp.exp(logits_ref[layer : layer + 1, :])
    weights = exponents / jnp.sum(exponents, axis=1, keepdims=True)
    return [weights[:, i : i + 1] for i in range(3)]


def mix_kernel(logits_ref, received_ref, weights_all, order_ref, out_ref, marker_ref, weights_ref, sem, *, layer):
    (copy,) = fetch([(weights_all.at[layer], weights_ref, sem)])
    total = jnp.sum(received_ref[...].astype(f32), axis=0)
    total = jnp.concatenate([total, jnp.zeros((8 - GROUPS, 128), f32)], axis=0)
    columns = jnp.transpose(total)
    real = jnp.zeros((16, C), f32)
    imaginary = jnp.zeros((16, C), f32)
    copy.wait()
    for c in range(C):
        group, start = c // 4, c % 4 * 32
        in_real = columns[start : start + 16, group : group + 1]
        in_imaginary = columns[start + 16 : start + 32, group : group + 1]
        weight_real, weight_imaginary = weights_ref[0, c], weights_ref[1, c]
        real = real + weight_real * in_real - weight_imaginary * in_imaginary
        imaginary = imaginary + weight_real * in_imaginary + weight_imaginary * in_real
    scale = mixture_of(logits_ref, layer)[0]
    lines = jnp.transpose(jnp.concatenate([real * scale, imaginary * scale] * 4, axis=0))
    lane = lax.broadcasted_iota(jnp.int32, (C, 128), 1)
    row = lax.broadcasted_iota(jnp.int32, (C, 128), 0)
    lines = jnp.where((lane >> 5) == (row & 3), lines, 0.0)
    group = lax.broadcasted_iota(jnp.int32, (8, C), 0)
    member = lax.broadcasted_iota(jnp.int32, (8, C), 1)
    gather = jnp.where((member >> 2) == group, 1.0, 0.0)
    mixed = jnp.dot(gather, lines, precision=lax.Precision.HIGHEST, preferred_element_type=f32)
    mixed = mixed[:GROUPS].astype(out_ref.dtype)
    out_ref[...] = jnp.broadcast_to(mixed[None], out_ref.shape)
    marker_ref[...] = lines[:8]


def edge_patterns():
    pick = lax.broadcasted_iota(jnp.int32, (8, COLS), 1) - lax.broadcasted_iota(
        jnp.int32, (8, COLS), 0
    )
    first = jnp.where(pick == 0, 1.0, 0.0).astype(bf16)
    last = jnp.where(pick == COLS - 8, 1.0, 0.0).astype(bf16)
    return first, last


def edge_columns(rows):
    dims = (((1,), (1,)), ((), ()))
    return [
        lax.dot_general(pattern, rows, dims, preferred_element_type=f32).astype(bf16)
        for pattern in edge_patterns()
    ]


def edges(rows, first_ref, last_ref):
    first_ref[...], last_ref[...] = edge_columns(rows)


def edges_kernel(top_ref, bottom_ref, first_ref, last_ref, first_out, last_out):
    rows = [r[...].reshape(BLOCK, COLS) for r in (top_ref, bottom_ref)]
    found = edge_columns(jnp.concatenate(rows, axis=0))
    for own_ref, extra, out_ref in zip((first_ref, last_ref), found, (first_out, last_out)):
        out_ref[:, : C * ROWS] = own_ref[...]
        out_ref[:, C * ROWS :] = extra


def banded(weights, spread_ref, offsets_ref, steps, width):
    offset = offsets_ref[...][None]
    total = jnp.zeros((C, 8, width), f32)
    taps = len(steps) * C
    for index, step in enumerate(steps):
        own = mul(weights[:, taps * index : taps * index + taps], spread_ref[...])
        total = jnp.where(offset == step, own[:, None, :], total)
    return total.reshape(BLOCK, width).astype(bf16)


NEAR = (-1, 0, 1)
FAR = (-4, -2, 0, 2, 4)


def conv_kernel(logits_ref, *refs, layer, count):
    sources, refs = (refs[:3], refs[3:]) if layer == 0 else (refs[:1], refs[1:])
    left_ref, right_ref, near_ref, far_ref, refs = *refs[:4], refs[4:]
    near_spread, far_spread, near_offsets, far_offsets, order_ref, out_all, marker_ref, *refs = refs
    field, out_ref, near_band, far_band, near_stack, far_stack, *refs = refs
    sems, out_sems, *refs = refs
    if layer == 0:
        grid_all, top_ref, bottom_ref = sources
        (grid_ref,) = refs
        copies = fetch(
            [
                (grid_all.at[pl.ds(4 * g, 4)], grid_ref.at[pl.ds(4 * g, 4)], sems.at[g])
                for g in range(GROUPS)
            ]
        )
    else:
        (field_all,) = sources
        pieces = [pl.ds(i * BLOCK, min(3, count + 1 - i) * BLOCK) for i in range(0, count + 1, 3)]
        copies = fetch(
            [(field_all.at[p], field.at[p], sems.at[k]) for k, p in enumerate(pieces)]
        )
    near_band[...] = banded(near_ref[layer], near_spread, near_offsets, NEAR, 6 * BLOCK)
    far_band[...] = banded(far_ref[layer], far_spread, far_offsets, FAR, 10 * BLOCK)
    lane = lax.broadcasted_iota(jnp.int32, (16, 128), 1)
    row = lax.broadcasted_iota(jnp.int32, (16, 128), 0)
    sides_place = jnp.where(lane == jnp.where(row < 8, row, row + 112), 1.0, 0.0).astype(bf16)
    sides = jnp.concatenate([right_ref[...].astype(f32), left_ref[...].astype(f32)], axis=0)
    side = lax.dot_general(
        sides.astype(bf16), sides_place, (((0,), (0,)), ((), ())), preferred_element_type=f32
    )
    if layer == 0:
        for pair in range(C // 2):
            if pair % 2 == 0:
                copies[pair // 2].wait()
            inner = [grid_ref[2 * pair + i].astype(f32) for i in range(2)]
            upper = [top_ref[2 * pair + i].astype(f32) for i in range(2)]
            lower = [bottom_ref[2 * pair + i].astype(f32) for i in range(2)]
            for block in range(18):
                if block == 0:
                    value = upper
                elif block == 17:
                    value = lower
                else:
                    value = [v[8 * block - 8 : 8 * block] for v in inner]
                place = block * BLOCK + 16 * pair
                field[place : place + 16, :] = jnp.concatenate(value, axis=0).astype(bf16)

    def side_of(block):
        if layer == 1 or block in (0, 17):
            start = block * BLOCK if layer == 1 else C * ROWS + (block > 0) * BLOCK
            return side[start : start + BLOCK].astype(bf16)
        starts = [c * ROWS + 8 * block - 8 for c in range(C)]
        return jnp.concatenate([side[p : p + 8] for p in starts], axis=0).astype(bf16)

    _, near_scale, far_scale = mixture_of(logits_ref, layer)
    results = []
    for index in range(count + 1):
        if layer == 1 and index % 3 == 0:
            copies[index // 3].wait()
        rows = slice(index * BLOCK, index * BLOCK + BLOCK)
        block = jnp.concatenate([field[rows, :], side_of(index)], axis=1)
        moved = {0: block}
        for step in (-4, -2, -1, 1, 2, 4):
            moved[step] = pltpu.roll(block, (-step) % WIDE, 1)
        for steps, stack in ((NEAR, near_stack), (FAR, far_stack)):
            for position, step in enumerate(steps):
                start = (index * len(steps) + position) * BLOCK
                stack[start : start + BLOCK, :] = moved[step][:, :COLS]
        if index == 0:
            continue
        done = index - 1
        near_rows = near_stack[done * 3 * BLOCK : (done + 2) * 3 * BLOCK, :]
        far_rows = far_stack[done * 5 * BLOCK : (done + 2) * 5 * BLOCK, :]
        total = near_scale * mul(near_band[...], near_rows) + far_scale * mul(
            far_band[...], far_rows
        )
        out_ref[done * BLOCK : done * BLOCK + BLOCK, :] = total
        piece = pl.ds(done * BLOCK, BLOCK)
        results += fetch([(out_ref.at[piece], out_all.at[piece], out_sems.at[done])])
    marker_ref[...] = total[:8, :128]
    for copy in results:
        copy.wait()


def gelu(value):
    return 0.5 * value * (1.0 + lax.erf(value * math.sqrt(0.5)))


def expand(bias_ref, gathered, cols, rows, conv_ref, conv_copy, layer, blocks, emit):
    parts = []
    for group in range(GROUPS):
        pair = [gathered[pl.ds(half, 64, stride=2), group, :] for half in range(2)]
        parts.append(jnp.concatenate(pair, axis=1))
    high, low = split(jnp.concatenate(parts, axis=0))
    stacked = jnp.concatenate([high, low], axis=0)
    rows_high, rows_low = rows[0], rows[1]
    rows_twice = jnp.concatenate([rows_high, rows_high], axis=1)
    empty = jnp.zeros((32, 2 * COLS), bf16)
    for slot in range(4):
        placed = []
        for t in range(2):
            table = cols[t]
            pieces = []
            for half in range(2):
                own = table[32 * half : 32 * half + 32]
                pieces += [own if i == slot else empty for i in range(4)]
            placed.append(jnp.concatenate(pieces, axis=0))
        first = mul(stacked, placed[0])
        lines = first[:320] + first[320:] + mul(high, placed[1])
        if slot == 0:
            conv_copy.wait()
        for group in range(GROUPS):
            channel = 4 * group + slot
            here = lines[64 * group : 64 * group + 64]
            line_high, line_low = split(jnp.concatenate([here[:, :COLS], here[:, COLS:]], axis=0))
            value = mul(rows_twice, jnp.concatenate([line_high, line_low], axis=0)) + mul(
                rows_low, line_high
            )
            local = []
            for block in range(blocks):
                place = block * BLOCK + 8 * channel
                local.append(conv_ref[place : place + 8, :])
            value = value + jnp.concatenate(local, axis=0) + bias_ref[layer, channel]
            emit(slot * GROUPS + group, channel, gelu(value))


def middle_kernel(
    bias_ref, gathered_ref, icols_all, irows_all, fcols_all, frows_all, conv_all,
    field_all, first_ref, last_ref, out_ref,
    planes, chunk, icols, irows, fcols, frows, conv_ref, field_ref, sems,
):
    gx, gy = indices()
    start = pl.multiple_of(gy * COLS, COLS)
    copies = fetch(
        [
            (icols_all.at[0, gy], icols, sems.at[0]),
            (irows_all.at[1, gx], irows, sems.at[1]),
            (fcols_all.at[:, pl.ds(start, COLS), :], fcols, sems.at[2]),
            (conv_all, conv_ref, sems.at[4]),
            (frows_all.at[1, gx], frows, sems.at[3]),
        ]
    )
    copies[0].wait()
    copies[1].wait()
    waiting = []

    def emit(order, channel, value):
        rounded = value.astype(bf16)
        planes[channel, :136] = rounded
        planes[channel, 136:] = jnp.zeros((8, COLS), bf16)
        waiting.append(rounded.astype(f32))
        if order % 2 == 1:
            for block in range(17):
                rows = slice(8 * block, 8 * block + 8)
                both_rows = jnp.concatenate([waiting[0][rows], waiting[1][rows]], axis=0)
                place = block * BLOCK + 8 * (order - 1)
                field_ref[place : place + 16, :] = both_rows.astype(bf16)
            waiting.clear()

    expand(bias_ref, gathered_ref, icols, irows, conv_ref, copies[3], 0, 17, emit)
    (result,) = fetch([(field_ref, field_all, sems.at[5])])
    edges(field_ref[...], first_ref, last_ref)
    copies[2].wait()
    copies[4].wait()

    def write(half, group, value):
        chunk[pl.ds(half, 64, stride=2), group, :] = value

    transform(lambda c: planes[c], fcols, frows, write)
    out_ref[...] = chunk[...].astype(out_ref.dtype)
    result.wait()


def last_kernel(
    bias_ref, gathered_ref, icols_all, irows_all, conv_all, out_all,
    wide, icols, irows, conv_ref, out_ref, sems, out_sems,
):
    gx, gy = indices()
    copies = fetch(
        [
            (icols_all.at[0, gy], icols, sems.at[0]),
            (irows_all.at[0, gx, :, pl.ds(0, ROWS)], irows, sems.at[1]),
            (conv_all, conv_ref, sems.at[2]),
        ]
    )
    wide[...] = gathered_ref[...].astype(f32)
    copies[0].wait()
    copies[1].wait()
    results = []

    def emit(order, channel, value):
        out_ref[channel] = value.astype(bf16)
        results.extend(fetch([(out_ref.at[channel], out_all.at[channel], out_sems.at[channel])]))

    expand(bias_ref, wide, icols, irows, conv_ref, copies[2], 1, 16, emit)
    for copy in results:
        copy.wait()


vmem = pl.BlockSpec(memory_space=pltpu.VMEM)
smem = pl.BlockSpec(memory_space=pltpu.SMEM)
anywhere = pl.BlockSpec(memory_space=pl.ANY)
hbm = pl.BlockSpec(memory_space=pltpu.HBM)
LIMIT = 56 * 10**6
SMALL = 4 * 10**6


def call(kernel, outs, args, specs, scratch=(), out_specs=None, flops=10**9, limit=LIMIT, name=None):
    single = not isinstance(outs, (list, tuple))
    if out_specs is None:
        out_specs = vmem if single else [vmem] * len(outs)
    return pl.pallas_call(
        kernel,
        out_shape=outs,
        in_specs=specs,
        out_specs=out_specs,
        scratch_shapes=list(scratch),
        compiler_params=pltpu.CompilerParams(vmem_limit_bytes=limit),
        cost_estimate=pl.CostEstimate(flops=flops, bytes_accessed=4 * 10**6, transcendentals=0),
        name=name,
    )(*args)


def shape_of(dims, kind):
    return jax.ShapeDtypeStruct(dims, kind)


def exchange(value):
    return lax.all_to_all(value, both, split_axis=0, concat_axis=0, tiled=True)


def ring(axis, step):
    size = lax.axis_size(axis)
    return [(i, (i + step) % size) for i in range(size)]


def sides(first, last):
    left = lax.ppermute(last, "gy", ring("gy", 1))
    right = lax.ppermute(first, "gy", ring("gy", -1))
    return left, right


def on_device(grid_field, spectral_weight, conv_near, conv_far, mix_logits, channel_bias):
    grid = grid_field[0]
    top = lax.ppermute(grid[:, ROWS - 8 :], "gx", ring("gx", 1))
    bottom = lax.ppermute(grid[:, :8], "gx", ring("gx", -1))
    mode_weights = jnp.swapaxes(spectral_weight, 3, 4)

    fcols = jnp.asarray(forward_cols())
    plain, wide = forward_rows(0, ROWS), forward_rows(4, 144)
    frows = np.zeros((2,) + wide.shape, wide.dtype)
    frows[0, ..., : 2 * ROWS], frows[1] = plain, wide
    plain, wide = inverse_rows(0, ROWS), inverse_rows(4, 136)
    irows = np.zeros((2,) + wide.shape, wide.dtype)
    irows[0, :, :, :ROWS], irows[1] = plain, wide
    icols = np.stack([inverse_cols()] * 2)
    frows, irows, icols = jnp.asarray(frows), jnp.asarray(irows), jnp.asarray(icols)

    chunks = [shape_of((128, GROUPS, 128), kind) for kind in WIRES]
    dma = pltpu.SemaphoreType.DMA
    icols_buffer = pltpu.VMEM((2, 64, 2 * COLS), bf16)
    fcols_buffer = pltpu.VMEM((2, COLS, 256), bf16)

    partial, first, last = call(
        forward_kernel, [chunks[0]] + [shape_of((8, C * ROWS), bf16)] * 2, (grid, fcols, frows),
        [hbm] * 3,
        (
            pltpu.VMEM((C, ROWS, COLS), bf16), fcols_buffer, pltpu.VMEM((2, 64, 2 * ROWS), bf16),
            dma((2 + GROUPS,)),
        ),
        name="forward",
    )
    received = exchange(partial)
    first, last = call(
        edges_kernel, [shape_of((8, 18 * BLOCK), bf16)] * 2, (top, bottom, first, last),
        [vmem] * 4, limit=SMALL, name="edges",
    )

    def mix(layer, received, order):
        return call(
            functools.partial(mix_kernel, layer=layer), [chunks[layer], shape_of((8, 128), f32)],
            (mix_logits, received, mode_weights, order), [vmem, vmem, hbm, anywhere],
            (pltpu.VMEM((2, C, 16, C), f32), dma), flops=10**6, limit=SMALL, name="mix",
        )

    def conv(layer, sources, specs, sides, count, order):
        tables = (spread(3, layer), spread(5, layer), offsets(3), offsets(5))
        return call(
            functools.partial(conv_kernel, layer=layer, count=count),
            [shape_of((count * BLOCK, COLS), f32), shape_of((8, 128), f32)],
            (mix_logits, *sources, *sides, conv_near, conv_far, *map(jnp.asarray, tables), order),
            [vmem] + specs + [vmem] * 8 + [anywhere],
            [
                pltpu.VMEM(((count + 1) * BLOCK, COLS), bf16),
                pltpu.VMEM((count * BLOCK, COLS), f32),
                pltpu.VMEM((BLOCK, 6 * BLOCK), bf16),
                pltpu.VMEM((BLOCK, 10 * BLOCK), bf16),
                pltpu.VMEM(((count + 1) * 3 * BLOCK, COLS), bf16),
                pltpu.VMEM(((count + 1) * 5 * BLOCK, COLS), bf16),
                dma((6,)), dma((count,)),
            ]
            + [pltpu.VMEM((C, ROWS, COLS), bf16)] * (1 - layer),
            out_specs=[hbm, vmem], flops=2 * 10**10, name="conv",
        )

    around = sides(first, last)
    mixed, marker = mix(0, received, mix_logits)
    gathered = exchange(mixed)
    local, _ = conv(0, (grid, top, bottom), [hbm, vmem, vmem], around, 17, marker)
    field, first, last, partial = call(
        middle_kernel,
        [shape_of((17 * BLOCK, COLS), bf16)] + [shape_of((8, 17 * BLOCK), bf16)] * 2 + [chunks[1]],
        (channel_bias, gathered, icols, irows, fcols, frows, local),
        [smem, vmem] + [hbm] * 5,
        (
            pltpu.VMEM((C, 144, COLS), bf16), pltpu.VMEM((128, GROUPS, 128), f32),
            icols_buffer, pltpu.VMEM((2, 136, 128), bf16),
            fcols_buffer, pltpu.VMEM((2, 64, 288), bf16),
            pltpu.VMEM((17 * BLOCK, COLS), f32), pltpu.VMEM((17 * BLOCK, COLS), bf16), dma((6,)),
        ),
        out_specs=[hbm, vmem, vmem, vmem],
        name="middle",
    )
    received = exchange(partial)
    local, marker = conv(1, (field,), [hbm], sides(first, last), 16, mix_logits)
    mixed, _ = mix(1, received, marker)
    gathered = exchange(mixed)
    result = call(
        last_kernel, shape_of((C, ROWS, COLS), bf16),
        (channel_bias, gathered, icols, irows, local),
        [smem, vmem] + [hbm] * 3,
        (
            pltpu.VMEM((128, GROUPS, 128), f32), icols_buffer, pltpu.VMEM((2, ROWS, 128), bf16),
            pltpu.VMEM((16 * BLOCK, COLS), f32), pltpu.VMEM((C, ROWS, COLS), bf16),
            dma((3,)), dma((C,)),
        ),
        out_specs=hbm,
        name="last",
    )
    return result[None]


def solution(mesh):
    in_specs = (
        P(None, None, "gx", "gy"),
        P(None, None, None, None, both),
        P(),
        P(),
        P(),
        P(),
    )
    out_specs = P(None, None, "gx", "gy")
    return jax.shard_map(
        on_device, mesh=mesh, in_specs=in_specs, out_specs=out_specs, check_vma=False
    )
```

time: 146 us -> 110 us (0.75)
  Pallas kernels: 75.4 us -> 41.1 us
  waiting for transfers between devices: 0.02 us -> 12 us
  local copies, waits for them, and re-layouts: 12 us -> 1.86 us
  blocking collectives: 22.9 us -> 18.9 us
  other arithmetic: 1.68 us -> 0 us
  starting transfers between devices: 32.8 us -> 34.3 us
    pallas_call x10 -> x8, Pallas kernels: 75.4 us -> 41.1 us  [call(): pl.pallas_call(kernel, out_shape=outs, in_specs=specs, out_specs=out_spec...]
    ppermute x1, waiting for transfers between devices: 0.01 us -> 5.62 us  [on_device(): top = lax.ppermute(grid[:, ROWS - 8:], 'gx', ring('gx', 1))]
    all_to_all x3, waiting for transfers between devices: 0.01 us -> 4.29 us  [exchange(): return lax.all_to_all(value, both, split_axis=0, concat_axis=0, tiled=True)]
    ppermute x2 -> x4, starting transfers between devices: 4.14 us -> 8.41 us  [the longest x2 6.27 us: sides(): right = lax.ppermute(first, 'gy', ring('gy', -1))]
    all_to_all x1, blocking collectives: 22.9 us -> 18.9 us  [exchange(): return lax.all_to_all(value, both, split_axis=0, concat_axis=0, tiled=True)]
    unnamed x20, local copies, waits for them, and re-layouts: 3.64 us -> 0.85 us
    another operation x2 -> x0, local copies, waits for them, and re-layouts: 2.54 us -> none  [the longest x1 2.49 us: on_device(): weights = jnp.stack([from_real, from_imaginary], axis=2)]
    reshape x6 -> x0, local copies, waits for them, and re-layouts: 2.26 us -> none  [the longest x2 2.03 us: on_device(): weights = weights.reshape(LAYERS, 2 * C, GROUPS, 128)]
  transfers between devices with their start and end apart: 7 -> 9, of which waited for: 0 -> 4; matrix products, arithmetic and copies ran while one was open for 6% -> 1% of each run, Pallas kernels for 39% -> 19%
where the time goes in v2:
time: 110 us; the launch traced here: 109 us
  Pallas kernels  41.1 us (37%)
  starting transfers between devices  34.3 us (31%)
  blocking collectives  18.9 us (17%)
  waiting for transfers between devices  12 us (11%)
  local copies, waits for them, and re-layouts  1.86 us (2%)
    pallas_call x8, Pallas kernels, call(): pl.pallas_call(kernel, out_shape=outs, in_specs=specs, out_specs=out_spec...  41.1 us
    all_to_all x3, starting transfers between devices, exchange(): return lax.all_to_all(value, both, split_axis=0, concat_axis=0, tiled=True)  20.8 us
    all_to_all x1, blocking collectives, exchange(): return lax.all_to_all(value, both, split_axis=0, concat_axis=0, tiled=True)  18.9 us
    ppermute x2, starting transfers between devices, sides(): right = lax.ppermute(first, 'gy', ring('gy', -1))  6.27 us
    ppermute x1, waiting for transfers between devices, on_device(): top = lax.ppermute(grid[:, ROWS - 8:], 'gx', ring('gx', 1))  5.62 us
    ppermute x1, starting transfers between devices, on_device(): bottom = lax.ppermute(grid[:, :8], 'gx', ring('gx', -1))  5.09 us
    all_to_all x3, waiting for transfers between devices, exchange(): return lax.all_to_all(value, both, split_axis=0, concat_axis=0, tiled=True)  4.29 us
  transfers between devices with their start and end apart: 9, of which 4 were waited for; matrix products, arithmetic and copies ran while one was open for 1% of the time, Pallas kernels for 19%

profile of v2, /device:TPU:0, one launch (start us, length us, event | category | flops | bytes accessed | tf_op | source)
XLA Modules:
  0.0 108.5 jit_solution(6345125786743373948)
XLA Ops:
  0.0 4.7 %forward.1 = (f32[128,5,128]{2,1,0:T(8,128)}, bf16[8,2560]{1,0:T(8,128)(2,1)S(1)}, bf16[8,2560]{1,0:T(8,128)(2,1)S(1)}) custom-call(bf16[20,128,256]{2,1,0:T(8,128)(2,1)} %bitcast.5, bf16[2,2048,256]{2,1,0:T(8,128)(2,1)} %constant.20.clone.cols_all.fcols_all, bf16[2,16,2,64,288]{4,3,2,1,0:T(8,128)(2,1)} %constant.21.clone.rows_all.frows_all), custom_call_target="tpu_custom_call" | custom-call | flops 1000000000 | bytes 4000000 | tf_op jit(solution)/shard_map/forward/pallas_call | solution.py:469
  4.7 11.2 %all-to-all-start = ((f32[128,5,128]{2,1,0:T(8,128)}), f32[128,5,128]{2,1,0:T(8,128)S(1)}, u32[]{:S(2)}, u32[]{:S(2)}) async-start(f32[128,5,128]{2,1,0:T(8,128)} %get-tuple-element.20), calls=%async_computation | async-start | bytes 1048576 | tf_op jit(solution)/shard_map/all_to_all | solution.py:486
  15.9 0.0 copy-start.8
  15.9 0.0 copy-start.7
  15.9 0.0 copy-start
  15.9 0.0 copy-start.1
  15.9 1.0 fusion
  17.0 5.1 %collective-permute-start.1 = (bf16[20,8,256]{2,1,0:T(8,128)(2,1)S(1)}, bf16[20,8,256]{2,1,0:T(8,128)(2,1)S(1)}, u32[]{:S(2)}, u32[]{:S(2)}) collective-permute-start(bf16[20,8,256]{2,1,0:T(8,128)(2,1)S(1)} %get-tuple-element.35), channel_id=1, source_target_pairs={{0,120},{8,0},{16,8},{24,16},{32,24},{40,32},{48,40},{56,48},{64,5... | collective-permute-start | bytes 245768 | tf_op jit(solution)/shard_map/ppermute | solution.py:503
  22.0 0.0 collective-permute-start
  22.0 2.1 %collective-permute-done.1.bottom_ref.refs_2_ = bf16[20,8,256]{2,1,0:T(8,128)(2,1)S(1)} collective-permute-done((bf16[20,8,256]{2,1,0:T(8,128)(2,1)S(1)}, bf16[20,8,256]{2,1,0:T(8,128)(2,1)S(1)}, u32[]{:S(2)}, u32[]{:S(2)}) %collective-permute-start.1) | collective-permute-done | bytes 81952 | tf_op jit(solution)/shard_map/ppermute | solution.py:503
  24.1 5.6 %collective-permute-done.top_ref.refs_1_ = bf16[20,8,256]{2,1,0:T(8,128)(2,1)S(1)} collective-permute-done((bf16[20,8,256]{2,1,0:T(8,128)(2,1)S(1)}, bf16[20,8,256]{2,1,0:T(8,128)(2,1)S(1)}, u32[]{:S(2)}, u32[]{:S(2)}) %collective-permute-start) | collective-permute-done | bytes 81952 | tf_op jit(solution)/shard_map/ppermute | solution.py:502
  29.7 0.2 edges.1
  29.9 0.0 copy-start.4
  29.9 0.0 copy-start.5
  29.9 1.4 %collective-permute-start.2 = (bf16[8,2880]{1,0:T(8,128)(2,1)S(1)}, bf16[8,2880]{1,0:T(8,128)(2,1)S(1)}, u32[]{:S(2)}, u32[]{:S(2)}) collective-permute-start(bf16[8,2880]{1,0:T(8,128)(2,1)S(1)} %get-tuple-element.24), channel_id=1, source_target_pairs={{0,1},{1,2},{2,3},{3,4},{4,5},{5,6},{6,7},{7,0},{8,9},{9,10},{10,1... | collective-permute-start | bytes 138248 | tf_op jit(solution)/shard_map/ppermute | solution.py:495
  31.3 2.8 %collective-permute-start.3 = (bf16[8,2880]{1,0:T(8,128)(2,1)S(1)}, bf16[8,2880]{1,0:T(8,128)(2,1)S(1)}, u32[]{:S(2)}, u32[]{:S(2)}) collective-permute-start(bf16[8,2880]{1,0:T(8,128)(2,1)S(1)} %get-tuple-element.25), channel_id=1, source_target_pairs={{0,7},{1,0},{2,1},{3,2},{4,3},{5,4},{6,5},{7,6},{8,15},{9,8},{10,9... | collective-permute-start | bytes 138248 | tf_op jit(solution)/shard_map/ppermute | solution.py:496
  34.1 0.0 copy-done.8
  34.1 0.0 copy-done.7
  34.2 0.0 all-to-all-done.received_ref
  34.2 0.0 copy-done
  34.2 0.0 copy-done.1
  34.2 1.5 %mix.2 = (f32[128,5,128]{2,1,0:T(8,128)}, f32[8,128]{1,0:T(8,128)S(1)}) custom-call(f32[2,3]{1,0:T(2,128)S(1)} %copy-done.1, f32[128,5,128]{2,1,0:T(8,128)S(1)} %all-to-all-done.received_ref, f32[2,2,20,16,20]{4,3,2,1,0:T(8,128)S(1)} %bitcast.3, f32[2,3]{1,0:T(2,128)S(1)} %copy-done.1), custom_call_target="tpu_custom_call" | custom-call | flops 1000000 | bytes 4000000 | tf_op jit(solution)/shard_map/mix/pallas_call | solution.py:469
  35.7 4.8 %all-to-all-start.1 = ((f32[128,5,128]{2,1,0:T(8,128)}), f32[128,5,128]{2,1,0:T(8,128)S(1)}, u32[]{:S(2)}, u32[]{:S(2)}) async-start(f32[128,5,128]{2,1,0:T(8,128)} %get-tuple-element.21), calls=%async_computation.1 | async-start | bytes 1048576 | tf_op jit(solution)/shard_map/all_to_all | solution.py:486
  40.6 0.0 collective-permute-done.2.refs_3_
  40.6 0.0 collective-permute-done.3.refs_4_
  40.6 0.0 copy-done.4
  40.6 0.0 copy-done.5
  40.6 0.0 copy-start.2
  40.6 9.8 %conv.2 = (f32[2720,256]{1,0:T(8,128)}, f32[8,128]{1,0:T(8,128)}) custom-call(f32[2,3]{1,0:T(2,128)S(1)} %copy-done.1, bf16[20,128,256]{2,1,0:T(8,128)(2,1)} %bitcast.7, bf16[20,8,256]{2,1,0:T(8,128)(2,1)S(1)} %collective-permute-done.top_ref.refs_1_, bf16[20,8,256]{2,1,0:T(8,128)(2,1)S(1)} %collective-permute-done.1.bottom_ref.refs_2_, ...), custom_call_target="tpu_custom_call" | custom-call | flops 20000000000 | bytes 4000000 | tf_op jit(solution)/shard_map/conv/pallas_call | solution.py:469
  50.5 3.2 %all-to-all-done.1.gathered_ref = f32[128,5,128]{2,1,0:T(8,128)S(1)} async-done(((f32[128,5,128]{2,1,0:T(8,128)}), f32[128,5,128]{2,1,0:T(8,128)S(1)}, u32[]{:S(2)}, u32[]{:S(2)}) %all-to-all-start.1) | async-done | bytes 327712 | tf_op jit(solution)/shard_map/all_to_all | solution.py:486
  53.6 0.0 copy-start.6
  53.6 0.8 copy-done.6
  54.4 0.0 copy-done.2
  54.4 0.0 copy-start.3
  54.4 9.2 %middle.1 = (bf16[2720,256]{1,0:T(8,128)(2,1)}, bf16[8,2720]{1,0:T(8,128)(2,1)S(1)}, bf16[8,2720]{1,0:T(8,128)(2,1)S(1)}, bf16[128,5,128]{2,1,0:T(8,128)(2,1)}) custom-call(f32[2,20]{1,0:T(2,128)S(1)} %copy-done.2, f32[128,5,128]{2,1,0:T(8,128)} %copy-done.6, bf16[2,8,2,64,512]{4,3,2,1,0:T(8,128)(2,1)} %constant.23.clone.icols_all, ...), custom_call_target="tpu_custom_call" | custom-call | flops 1000000000 | bytes 4000000 | tf_op jit(solution)/shard_map/middle/pallas_call | solution.py:469
  63.6 0.7 collective-permute-start.4
  64.3 3.5 %collective-permute-start.5 = (bf16[8,2720]{1,0:T(8,128)(2,1)S(1)}, bf16[8,2720]{1,0:T(8,128)(2,1)S(1)}, u32[]{:S(2)}, u32[]{:S(2)}) collective-permute-start(bf16[8,2720]{1,0:T(8,128)(2,1)S(1)} %get-tuple-element.31), channel_id=1, source_target_pairs={{0,7},{1,0},{2,1},{3,2},{4,3},{5,4},{6,5},{7,6},{8,15},{9,8},{10,9... | collective-permute-start | bytes 130568 | tf_op jit(solution)/shard_map/ppermute | solution.py:496
  67.8 4.8 %all-to-all-start.2 = ((bf16[128,5,128]{2,1,0:T(8,128)(2,1)}), bf16[128,5,128]{2,1,0:T(8,128)(2,1)S(1)}, u32[]{:S(2)}, u32[]{:S(2)}) async-start(bf16[128,5,128]{2,1,0:T(8,128)(2,1)} %get-tuple-element.28), calls=%async_computation.2 | async-start | bytes 524288 | tf_op jit(solution)/shard_map/all_to_all | solution.py:486
  72.6 0.0 collective-permute-done.4.refs_1_
  72.6 0.0 collective-permute-done.5.refs_2_
  72.7 0.0 copy-done.3
  72.7 9.3 %conv.3 = (f32[2560,256]{1,0:T(8,128)}, f32[8,128]{1,0:T(8,128)S(1)}) custom-call(f32[2,3]{1,0:T(2,128)S(1)} %copy-done.1, bf16[2720,256]{1,0:T(8,128)(2,1)} %get-tuple-element.29.refs_0_, bf16[8,2720]{1,0:T(8,128)(2,1)S(1)} %collective-permute-done.4.refs_1_, bf16[8,2720]{1,0:T(8,128)(2,1)S(1)} %collective-permute-done.5.refs_2_, ...), custom_call_target="tpu_custom_call" | custom-call | flops 20000000000 | bytes 4000000 | tf_op jit(solution)/shard_map/conv/pallas_call | solution.py:469
  81.9 1.1 %all-to-all-done.2.received_ref = bf16[128,5,128]{2,1,0:T(8,128)(2,1)S(1)} async-done(((bf16[128,5,128]{2,1,0:T(8,128)(2,1)}), bf16[128,5,128]{2,1,0:T(8,128)(2,1)S(1)}, u32[]{:S(2)}, u32[]{:S(2)}) %all-to-all-start.2) | async-done | bytes 163872 | tf_op jit(solution)/shard_map/all_to_all | solution.py:486
  83.1 1.2 %mix.3 = (bf16[128,5,128]{2,1,0:T(8,128)(2,1)S(1)}, f32[8,128]{1,0:T(8,128)}) custom-call(f32[2,3]{1,0:T(2,128)S(1)} %copy-done.1, bf16[128,5,128]{2,1,0:T(8,128)(2,1)S(1)} %all-to-all-done.2.received_ref, f32[2,2,20,16,20]{4,3,2,1,0:T(8,128)S(1)} %bitcast.4, f32[8,128]{1,0:T(8,128)S(1)} %get-tuple-element.32.order_ref), custom_call_target="tpu_custom_call" | custom-call | flops 1000000 | bytes 4000000 | tf_op jit(solution)/shard_map/mix/pallas_call | solution.py:469
  84.3 18.9 %all_to_all.20.gathered_ref = bf16[128,5,128]{2,1,0:T(8,128)(2,1)S(1)} all-to-all(bf16[128,5,128]{2,1,0:T(8,128)(2,1)S(1)} %get-tuple-element.33), channel_id=1, replica_groups=mesh['gx'=16,'gy'=8] {'gx','gy'}, dimensions={0} | all-to-all | bytes 327680 | tf_op jit(solution)/shard_map/all_to_all | solution.py:486
  103.2 5.2 %last.1 = bf16[20,128,256]{2,1,0:T(8,128)(2,1)} custom-call(f32[2,20]{1,0:T(2,128)S(1)} %copy-done.2, bf16[128,5,128]{2,1,0:T(8,128)(2,1)S(1)} %all_to_all.20.gathered_ref, bf16[2,8,2,64,512]{4,3,2,1,0:T(8,128)(2,1)} %constant.23.clone.icols_all, bf16[2,16,2,136,128]{4,3,2,1,0:T(8,128)(2,1)} %constant.22.clone.irows_all, f32[2560,256]{1,0:T(8,128)} %get-tuple-element.34.conv_all), custom_call_target="tpu_custom_call" | custom-call | flops 1000000000 | bytes 4000000 | tf_op jit(solution)/shard_map/last/pallas_call | solution.py:469
  (2 shorter events, 0.0 us)
Async XLA Ops:
  4.7 29.4 %all-to-all-start = ((f32[128,5,128]{2,1,0:T(8,128)}), f32[128,5,128]{2,1,0:T(8,128)S(1)}, u32[]{:S(2)}, u32[]{:S(2)}) async-start(f32[128,5,128]{2,1,0:T(8,128)} %get-tuple-element.20), calls=%async_computation | async-start | bytes 1048576 | tf_op jit(solution)/shard_map/all_to_all | solution.py:486
  15.9 18.2 %copy-start.8 = (bf16[2,20,180]{2,0,1:T(2,128)(2,1)S(1)}, bf16[2,20,180]{2,0,1:T(2,128)(2,1)}, u32[]{:S(2)}) copy-start(bf16[2,20,180]{2,0,1:T(2,128)(2,1)} %param.20) | copy-start | bytes 43204
  15.9 18.2 %copy-start.7 = (bf16[2,20,500]{2,0,1:T(2,128)(2,1)S(1)}, bf16[2,20,500]{2,0,1:T(2,128)(2,1)}, u32[]{:S(2)}) copy-start(bf16[2,20,500]{2,0,1:T(2,128)(2,1)} %param.21) | copy-start | bytes 120004
  15.9 18.3 %copy-start = (f32[2,2,20,20,16]{3,4,2,1,0:T(8,128)S(1)}, f32[2,2,20,20,16]{3,4,2,1,0:T(8,128)}, u32[]{:S(2)}) copy-start(f32[2,2,20,20,16]{3,4,2,1,0:T(8,128)} %param.19) | copy-start | bytes 307204
  15.9 18.3 %copy-start.1 = (f32[2,3]{1,0:T(2,128)S(1)}, f32[2,3]{1,0:T(2,128)}, u32[]{:S(2)}) copy-start(f32[2,3]{1,0:T(2,128)} %logits_ref.7) | copy-start | bytes 76
  17.0 7.1 %collective-permute-start.1 = (bf16[20,8,256]{2,1,0:T(8,128)(2,1)S(1)}, bf16[20,8,256]{2,1,0:T(8,128)(2,1)S(1)}, u32[]{:S(2)}, u32[]{:S(2)}) collective-permute-start(bf16[20,8,256]{2,1,0:T(8,128)(2,1)S(1)} %get-tuple-element.35), channel_id=1, source_target_pairs={{0,120},{8,0},{16,8},{24,16},{32,24},{40,32},{48,40},{56,48},{64,5... | collective-permute-start | bytes 245768 | tf_op jit(solution)/shard_map/ppermute | solution.py:503
  22.0 7.7 %collective-permute-start = (bf16[20,8,256]{2,1,0:T(8,128)(2,1)S(1)}, bf16[20,8,256]{2,1,0:T(8,128)(2,1)S(1)}, u32[]{:S(2)}, u32[]{:S(2)}) collective-permute-start(bf16[20,8,256]{2,1,0:T(8,128)(2,1)S(1)} %get-tuple-element.36), channel_id=1, source_target_pairs={{0,8},{8,16},{16,24},{24,32},{32,40},{40,48},{48,56},{56,64},{64,7... | collective-permute-start | bytes 245768 | tf_op jit(solution)/shard_map/ppermute | solution.py:502
  29.9 10.7 %copy-start.4 = (s32[8,1600]{1,0:T(8,128)S(1)}, s32[8,1600]{1,0:T(8,128)}, u32[]{:S(2)}) copy-start(s32[8,1600]{1,0:T(8,128)} %constant.27.clone.refs_10_.refs_8_) | copy-start | bytes 153604
  29.9 10.7 %copy-start.5 = (s32[8,960]{1,0:T(8,128)S(1)}, s32[8,960]{1,0:T(8,128)}, u32[]{:S(2)}) copy-start(s32[8,960]{1,0:T(8,128)} %constant.26.clone.refs_9_.refs_7_) | copy-start | bytes 92164
  29.9 10.7 %collective-permute-start.2 = (bf16[8,2880]{1,0:T(8,128)(2,1)S(1)}, bf16[8,2880]{1,0:T(8,128)(2,1)S(1)}, u32[]{:S(2)}, u32[]{:S(2)}) collective-permute-start(bf16[8,2880]{1,0:T(8,128)(2,1)S(1)} %get-tuple-element.24), channel_id=1, source_target_pairs={{0,1},{1,2},{2,3},{3,4},{4,5},{5,6},{6,7},{7,0},{8,9},{9,10},{10,1... | collective-permute-start | bytes 138248 | tf_op jit(solution)/shard_map/ppermute | solution.py:495
  31.3 9.3 %collective-permute-start.3 = (bf16[8,2880]{1,0:T(8,128)(2,1)S(1)}, bf16[8,2880]{1,0:T(8,128)(2,1)S(1)}, u32[]{:S(2)}, u32[]{:S(2)}) collective-permute-start(bf16[8,2880]{1,0:T(8,128)(2,1)S(1)} %get-tuple-element.25), channel_id=1, source_target_pairs={{0,7},{1,0},{2,1},{3,2},{4,3},{5,4},{6,5},{7,6},{8,15},{9,8},{10,9... | collective-permute-start | bytes 138248 | tf_op jit(solution)/shard_map/ppermute | solution.py:496
  35.7 17.9 %all-to-all-start.1 = ((f32[128,5,128]{2,1,0:T(8,128)}), f32[128,5,128]{2,1,0:T(8,128)S(1)}, u32[]{:S(2)}, u32[]{:S(2)}) async-start(f32[128,5,128]{2,1,0:T(8,128)} %get-tuple-element.21), calls=%async_computation.1 | async-start | bytes 1048576 | tf_op jit(solution)/shard_map/all_to_all | solution.py:486
  40.6 13.8 %copy-start.2 = (f32[2,20]{1,0:T(2,128)S(1)}, f32[2,20]{1,0:T(2,128)}, u32[]{:S(2)}) copy-start(f32[2,20]{1,0:T(2,128)} %bias_ref.3) | copy-start | bytes 484
  53.6 0.8 copy-start.6
  54.4 18.2 %copy-start.3 = (bf16[60,960]{1,0:T(8,128)(2,1)S(1)}, bf16[60,960]{1,0:T(8,128)(2,1)}, u32[]{:S(2)}) copy-start(bf16[60,960]{1,0:T(8,128)(2,1)} %constant.28.clone.refs_5_) | copy-start | bytes 345604
  63.6 9.0 %collective-permute-start.4 = (bf16[8,2720]{1,0:T(8,128)(2,1)S(1)}, bf16[8,2720]{1,0:T(8,128)(2,1)S(1)}, u32[]{:S(2)}, u32[]{:S(2)}) collective-permute-start(bf16[8,2720]{1,0:T(8,128)(2,1)S(1)} %get-tuple-element.30), channel_id=1, source_target_pairs={{0,1},{1,2},{2,3},{3,4},{4,5},{5,6},{6,7},{7,0},{8,9},{9,10},{10,1... | collective-permute-start | bytes 130568 | tf_op jit(solution)/shard_map/ppermute | solution.py:495
  64.3 8.3 %collective-permute-start.5 = (bf16[8,2720]{1,0:T(8,128)(2,1)S(1)}, bf16[8,2720]{1,0:T(8,128)(2,1)S(1)}, u32[]{:S(2)}, u32[]{:S(2)}) collective-permute-start(bf16[8,2720]{1,0:T(8,128)(2,1)S(1)} %get-tuple-element.31), channel_id=1, source_target_pairs={{0,7},{1,0},{2,1},{3,2},{4,3},{5,4},{6,5},{7,6},{8,15},{9,8},{10,9... | collective-permute-start | bytes 130568 | tf_op jit(solution)/shard_map/ppermute | solution.py:496
  67.8 15.3 %all-to-all-start.2 = ((bf16[128,5,128]{2,1,0:T(8,128)(2,1)}), bf16[128,5,128]{2,1,0:T(8,128)(2,1)S(1)}, u32[]{:S(2)}, u32[]{:S(2)}) async-start(bf16[128,5,128]{2,1,0:T(8,128)(2,1)} %get-tuple-element.28), calls=%async_computation.2 | async-start | bytes 524288 | tf_op jit(solution)/shard_map/all_to_all | solution.py:486

commit v3 on v2

--- a/solution.py
+++ b/solution.py
@@ -23,7 +23,8 @@
 f32 = jnp.float32
 bf16 = jnp.bfloat16
 both = ("gx", "gy")
-WIRES = (jnp.float32, jnp.bfloat16)
+SUMS = (jnp.float32, jnp.bfloat16)
+MIXED = (jnp.bfloat16, jnp.bfloat16)
 
 
 def wave(numbers, positions, length):
@@ -90,14 +91,10 @@
     return out
 
 
-def spread(taps, slots_first):
+def spread(taps):
     width = 2 * taps * BLOCK
     lanes = np.arange(width) % (taps * BLOCK) // 8
-    step, channel = lanes // C, lanes % C
-    if slots_first:
-        channel = channel % GROUPS * 4 + channel // GROUPS
-    columns = step * C + channel
-    return (np.arange(taps * C)[:, None] == columns[None, :]).astype(ml_dtypes.bfloat16)
+    return (np.arange(taps * C)[:, None] == lanes[None, :]).astype(ml_dtypes.bfloat16)
 
 
 def offsets(taps):
@@ -127,17 +124,22 @@
     lane = lax.broadcasted_iota(jnp.int32, (COLS, 256), 1)
     slot = (lane >> 5) & 3
     zero = jnp.zeros((), bf16)
-    placed = [[jnp.where(slot == i, cols_ref[t], zero) for i in range(4)] for t in range(2)]
     rows_high, rows_low = rows_ref[0], rows_ref[1]
+    members = jnp.concatenate(
+        [
+            jnp.concatenate([planes(4 * group + i) for group in range(GROUPS)], axis=0)
+            for i in range(4)
+        ],
+        axis=1,
+    )
+    sums = []
+    for t in range(2):
+        placed = [jnp.where(slot == i, cols_ref[t], zero) for i in range(4)]
+        sums.append(mul(members, jnp.concatenate(placed, axis=0)))
+    count = members.shape[0] // GROUPS
     for group in range(GROUPS):
-        members = [planes(4 * group + i) for i in range(4)]
-        sums = []
-        for t in range(2):
-            total = mul(members[0], placed[t][0])
-            for i in range(1, 4):
-                total = total + mul(members[i], placed[t][i])
-            sums.append(total)
-        high, low = split(jnp.concatenate(sums, axis=0))
+        own = [total[group * count : group * count + count] for total in sums]
+        high, low = split(jnp.concatenate(own, axis=0))
         modes = mul(rows_high, high) + mul(rows_high, low) + mul(rows_low, high)
         for half in range(2):
             write(half, group, modes[:, 128 * half : 128 * half + 128])
@@ -148,7 +150,8 @@
 
 
 def forward_kernel(
-    grid_all, cols_all, rows_all, out_ref, first_ref, last_ref, grid_buffer, cols, rows, sems
+    grid_all, cols_all, rows_all, out_ref, upper_ref, lower_ref, grid_buffer, chunk, cols, rows,
+    sems,
 ):
     gx, gy = indices()
     start = pl.multiple_of(gy * COLS, COLS)
@@ -161,20 +164,19 @@
             (grid_all.at[pl.ds(4 * g, 4)], grid_buffer.at[pl.ds(4 * g, 4)], sems.at[2 + g])
             for g in range(GROUPS)
         ]
-    )
-    copies[0].wait()
-    copies[1].wait()
-
-    def plane(c):
-        if c % 4 == 0:
-            copies[2 + c // 4].wait()
-        return grid_buffer[c]
+        + [
+            (grid_all.at[:, pl.ds(0, 8)], upper_ref, sems.at[2 + GROUPS]),
+            (grid_all.at[:, pl.ds(ROWS - 8, 8)], lower_ref, sems.at[3 + GROUPS]),
+        ]
+    )
+    for copy in copies:
+        copy.wait()
 
     def write(half, group, value):
-        out_ref[pl.ds(half, 64, stride=2), group, :] = value
-
-    transform(plane, cols, rows, write)
-    edges(grid_buffer[...].reshape(C * ROWS, COLS), first_ref, last_ref)
+        chunk[pl.ds(half, 64, stride=2), group, :] = value
+
+    transform(lambda c: grid_buffer[c], cols, rows, write)
+    out_ref[...] = chunk[...].astype(out_ref.dtype)
 
 
 def mixture_of(logits_ref, layer):
@@ -233,14 +235,6 @@
     first_ref[...], last_ref[...] = edge_columns(rows)
 
 
-def edges_kernel(top_ref, bottom_ref, first_ref, last_ref, first_out, last_out):
-    rows = [r[...].reshape(BLOCK, COLS) for r in (top_ref, bottom_ref)]
-    found = edge_columns(jnp.concatenate(rows, axis=0))
-    for own_ref, extra, out_ref in zip((first_ref, last_ref), found, (first_out, last_out)):
-        out_ref[:, : C * ROWS] = own_ref[...]
-        out_ref[:, C * ROWS :] = extra
-
-
 def banded(weights, spread_ref, offsets_ref, steps, width):
     offset = offsets_ref[...][None]
     total = jnp.zeros((C, 8, width), f32)
@@ -253,67 +247,83 @@
 
 NEAR = (-1, 0, 1)
 FAR = (-4, -2, 0, 2, 4)
-
-
-def conv_kernel(logits_ref, *refs, layer, count):
-    sources, refs = (refs[:3], refs[3:]) if layer == 0 else (refs[:1], refs[1:])
-    left_ref, right_ref, near_ref, far_ref, refs = *refs[:4], refs[4:]
-    near_spread, far_spread, near_offsets, far_offsets, order_ref, out_all, marker_ref, *refs = refs
-    field, out_ref, near_band, far_band, near_stack, far_stack, *refs = refs
-    sems, out_sems, *refs = refs
+ENDS_LAST = (7, 15, 19)
+ENDS = {17: (8, 14, 17), 8: (5, 8)}
+
+
+def own_kernel(
+    grid_all, near_ref, far_ref, near_spread, far_spread, near_offsets, far_offsets, order_ref,
+    field_all, first_ref, last_ref, near_band, far_band, grid_ref, field, sems, out_sem,
+):
+    pieces = [pl.ds(4 * g, 4) for g in range(GROUPS)]
+    copies = fetch([(grid_all.at[p], grid_ref.at[p], sems.at[g]) for g, p in enumerate(pieces)])
+    near_band[...] = banded(near_ref[0], near_spread, near_offsets, NEAR, 6 * BLOCK)
+    far_band[...] = banded(far_ref[0], far_spread, far_offsets, FAR, 10 * BLOCK)
+    for copy in copies:
+        copy.wait()
+    for pair in range(C // 2):
+        inner = [grid_ref[2 * pair + i].astype(f32) for i in range(2)]
+        for block in range(16):
+            value = [v[8 * block : 8 * block + 8] for v in inner]
+            place = block * BLOCK + 16 * pair
+            field[place : place + 16, :] = jnp.concatenate(value, axis=0).astype(bf16)
+    (result,) = fetch([(field, field_all, out_sem)])
+    edges(field[...], first_ref, last_ref)
+    result.wait()
+
+
+def edges_kernel(top_ref, bottom_ref, first_ref, last_ref, first_out, last_out):
+    found = edge_columns(jnp.concatenate([top_ref[...], bottom_ref[...]], axis=0))
+    for own_ref, extra, out_ref in zip((first_ref, last_ref), found, (first_out, last_out)):
+        out_ref[:, : C * ROWS] = own_ref[...]
+        out_ref[:, C * ROWS :] = extra
+
+
+def conv_kernel(logits_ref, *refs, layer, first, count):
     if layer == 0:
-        grid_all, top_ref, bottom_ref = sources
-        (grid_ref,) = refs
+        main_all, top_all, bottom_all, left_ref, right_ref, near_all, far_all, *refs = refs
+        order_ref, out_all, marker_ref, *refs = refs
+    else:
+        field_all, left_ref, right_ref, near_ref, far_ref, near_spread, far_spread, *refs = refs
+        near_offsets, far_offsets, order_ref, out_all, marker_ref, *refs = refs
+    field, out_ref, near_band, far_band, near_stack, far_stack, sems, out_sems = refs
+    if layer == 0:
         copies = fetch(
             [
-                (grid_all.at[pl.ds(4 * g, 4)], grid_ref.at[pl.ds(4 * g, 4)], sems.at[g])
-                for g in range(GROUPS)
+                (top_all, field.at[pl.ds(0, BLOCK)], sems.at[0]),
+                (main_all, field.at[pl.ds(BLOCK, 16 * BLOCK)], sems.at[1]),
+                (bottom_all, field.at[pl.ds(17 * BLOCK, BLOCK)], sems.at[2]),
+                (near_all, near_band, sems.at[3]),
+                (far_all, far_band, sems.at[4]),
             ]
         )
     else:
-        (field_all,) = sources
-        pieces = [pl.ds(i * BLOCK, min(3, count + 1 - i) * BLOCK) for i in range(0, count + 1, 3)]
-        copies = fetch(
-            [(field_all.at[p], field.at[p], sems.at[k]) for k, p in enumerate(pieces)]
-        )
-    near_band[...] = banded(near_ref[layer], near_spread, near_offsets, NEAR, 6 * BLOCK)
-    far_band[...] = banded(far_ref[layer], far_spread, far_offsets, FAR, 10 * BLOCK)
+        piece = pl.ds(first * BLOCK, (count + 1) * BLOCK)
+        copies = fetch([(field_all.at[piece], field, sems.at[0])])
+        near_band[...] = banded(near_ref[layer], near_spread, near_offsets, NEAR, 6 * BLOCK)
+        far_band[...] = banded(far_ref[layer], far_spread, far_offsets, FAR, 10 * BLOCK)
     lane = lax.broadcasted_iota(jnp.int32, (16, 128), 1)
     row = lax.broadcasted_iota(jnp.int32, (16, 128), 0)
     sides_place = jnp.where(lane == jnp.where(row < 8, row, row + 112), 1.0, 0.0).astype(bf16)
-    sides = jnp.concatenate([right_ref[...].astype(f32), left_ref[...].astype(f32)], axis=0)
+    lanes = slice(first * BLOCK, (first + count + 1) * BLOCK)
+    sides = [r[:, lanes].astype(f32) for r in (right_ref, left_ref)]
+    sides = jnp.concatenate(sides, axis=0)
     side = lax.dot_general(
         sides.astype(bf16), sides_place, (((0,), (0,)), ((), ())), preferred_element_type=f32
     )
-    if layer == 0:
-        for pair in range(C // 2):
-            if pair % 2 == 0:
-                copies[pair // 2].wait()
-            inner = [grid_ref[2 * pair + i].astype(f32) for i in range(2)]
-            upper = [top_ref[2 * pair + i].astype(f32) for i in range(2)]
-            lower = [bottom_ref[2 * pair + i].astype(f32) for i in range(2)]
-            for block in range(18):
-                if block == 0:
-                    value = upper
-                elif block == 17:
-                    value = lower
-                else:
-                    value = [v[8 * block - 8 : 8 * block] for v in inner]
-                place = block * BLOCK + 16 * pair
-                field[place : place + 16, :] = jnp.concatenate(value, axis=0).astype(bf16)
+    side = side.astype(bf16)
+    for copy in copies:
+        copy.wait()
 
     def side_of(block):
-        if layer == 1 or block in (0, 17):
-            start = block * BLOCK if layer == 1 else C * ROWS + (block > 0) * BLOCK
-            return side[start : start + BLOCK].astype(bf16)
-        starts = [c * ROWS + 8 * block - 8 for c in range(C)]
-        return jnp.concatenate([side[p : p + 8] for p in starts], axis=0).astype(bf16)
+        start = block * BLOCK
+        if layer == 0:
+            start = {0: 16 * BLOCK, 17: 17 * BLOCK}.get(block, start - BLOCK)
+        return side[start : start + BLOCK]
 
     _, near_scale, far_scale = mixture_of(logits_ref, layer)
     results = []
     for index in range(count + 1):
-        if layer == 1 and index % 3 == 0:
-            copies[index // 3].wait()
         rows = slice(index * BLOCK, index * BLOCK + BLOCK)
         block = jnp.concatenate([field[rows, :], side_of(index)], axis=1)
         moved = {0: block}
@@ -331,9 +341,13 @@
         total = near_scale * mul(near_band[...], near_rows) + far_scale * mul(
             far_band[...], far_rows
         )
-        out_ref[done * BLOCK : done * BLOCK + BLOCK, :] = total
-        piece = pl.ds(done * BLOCK, BLOCK)
-        results += fetch([(out_ref.at[piece], out_all.at[piece], out_sems.at[done])])
+        out_ref[:, 8 * done : 8 * done + 8, :] = total.reshape(C, 8, COLS)
+        if done + 1 in ENDS[count]:
+            start = max((e for e in ENDS[count] if e < done + 1), default=0)
+            piece = pl.ds(8 * start, 8 * (done + 1 - start))
+            results += fetch(
+                [(out_ref.at[:, piece], out_all.at[:, piece], out_sems.at[len(results)])]
+            )
     marker_ref[...] = total[:8, :128]
     for copy in results:
         copy.wait()
@@ -343,7 +357,7 @@
     return 0.5 * value * (1.0 + lax.erf(value * math.sqrt(0.5)))
 
 
-def expand(bias_ref, gathered, cols, rows, conv_ref, conv_copy, layer, blocks, emit):
+def expand(bias_ref, gathered, cols, rows, lines, conv_ref, arrive, layer, emit):
     parts = []
     for group in range(GROUPS):
         pair = [gathered[pl.ds(half, 64, stride=2), group, :] for half in range(2)]
@@ -363,28 +377,23 @@
                 pieces += [own if i == slot else empty for i in range(4)]
             placed.append(jnp.concatenate(pieces, axis=0))
         first = mul(stacked, placed[0])
-        lines = first[:320] + first[320:] + mul(high, placed[1])
-        if slot == 0:
-            conv_copy.wait()
-        for group in range(GROUPS):
-            channel = 4 * group + slot
-            here = lines[64 * group : 64 * group + 64]
-            line_high, line_low = split(jnp.concatenate([here[:, :COLS], here[:, COLS:]], axis=0))
-            value = mul(rows_twice, jnp.concatenate([line_high, line_low], axis=0)) + mul(
-                rows_low, line_high
-            )
-            local = []
-            for block in range(blocks):
-                place = block * BLOCK + 8 * channel
-                local.append(conv_ref[place : place + 8, :])
-            value = value + jnp.concatenate(local, axis=0) + bias_ref[layer, channel]
-            emit(slot * GROUPS + group, channel, gelu(value))
+        lines[slot] = first[:320] + first[320:] + mul(high, placed[1])
+    arrive()
+    for channel in range(C):
+        group, slot = channel // 4, channel % 4
+        here = lines[slot, 64 * group : 64 * group + 64]
+        line_high, line_low = split(jnp.concatenate([here[:, :COLS], here[:, COLS:]], axis=0))
+        value = mul(rows_twice, jnp.concatenate([line_high, line_low], axis=0)) + mul(
+            rows_low, line_high
+        )
+        emit(channel, gelu(value + conv_ref[channel] + bias_ref[layer, channel]))
 
 
 def middle_kernel(
     bias_ref, gathered_ref, icols_all, irows_all, fcols_all, frows_all, conv_all,
     field_all, first_ref, last_ref, out_ref,
-    planes, chunk, icols, irows, fcols, frows, conv_ref, field_ref, sems,
+    planes, chunk, icols, irows, fcols, frows, conv_ref, field_ref, lines, sems, conv_sem,
+    field_sems,
 ):
     gx, gy = indices()
     start = pl.multiple_of(gy * COLS, COLS)
@@ -393,51 +402,62 @@
             (icols_all.at[0, gy], icols, sems.at[0]),
             (irows_all.at[1, gx], irows, sems.at[1]),
             (fcols_all.at[:, pl.ds(start, COLS), :], fcols, sems.at[2]),
-            (conv_all, conv_ref, sems.at[4]),
             (frows_all.at[1, gx], frows, sems.at[3]),
         ]
     )
+    (arrival,) = fetch([(conv_all, conv_ref, conv_sem)])
+    chunk[...] = gathered_ref[...].astype(f32)
     copies[0].wait()
     copies[1].wait()
     waiting = []
-
-    def emit(order, channel, value):
+    results = []
+
+    def emit(channel, value):
         rounded = value.astype(bf16)
         planes[channel, :136] = rounded
         planes[channel, 136:] = jnp.zeros((8, COLS), bf16)
         waiting.append(rounded.astype(f32))
-        if order % 2 == 1:
+        if channel % 2 == 1:
             for block in range(17):
                 rows = slice(8 * block, 8 * block + 8)
                 both_rows = jnp.concatenate([waiting[0][rows], waiting[1][rows]], axis=0)
-                place = block * BLOCK + 8 * (order - 1)
-                field_ref[place : place + 16, :] = both_rows.astype(bf16)
+                place = 8 * (channel - 1)
+                field_ref[block, place : place + 16, :] = both_rows.astype(bf16)
             waiting.clear()
-
-    expand(bias_ref, gathered_ref, icols, irows, conv_ref, copies[3], 0, 17, emit)
-    (result,) = fetch([(field_ref, field_all, sems.at[5])])
-    edges(field_ref[...], first_ref, last_ref)
+        if channel in (9, 19):
+            piece = pl.ds(8 * (channel - 9), 80)
+            sem = field_sems.at[len(results)]
+            results.extend(fetch([(field_ref.at[:, piece], field_all.at[:, piece], sem)]))
+
+    expand(bias_ref, chunk, icols, irows, lines, conv_ref, arrival.wait, 0, emit)
+    edges(field_ref[...].reshape(17 * BLOCK, COLS), first_ref, last_ref)
     copies[2].wait()
-    copies[4].wait()
+    copies[3].wait()
 
     def write(half, group, value):
         chunk[pl.ds(half, 64, stride=2), group, :] = value
 
     transform(lambda c: planes[c], fcols, frows, write)
     out_ref[...] = chunk[...].astype(out_ref.dtype)
-    result.wait()
+    for copy in results:
+        copy.wait()
 
 
 def last_kernel(
-    bias_ref, gathered_ref, icols_all, irows_all, conv_all, out_all,
-    wide, icols, irows, conv_ref, out_ref, sems, out_sems,
+    bias_ref, gathered_ref, icols_all, irows_all, upper_all, lower_all, out_all,
+    wide, icols, irows, conv_ref, out_ref, lines, sems, conv_sems, out_sems,
 ):
     gx, gy = indices()
     copies = fetch(
         [
             (icols_all.at[0, gy], icols, sems.at[0]),
             (irows_all.at[0, gx, :, pl.ds(0, ROWS)], irows, sems.at[1]),
-            (conv_all, conv_ref, sems.at[2]),
+        ]
+    )
+    arrivals = fetch(
+        [
+            (upper_all, conv_ref.at[:, pl.ds(0, 64)], conv_sems.at[0]),
+            (lower_all, conv_ref.at[:, pl.ds(64, 64)], conv_sems.at[1]),
         ]
     )
     wide[...] = gathered_ref[...].astype(f32)
@@ -445,11 +465,19 @@
     copies[1].wait()
     results = []
 
-    def emit(order, channel, value):
+    def emit(channel, value):
         out_ref[channel] = value.astype(bf16)
-        results.extend(fetch([(out_ref.at[channel], out_all.at[channel], out_sems.at[channel])]))
-
-    expand(bias_ref, wide, icols, irows, conv_ref, copies[2], 1, 16, emit)
+        if channel in ENDS_LAST:
+            start = max((e + 1 for e in ENDS_LAST if e < channel), default=0)
+            piece = pl.ds(start, channel + 1 - start)
+            sem = out_sems.at[len(results)]
+            results.extend(fetch([(out_ref.at[piece], out_all.at[piece], sem)]))
+
+    def arrive():
+        for copy in arrivals:
+            copy.wait()
+
+    expand(bias_ref, wide, icols, irows, lines, conv_ref, arrive, 1, emit)
     for copy in results:
         copy.wait()
 
@@ -499,8 +527,6 @@
 
 def on_device(grid_field, spectral_weight, conv_near, conv_far, mix_logits, channel_bias):
     grid = grid_field[0]
-    top = lax.ppermute(grid[:, ROWS - 8 :], "gx", ring("gx", 1))
-    bottom = lax.ppermute(grid[:, :8], "gx", ring("gx", -1))
     mode_weights = jnp.swapaxes(spectral_weight, 3, 4)
 
     fcols = jnp.asarray(forward_cols())
@@ -513,21 +539,38 @@
     icols = np.stack([inverse_cols()] * 2)
     frows, irows, icols = jnp.asarray(frows), jnp.asarray(irows), jnp.asarray(icols)
 
-    chunks = [shape_of((128, GROUPS, 128), kind) for kind in WIRES]
+    chunks = [shape_of((128, GROUPS, 128), kind) for kind in SUMS]
+    answers = [shape_of((128, GROUPS, 128), kind) for kind in MIXED]
     dma = pltpu.SemaphoreType.DMA
     icols_buffer = pltpu.VMEM((2, 64, 2 * COLS), bf16)
     fcols_buffer = pltpu.VMEM((2, COLS, 256), bf16)
 
-    partial, first, last = call(
-        forward_kernel, [chunks[0]] + [shape_of((8, C * ROWS), bf16)] * 2, (grid, fcols, frows),
+    partial, upper, lower = call(
+        forward_kernel, [chunks[0]] + [shape_of((C, 8, COLS), bf16)] * 2, (grid, fcols, frows),
         [hbm] * 3,
         (
-            pltpu.VMEM((C, ROWS, COLS), bf16), fcols_buffer, pltpu.VMEM((2, 64, 2 * ROWS), bf16),
-            dma((2 + GROUPS,)),
+            pltpu.VMEM((C, ROWS, COLS), bf16), pltpu.VMEM((128, GROUPS, 128), f32), fcols_buffer,
+            pltpu.VMEM((2, 64, 2 * ROWS), bf16),
+            dma((4 + GROUPS,)),
         ),
         name="forward",
     )
+    top = lax.ppermute(lower, "gx", ring("gx", 1)).reshape(BLOCK, COLS)
+    bottom = lax.ppermute(upper, "gx", ring("gx", -1)).reshape(BLOCK, COLS)
     received = exchange(partial)
+    tables = [jnp.asarray(t) for t in (spread(3), spread(5), offsets(3), offsets(5))]
+    near_shape, far_shape = (BLOCK, 6 * BLOCK), (BLOCK, 10 * BLOCK)
+    field, first, last, near_band, far_band = call(
+        own_kernel,
+        [shape_of((16 * BLOCK, COLS), bf16)] + [shape_of((8, 16 * BLOCK), bf16)] * 2
+        + [shape_of(near_shape, bf16), shape_of(far_shape, bf16)],
+        (grid, conv_near, conv_far, *tables, upper), [hbm] + [vmem] * 6 + [anywhere],
+        (
+            pltpu.VMEM((C, ROWS, COLS), bf16), pltpu.VMEM((16 * BLOCK, COLS), bf16),
+            dma((GROUPS,)), dma,
+        ),
+        out_specs=[hbm] + [vmem] * 4, name="own",
+    )
     first, last = call(
         edges_kernel, [shape_of((8, 18 * BLOCK), bf16)] * 2, (top, bottom, first, last),
         [vmem] * 4, limit=SMALL, name="edges",
@@ -535,61 +578,63 @@
 
     def mix(layer, received, order):
         return call(
-            functools.partial(mix_kernel, layer=layer), [chunks[layer], shape_of((8, 128), f32)],
+            functools.partial(mix_kernel, layer=layer), [answers[layer], shape_of((8, 128), f32)],
             (mix_logits, received, mode_weights, order), [vmem, vmem, hbm, anywhere],
             (pltpu.VMEM((2, C, 16, C), f32), dma), flops=10**6, limit=SMALL, name="mix",
         )
 
-    def conv(layer, sources, specs, sides, count, order):
-        tables = (spread(3, layer), spread(5, layer), offsets(3), offsets(5))
+    def conv(layer, sources, specs, first, count, order):
         return call(
-            functools.partial(conv_kernel, layer=layer, count=count),
-            [shape_of((count * BLOCK, COLS), f32), shape_of((8, 128), f32)],
-            (mix_logits, *sources, *sides, conv_near, conv_far, *map(jnp.asarray, tables), order),
-            [vmem] + specs + [vmem] * 8 + [anywhere],
-            [
+            functools.partial(conv_kernel, layer=layer, first=first, count=count),
+            [shape_of((C, 8 * count, COLS), f32), shape_of((8, 128), f32)],
+            (mix_logits, *sources, order), [vmem] + specs + [anywhere],
+            (
                 pltpu.VMEM(((count + 1) * BLOCK, COLS), bf16),
-                pltpu.VMEM((count * BLOCK, COLS), f32),
-                pltpu.VMEM((BLOCK, 6 * BLOCK), bf16),
-                pltpu.VMEM((BLOCK, 10 * BLOCK), bf16),
+                pltpu.VMEM((C, 8 * count, COLS), f32),
+                pltpu.VMEM(near_shape, bf16),
+                pltpu.VMEM(far_shape, bf16),
                 pltpu.VMEM(((count + 1) * 3 * BLOCK, COLS), bf16),
                 pltpu.VMEM(((count + 1) * 5 * BLOCK, COLS), bf16),
-                dma((6,)), dma((count,)),
-            ]
-            + [pltpu.VMEM((C, ROWS, COLS), bf16)] * (1 - layer),
+                dma((5,)), dma((3,)),
+            ),
             out_specs=[hbm, vmem], flops=2 * 10**10, name="conv",
         )
 
     around = sides(first, last)
     mixed, marker = mix(0, received, mix_logits)
     gathered = exchange(mixed)
-    local, _ = conv(0, (grid, top, bottom), [hbm, vmem, vmem], around, 17, marker)
+    specs = [hbm] * 3 + [vmem] * 2 + [hbm] * 2
+    local, _ = conv(0, (field, top, bottom, *around, near_band, far_band), specs, 0, 17, marker)
     field, first, last, partial = call(
         middle_kernel,
-        [shape_of((17 * BLOCK, COLS), bf16)] + [shape_of((8, 17 * BLOCK), bf16)] * 2 + [chunks[1]],
+        [shape_of((17, BLOCK, COLS), bf16)] + [shape_of((8, 17 * BLOCK), bf16)] * 2 + [chunks[1]],
         (channel_bias, gathered, icols, irows, fcols, frows, local),
         [smem, vmem] + [hbm] * 5,
         (
             pltpu.VMEM((C, 144, COLS), bf16), pltpu.VMEM((128, GROUPS, 128), f32),
             icols_buffer, pltpu.VMEM((2, 136, 128), bf16),
             fcols_buffer, pltpu.VMEM((2, 64, 288), bf16),
-            pltpu.VMEM((17 * BLOCK, COLS), f32), pltpu.VMEM((17 * BLOCK, COLS), bf16), dma((6,)),
+            pltpu.VMEM((C, 136, COLS), f32), pltpu.VMEM((17, BLOCK, COLS), bf16),
+            pltpu.VMEM((4, 320, 2 * COLS), f32), dma((4,)), dma, dma((2,)),
         ),
         out_specs=[hbm, vmem, vmem, vmem],
         name="middle",
     )
     received = exchange(partial)
-    local, marker = conv(1, (field,), [hbm], sides(first, last), 16, mix_logits)
-    mixed, _ = mix(1, received, marker)
+    field, around = field.reshape(17 * BLOCK, COLS), sides(first, last)
+    sources, specs = (field, *around, conv_near, conv_far, *tables), [hbm] + [vmem] * 8
+    upper, marker = conv(1, sources, specs, 0, 8, mix_logits)
+    mixed, marker = mix(1, received, marker)
     gathered = exchange(mixed)
+    lower, _ = conv(1, sources, specs, 8, 8, marker)
     result = call(
         last_kernel, shape_of((C, ROWS, COLS), bf16),
-        (channel_bias, gathered, icols, irows, local),
-        [smem, vmem] + [hbm] * 3,
+        (channel_bias, gathered, icols, irows, upper, lower),
+        [smem, vmem] + [hbm] * 4,
         (
             pltpu.VMEM((128, GROUPS, 128), f32), icols_buffer, pltpu.VMEM((2, ROWS, 128), bf16),
-            pltpu.VMEM((16 * BLOCK, COLS), f32), pltpu.VMEM((C, ROWS, COLS), bf16),
-            dma((3,)), dma((C,)),
+            pltpu.VMEM((C, ROWS, COLS), f32), pltpu.VMEM((C, ROWS, COLS), bf16),
+            pltpu.VMEM((4, 320, 2 * COLS), f32), dma((2,)), dma((2,)), dma((3,)),
         ),
         out_specs=hbm,
         name="last",

time: 110 us -> 102 us (0.927)
  blocking collectives: 18.9 us -> 0 us
  starting transfers between devices: 34.3 us -> 40.8 us
  Pallas kernels: 41.1 us -> 45.3 us
  local copies, waits for them, and re-layouts: 1.86 us -> 0.75 us
    all_to_all x1 -> x0, blocking collectives: 18.9 us -> none  [exchange(): return lax.all_to_all(value, both, split_axis=0, concat_axis=0, tiled=True)]
    all_to_all x3 -> x4, waiting for transfers between devices: 4.29 us -> 10.7 us  [exchange(): return lax.all_to_all(value, both, split_axis=0, concat_axis=0, tiled=True)]
    all_to_all x3 -> x4, starting transfers between devices: 20.8 us -> 27 us  [exchange(): return lax.all_to_all(value, both, split_axis=0, concat_axis=0, tiled=True)]
    ppermute x2, waiting for transfers between devices: 7.68 us -> 2.12 us  [the longest x1 2.12 us: on_device(): top = lax.ppermute(lower, 'gx', ring('gx', 1)).reshape(BLOCK, COLS)]
    pallas_call x8 -> x10, Pallas kernels: 41.1 us -> 45.3 us  [call(): pl.pallas_call(kernel, out_shape=outs, in_specs=specs, out_specs=out_spec...]
  transfers between devices with their start and end apart: 9 -> 10, of which waited for: 4 -> 4; matrix products, arithmetic and copies ran while one was open for 1% -> 0% of each run, Pallas kernels for 19% -> 27%
where the time goes in v3:
time: 102 us; the launch traced here: 100 us
  Pallas kernels  45.3 us (44%)
  starting transfers between devices  40.8 us (40%)
  waiting for transfers between devices  12.8 us (13%)
    pallas_call x10, Pallas kernels, call(): pl.pallas_call(kernel, out_shape=outs, in_specs=specs, out_specs=out_spec...  45.3 us
    all_to_all x4, starting transfers between devices, exchange(): return lax.all_to_all(value, both, split_axis=0, concat_axis=0, tiled=True)  27 us
    all_to_all x4, waiting for transfers between devices, exchange(): return lax.all_to_all(value, both, split_axis=0, concat_axis=0, tiled=True)  10.7 us
    ppermute x2, starting transfers between devices, sides(): right = lax.ppermute(first, 'gy', ring('gy', -1))  6.22 us
    ppermute x1, starting transfers between devices, on_device(): bottom = lax.ppermute(upper, 'gx', ring('gx', -1)).reshape(BLOCK, COLS)  5.35 us
    ppermute x2, starting transfers between devices, sides(): left = lax.ppermute(last, 'gy', ring('gy', 1))  2.15 us
    ppermute x1, waiting for transfers between devices, on_device(): top = lax.ppermute(lower, 'gx', ring('gx', 1)).reshape(BLOCK, COLS)  2.12 us
  transfers between devices with their start and end apart: 10, of which 4 were waited for; matrix products, arithmetic and copies ran while one was open for 0% of the time, Pallas kernels for 27%

profile of v3, /device:TPU:0, one launch (start us, length us, event | category | flops | bytes accessed | tf_op | source)
XLA Modules:
  0.0 100.1 jit_solution(11232767814651605588)
XLA Ops:
  0.0 0.0 copy-start.8
  0.0 0.0 copy-start.7
  0.0 0.0 copy-start.3
  0.0 0.0 copy-start.4
  0.0 0.0 copy-start.5
  0.0 3.7 %forward.1 = (f32[128,5,128]{2,1,0:T(8,128)}, bf16[20,8,256]{2,1,0:T(8,128)(2,1)S(1)}, bf16[20,8,256]{2,1,0:T(8,128)(2,1)S(1)}) custom-call(bf16[20,128,256]{2,1,0:T(8,128)(2,1)} %bitcast.12, bf16[2,2048,256]{2,1,0:T(8,128)(2,1)} %constant.16.clone.cols_all.fcols_all, bf16[2,16,2,64,288]{4,3,2,1,0:T(8,128)(2,1)} %constant.17.clone.rows_all.frows_all), custom_call_target="tpu_custom_call" | custom-call | flops 1000000000 | bytes 4000000 | tf_op jit(solution)/shard_map/forward/pallas_call | solution.py:497
  3.7 11.2 %all-to-all-start = ((f32[128,5,128]{2,1,0:T(8,128)}), f32[128,5,128]{2,1,0:T(8,128)S(1)}, u32[]{:S(2)}, u32[]{:S(2)}) async-start(f32[128,5,128]{2,1,0:T(8,128)} %get-tuple-element.27), calls=%async_computation | async-start | bytes 1048576 | tf_op jit(solution)/shard_map/all_to_all | solution.py:514
  14.9 0.1 collective-permute-start
  15.0 5.3 %collective-permute-start.1 = (bf16[20,8,256]{2,1,0:T(8,128)(2,1)S(1)}, bf16[20,8,256]{2,1,0:T(8,128)(2,1)S(1)}, u32[]{:S(2)}, u32[]{:S(2)}) collective-permute-start(bf16[20,8,256]{2,1,0:T(8,128)(2,1)S(1)} %get-tuple-element.29.order_ref), channel_id=1, source_target_pairs={{0,120},{8,0},{16,8},{24,16},{32,24},{40,32},{48,40},{56,48},{64,5... | collective-permute-start | bytes 245768 | tf_op jit(solution)/shard_map/ppermute | solution.py:559
  20.3 0.0 copy-done.8
  20.4 0.0 copy-done.7
  20.4 0.0 copy-done.3
  20.4 0.0 copy-done.4
  20.4 0.0 copy-done.5
  20.4 4.9 %own.1 = (bf16[2560,256]{1,0:T(8,128)(2,1)}, bf16[8,2560]{1,0:T(8,128)(2,1)S(1)}, bf16[8,2560]{1,0:T(8,128)(2,1)S(1)}, bf16[160,960]{1,0:T(8,128)(2,1)}, bf16[160,1600]{1,0:T(8,128)(2,1)}) custom-call(bf16[20,128,256]{2,1,0:T(8,128)(2,1)} %bitcast.13, bf16[2,20,180]{2,1,0:T(8,128)(2,1)S(1)} %copy.15.near_ref.refs_3_, ...), custom_call_target="tpu_custom_call" | custom-call | flops 1000000000 | bytes 4000000 | tf_op jit(solution)/shard_map/own/pallas_call | solution.py:497
  25.3 2.1 %collective-permute-done = bf16[20,8,256]{2,1,0:T(8,128)(2,1)S(1)} collective-permute-done((bf16[20,8,256]{2,1,0:T(8,128)(2,1)S(1)}, bf16[20,8,256]{2,1,0:T(8,128)(2,1)S(1)}, u32[]{:S(2)}, u32[]{:S(2)}) %collective-permute-start) | collective-permute-done | bytes 81952 | tf_op jit(solution)/shard_map/ppermute | solution.py:558
  27.4 0.0 collective-permute-done.1
  27.4 0.0 copy-start
  27.4 0.0 copy-start.1
  27.4 0.2 edges.1
  27.6 1.6 %collective-permute-start.2 = (bf16[8,2880]{1,0:T(8,128)(2,1)S(1)}, bf16[8,2880]{1,0:T(8,128)(2,1)S(1)}, u32[]{:S(2)}, u32[]{:S(2)}) collective-permute-start(bf16[8,2880]{1,0:T(8,128)(2,1)S(1)} %get-tuple-element.34), channel_id=1, source_target_pairs={{0,1},{1,2},{2,3},{3,4},{4,5},{5,6},{6,7},{7,0},{8,9},{9,10},{10,1... | collective-permute-start | bytes 138248 | tf_op jit(solution)/shard_map/ppermute | solution.py:523
  29.2 2.6 %collective-permute-start.3 = (bf16[8,2880]{1,0:T(8,128)(2,1)S(1)}, bf16[8,2880]{1,0:T(8,128)(2,1)S(1)}, u32[]{:S(2)}, u32[]{:S(2)}) collective-permute-start(bf16[8,2880]{1,0:T(8,128)(2,1)S(1)} %get-tuple-element.35), channel_id=1, source_target_pairs={{0,7},{1,0},{2,1},{3,2},{4,3},{5,4},{6,5},{7,6},{8,15},{9,8},{10,9... | collective-permute-start | bytes 138248 | tf_op jit(solution)/shard_map/ppermute | solution.py:524
  31.8 0.0 all-to-all-done.received_ref
  31.8 0.0 copy-done
  31.8 0.0 copy-done.1
  31.8 1.5 %mix.2 = (bf16[128,5,128]{2,1,0:T(8,128)(2,1)}, f32[8,128]{1,0:T(8,128)S(1)}) custom-call(f32[2,3]{1,0:T(2,128)S(1)} %copy-done.1, f32[128,5,128]{2,1,0:T(8,128)S(1)} %all-to-all-done.received_ref, f32[2,2,20,16,20]{4,3,2,1,0:T(8,128)S(1)} %bitcast.6, f32[2,3]{1,0:T(2,128)S(1)} %copy-done.1), custom_call_target="tpu_custom_call" | custom-call | flops 1000000 | bytes 4000000 | tf_op jit(solution)/shard_map/mix/pallas_call | solution.py:497
  33.2 4.8 %all-to-all-start.1 = ((bf16[128,5,128]{2,1,0:T(8,128)(2,1)}), bf16[128,5,128]{2,1,0:T(8,128)(2,1)S(1)}, u32[]{:S(2)}, u32[]{:S(2)}) async-start(bf16[128,5,128]{2,1,0:T(8,128)(2,1)} %get-tuple-element.28), calls=%async_computation.1 | async-start | bytes 524288 | tf_op jit(solution)/shard_map/all_to_all | solution.py:514
  38.0 0.0 collective-permute-done.2.refs_3_
  38.0 0.0 collective-permute-done.3.refs_4_
  38.1 0.0 copy-start.2
  38.1 8.0 %conv.3 = (f32[20,136,256]{2,1,0:T(8,128)}, f32[8,128]{1,0:T(8,128)}) custom-call(f32[2,3]{1,0:T(2,128)S(1)} %copy-done.1, bf16[2560,256]{1,0:T(8,128)(2,1)} %get-tuple-element.30.refs_0_, bf16[160,256]{1,0:T(8,128)(2,1)S(1)} %bitcast.9, bf16[160,256]{1,0:T(8,128)(2,1)S(1)} %bitcast.11, bf16[8,2880]{1,0:T(8,128)(2,1)S(1)} %collective-permute-done.2.refs_3_, ...), custom_call_target="tpu_custom_call" | custom-call | flops 20000000000 | bytes 4000000 | tf_op jit(solution)/shard_map/conv/pallas_call | solution.py:497
  46.1 2.4 %all-to-all-done.1.gathered_ref = bf16[128,5,128]{2,1,0:T(8,128)(2,1)S(1)} async-done(((bf16[128,5,128]{2,1,0:T(8,128)(2,1)}), bf16[128,5,128]{2,1,0:T(8,128)(2,1)S(1)}, u32[]{:S(2)}, u32[]{:S(2)}) %all-to-all-start.1) | async-done | bytes 163872 | tf_op jit(solution)/shard_map/all_to_all | solution.py:514
  48.5 0.0 copy-start.6
  48.5 0.7 copy-done.6
  49.2 0.0 copy-done.2
  49.2 7.7 %middle.1 = (bf16[17,160,256]{2,1,0:T(8,128)(2,1)}, bf16[8,2720]{1,0:T(8,128)(2,1)S(1)}, bf16[8,2720]{1,0:T(8,128)(2,1)S(1)}, bf16[128,5,128]{2,1,0:T(8,128)(2,1)}) custom-call(f32[2,20]{1,0:T(2,128)S(1)} %copy-done.2, bf16[128,5,128]{2,1,0:T(8,128)(2,1)} %copy-done.6, bf16[2,8,2,64,512]{4,3,2,1,0:T(8,128)(2,1)} %constant.19.clone.icols_all, ...), custom_call_target="tpu_custom_call" | custom-call | flops 1000000000 | bytes 4000000 | tf_op jit(solution)/shard_map/middle/pallas_call | solution.py:497
  56.9 0.6 collective-permute-start.4
  57.5 3.6 %collective-permute-start.5 = (bf16[8,2720]{1,0:T(8,128)(2,1)S(1)}, bf16[8,2720]{1,0:T(8,128)(2,1)S(1)}, u32[]{:S(2)}, u32[]{:S(2)}) collective-permute-start(bf16[8,2720]{1,0:T(8,128)(2,1)S(1)} %get-tuple-element.43), channel_id=1, source_target_pairs={{0,7},{1,0},{2,1},{3,2},{4,3},{5,4},{6,5},{7,6},{8,15},{9,8},{10,9... | collective-permute-start | bytes 130568 | tf_op jit(solution)/shard_map/ppermute | solution.py:524
  61.1 5.3 %all-to-all-start.2 = ((bf16[128,5,128]{2,1,0:T(8,128)(2,1)}), bf16[128,5,128]{2,1,0:T(8,128)(2,1)S(1)}, u32[]{:S(2)}, u32[]{:S(2)}) async-start(bf16[128,5,128]{2,1,0:T(8,128)(2,1)} %get-tuple-element.40), calls=%async_computation.2 | async-start | bytes 524288 | tf_op jit(solution)/shard_map/all_to_all | solution.py:514
  66.4 0.0 collective-permute-done.4.refs_1_
  66.4 0.0 collective-permute-done.5.refs_2_
  66.4 6.6 %conv.4 = (f32[20,64,256]{2,1,0:T(8,128)}, f32[8,128]{1,0:T(8,128)S(1)}) custom-call(f32[2,3]{1,0:T(2,128)S(1)} %copy-done.1, bf16[2720,256]{1,0:T(8,128)(2,1)} %bitcast.14, bf16[8,2720]{1,0:T(8,128)(2,1)S(1)} %collective-permute-done.4.refs_1_, bf16[8,2720]{1,0:T(8,128)(2,1)S(1)} %collective-permute-done.5.refs_2_, ...), custom_call_target="tpu_custom_call" | custom-call | flops 20000000000 | bytes 4000000 | tf_op jit(solution)/shard_map/conv/pallas_call | solution.py:497
  73.0 3.8 %all-to-all-done.2.received_ref = bf16[128,5,128]{2,1,0:T(8,128)(2,1)S(1)} async-done(((bf16[128,5,128]{2,1,0:T(8,128)(2,1)}), bf16[128,5,128]{2,1,0:T(8,128)(2,1)S(1)}, u32[]{:S(2)}, u32[]{:S(2)}) %all-to-all-start.2) | async-done | bytes 163872 | tf_op jit(solution)/shard_map/all_to_all | solution.py:514
  76.9 1.5 %mix.3 = (bf16[128,5,128]{2,1,0:T(8,128)(2,1)}, f32[8,128]{1,0:T(8,128)S(1)}) custom-call(f32[2,3]{1,0:T(2,128)S(1)} %copy-done.1, bf16[128,5,128]{2,1,0:T(8,128)(2,1)S(1)} %all-to-all-done.2.received_ref, f32[2,2,20,16,20]{4,3,2,1,0:T(8,128)S(1)} %bitcast.7, f32[8,128]{1,0:T(8,128)S(1)} %get-tuple-element.44.order_ref), custom_call_target="tpu_custom_call" | custom-call | flops 1000000 | bytes 4000000 | tf_op jit(solution)/shard_map/mix/pallas_call | solution.py:497
  78.3 5.7 %all-to-all-start.3 = ((bf16[128,5,128]{2,1,0:T(8,128)(2,1)}), bf16[128,5,128]{2,1,0:T(8,128)(2,1)S(1)}, u32[]{:S(2)}, u32[]{:S(2)}) async-start(bf16[128,5,128]{2,1,0:T(8,128)(2,1)} %get-tuple-element.45), calls=%async_computation.3 | async-start | bytes 524288 | tf_op jit(solution)/shard_map/all_to_all | solution.py:514
  84.1 6.3 %conv.5 = (f32[20,64,256]{2,1,0:T(8,128)}, f32[8,128]{1,0:T(8,128)}) custom-call(f32[2,3]{1,0:T(2,128)S(1)} %copy-done.1, bf16[2720,256]{1,0:T(8,128)(2,1)} %bitcast.15, bf16[8,2720]{1,0:T(8,128)(2,1)S(1)} %collective-permute-done.4.refs_1_, bf16[8,2720]{1,0:T(8,128)(2,1)S(1)} %collective-permute-done.5.refs_2_, ...), custom_call_target="tpu_custom_call" | custom-call | flops 20000000000 | bytes 4000000 | tf_op jit(solution)/shard_map/conv/pallas_call | solution.py:497
  90.4 4.4 %all-to-all-done.3.gathered_ref = bf16[128,5,128]{2,1,0:T(8,128)(2,1)S(1)} async-done(((bf16[128,5,128]{2,1,0:T(8,128)(2,1)}), bf16[128,5,128]{2,1,0:T(8,128)(2,1)S(1)}, u32[]{:S(2)}, u32[]{:S(2)}) %all-to-all-start.3) | async-done | bytes 163872 | tf_op jit(solution)/shard_map/all_to_all | solution.py:514
  94.8 5.1 %last.1 = bf16[20,128,256]{2,1,0:T(8,128)(2,1)} custom-call(f32[2,20]{1,0:T(2,128)S(1)} %copy-done.2, bf16[128,5,128]{2,1,0:T(8,128)(2,1)S(1)} %all-to-all-done.3.gathered_ref, bf16[2,8,2,64,512]{4,3,2,1,0:T(8,128)(2,1)} %constant.19.clone.icols_all, bf16[2,16,2,136,128]{4,3,2,1,0:T(8,128)(2,1)} %constant.18.clone.irows_all, ...), custom_call_target="tpu_custom_call" | custom-call | flops 1000000000 | bytes 4000000 | tf_op jit(solution)/shard_map/last/pallas_call | solution.py:497
  (2 shorter events, 0.0 us)
Async XLA Ops:
  0.0 20.3 %copy-start.8 = (bf16[2,20,180]{2,0,1:T(2,128)(2,1)S(1)}, bf16[2,20,180]{2,0,1:T(2,128)(2,1)}, u32[]{:S(2)}) copy-start(bf16[2,20,180]{2,0,1:T(2,128)(2,1)} %param.16) | copy-start | bytes 43204
  0.0 20.4 %copy-start.7 = (bf16[2,20,500]{2,0,1:T(2,128)(2,1)S(1)}, bf16[2,20,500]{2,0,1:T(2,128)(2,1)}, u32[]{:S(2)}) copy-start(bf16[2,20,500]{2,0,1:T(2,128)(2,1)} %param.17) | copy-start | bytes 120004
  0.0 20.4 %copy-start.3 = (bf16[60,960]{1,0:T(8,128)(2,1)S(1)}, bf16[60,960]{1,0:T(8,128)(2,1)}, u32[]{:S(2)}) copy-start(bf16[60,960]{1,0:T(8,128)(2,1)} %constant.20.clone.near_spread.refs_5_) | copy-start | bytes 345604
  0.0 20.4 %copy-start.4 = (s32[8,1600]{1,0:T(8,128)S(1)}, s32[8,1600]{1,0:T(8,128)}, u32[]{:S(2)}) copy-start(s32[8,1600]{1,0:T(8,128)} %constant.23.clone.far_offsets.refs_8_) | copy-start | bytes 153604
  0.0 20.4 %copy-start.5 = (s32[8,960]{1,0:T(8,128)S(1)}, s32[8,960]{1,0:T(8,128)}, u32[]{:S(2)}) copy-start(s32[8,960]{1,0:T(8,128)} %constant.22.clone.near_offsets.refs_7_) | copy-start | bytes 92164
  3.7 28.0 %all-to-all-start = ((f32[128,5,128]{2,1,0:T(8,128)}), f32[128,5,128]{2,1,0:T(8,128)S(1)}, u32[]{:S(2)}, u32[]{:S(2)}) async-start(f32[128,5,128]{2,1,0:T(8,128)} %get-tuple-element.27), calls=%async_computation | async-start | bytes 1048576 | tf_op jit(solution)/shard_map/all_to_all | solution.py:514
  14.9 12.5 %collective-permute-start = (bf16[20,8,256]{2,1,0:T(8,128)(2,1)S(1)}, bf16[20,8,256]{2,1,0:T(8,128)(2,1)S(1)}, u32[]{:S(2)}, u32[]{:S(2)}) collective-permute-start(bf16[20,8,256]{2,1,0:T(8,128)(2,1)S(1)} %get-tuple-element.31), channel_id=1, source_target_pairs={{0,8},{8,16},{16,24},{24,32},{32,40},{40,48},{48,56},{56,64},{64,7... | collective-permute-start | bytes 245768 | tf_op jit(solution)/shard_map/ppermute | solution.py:558
  15.0 12.4 %collective-permute-start.1 = (bf16[20,8,256]{2,1,0:T(8,128)(2,1)S(1)}, bf16[20,8,256]{2,1,0:T(8,128)(2,1)S(1)}, u32[]{:S(2)}, u32[]{:S(2)}) collective-permute-start(bf16[20,8,256]{2,1,0:T(8,128)(2,1)S(1)} %get-tuple-element.29.order_ref), channel_id=1, source_target_pairs={{0,120},{8,0},{16,8},{24,16},{32,24},{40,32},{48,40},{56,48},{64,5... | collective-permute-start | bytes 245768 | tf_op jit(solution)/shard_map/ppermute | solution.py:559
  27.4 4.3 %copy-start = (f32[2,2,20,20,16]{3,4,2,1,0:T(8,128)S(1)}, f32[2,2,20,20,16]{3,4,2,1,0:T(8,128)}, u32[]{:S(2)}) copy-start(f32[2,2,20,20,16]{3,4,2,1,0:T(8,128)} %param.15) | copy-start | bytes 307204
  27.4 4.4 %copy-start.1 = (f32[2,3]{1,0:T(2,128)S(1)}, f32[2,3]{1,0:T(2,128)}, u32[]{:S(2)}) copy-start(f32[2,3]{1,0:T(2,128)} %logits_ref.9) | copy-start | bytes 76
  27.6 10.4 %collective-permute-start.2 = (bf16[8,2880]{1,0:T(8,128)(2,1)S(1)}, bf16[8,2880]{1,0:T(8,128)(2,1)S(1)}, u32[]{:S(2)}, u32[]{:S(2)}) collective-permute-start(bf16[8,2880]{1,0:T(8,128)(2,1)S(1)} %get-tuple-element.34), channel_id=1, source_target_pairs={{0,1},{1,2},{2,3},{3,4},{4,5},{5,6},{6,7},{7,0},{8,9},{9,10},{10,1... | collective-permute-start | bytes 138248 | tf_op jit(solution)/shard_map/ppermute | solution.py:523
  29.2 8.9 %collective-permute-start.3 = (bf16[8,2880]{1,0:T(8,128)(2,1)S(1)}, bf16[8,2880]{1,0:T(8,128)(2,1)S(1)}, u32[]{:S(2)}, u32[]{:S(2)}) collective-permute-start(bf16[8,2880]{1,0:T(8,128)(2,1)S(1)} %get-tuple-element.35), channel_id=1, source_target_pairs={{0,7},{1,0},{2,1},{3,2},{4,3},{5,4},{6,5},{7,6},{8,15},{9,8},{10,9... | collective-permute-start | bytes 138248 | tf_op jit(solution)/shard_map/ppermute | solution.py:524
  33.2 15.3 %all-to-all-start.1 = ((bf16[128,5,128]{2,1,0:T(8,128)(2,1)}), bf16[128,5,128]{2,1,0:T(8,128)(2,1)S(1)}, u32[]{:S(2)}, u32[]{:S(2)}) async-start(bf16[128,5,128]{2,1,0:T(8,128)(2,1)} %get-tuple-element.28), calls=%async_computation.1 | async-start | bytes 524288 | tf_op jit(solution)/shard_map/all_to_all | solution.py:514
  38.1 11.2 %copy-start.2 = (f32[2,20]{1,0:T(2,128)S(1)}, f32[2,20]{1,0:T(2,128)}, u32[]{:S(2)}) copy-start(f32[2,20]{1,0:T(2,128)} %bias_ref.3) | copy-start | bytes 484
  48.5 0.7 copy-start.6
  56.9 9.5 %collective-permute-start.4 = (bf16[8,2720]{1,0:T(8,128)(2,1)S(1)}, bf16[8,2720]{1,0:T(8,128)(2,1)S(1)}, u32[]{:S(2)}, u32[]{:S(2)}) collective-permute-start(bf16[8,2720]{1,0:T(8,128)(2,1)S(1)} %get-tuple-element.42), channel_id=1, source_target_pairs={{0,1},{1,2},{2,3},{3,4},{4,5},{5,6},{6,7},{7,0},{8,9},{9,10},{10,1... | collective-permute-start | bytes 130568 | tf_op jit(solution)/shard_map/ppermute | solution.py:523
  57.5 8.9 %collective-permute-start.5 = (bf16[8,2720]{1,0:T(8,128)(2,1)S(1)}, bf16[8,2720]{1,0:T(8,128)(2,1)S(1)}, u32[]{:S(2)}, u32[]{:S(2)}) collective-permute-start(bf16[8,2720]{1,0:T(8,128)(2,1)S(1)} %get-tuple-element.43), channel_id=1, source_target_pairs={{0,7},{1,0},{2,1},{3,2},{4,3},{5,4},{6,5},{7,6},{8,15},{9,8},{10,9... | collective-permute-start | bytes 130568 | tf_op jit(solution)/shard_map/ppermute | solution.py:524
  61.1 15.7 %all-to-all-start.2 = ((bf16[128,5,128]{2,1,0:T(8,128)(2,1)}), bf16[128,5,128]{2,1,0:T(8,128)(2,1)S(1)}, u32[]{:S(2)}, u32[]{:S(2)}) async-start(bf16[128,5,128]{2,1,0:T(8,128)(2,1)} %get-tuple-element.40), calls=%async_computation.2 | async-start | bytes 524288 | tf_op jit(solution)/shard_map/all_to_all | solution.py:514
  78.3 16.4 %all-to-all-start.3 = ((bf16[128,5,128]{2,1,0:T(8,128)(2,1)}), bf16[128,5,128]{2,1,0:T(8,128)(2,1)S(1)}, u32[]{:S(2)}, u32[]{:S(2)}) async-start(bf16[128,5,128]{2,1,0:T(8,128)(2,1)} %get-tuple-element.45), calls=%async_computation.3 | async-start | bytes 524288 | tf_op jit(solution)/shard_map/all_to_all | solution.py:514

commit v4 on v3

--- a/solution.py
+++ b/solution.py
@@ -150,8 +150,7 @@
 
 
 def forward_kernel(
-    grid_all, cols_all, rows_all, out_ref, upper_ref, lower_ref, grid_buffer, chunk, cols, rows,
-    sems,
+    grid_all, cols_all, rows_all, out_ref, upper_ref, lower_ref, grid_buffer, cols, rows, sems
 ):
     gx, gy = indices()
     start = pl.multiple_of(gy * COLS, COLS)
@@ -173,10 +172,9 @@
         copy.wait()
 
     def write(half, group, value):
-        chunk[pl.ds(half, 64, stride=2), group, :] = value
+        out_ref[pl.ds(half, 64, stride=2), group, :] = value
 
     transform(lambda c: grid_buffer[c], cols, rows, write)
-    out_ref[...] = chunk[...].astype(out_ref.dtype)
 
 
 def mixture_of(logits_ref, layer):
@@ -224,11 +222,12 @@
 
 
 def edge_columns(rows):
-    dims = (((1,), (1,)), ((), ()))
-    return [
-        lax.dot_general(pattern, rows, dims, preferred_element_type=f32).astype(bf16)
-        for pattern in edge_patterns()
-    ]
+    patterns = [p.astype(f32) for p in edge_patterns()]
+    patterns = jnp.concatenate(patterns, axis=0).astype(bf16)
+    found = lax.dot_general(
+        patterns, rows, (((1,), (1,)), ((), ())), preferred_element_type=f32
+    )
+    return found[:8].astype(bf16), found[8:].astype(bf16)
 
 
 def edges(rows, first_ref, last_ref):
@@ -247,7 +246,7 @@
 
 NEAR = (-1, 0, 1)
 FAR = (-4, -2, 0, 2, 4)
-ENDS_LAST = (7, 15, 19)
+ENDS_LAST = (4, 9, 14, 17, 19)
 ENDS = {17: (8, 14, 17), 8: (5, 8)}
 
 
@@ -488,6 +487,7 @@
 hbm = pl.BlockSpec(memory_space=pltpu.HBM)
 LIMIT = 56 * 10**6
 SMALL = 4 * 10**6
+MIDDLE = 55 * 10**6
 
 
 def call(kernel, outs, args, specs, scratch=(), out_specs=None, flops=10**9, limit=LIMIT, name=None):
@@ -549,8 +549,7 @@
         forward_kernel, [chunks[0]] + [shape_of((C, 8, COLS), bf16)] * 2, (grid, fcols, frows),
         [hbm] * 3,
         (
-            pltpu.VMEM((C, ROWS, COLS), bf16), pltpu.VMEM((128, GROUPS, 128), f32), fcols_buffer,
-            pltpu.VMEM((2, 64, 2 * ROWS), bf16),
+            pltpu.VMEM((C, ROWS, COLS), bf16), fcols_buffer, pltpu.VMEM((2, 64, 2 * ROWS), bf16),
             dma((4 + GROUPS,)),
         ),
         name="forward",
@@ -618,7 +617,7 @@
             pltpu.VMEM((4, 320, 2 * COLS), f32), dma((4,)), dma, dma((2,)),
         ),
         out_specs=[hbm, vmem, vmem, vmem],
-        name="middle",
+        limit=MIDDLE, name="middle",
     )
     received = exchange(partial)
     field, around = field.reshape(17 * BLOCK, COLS), sides(first, last)
@@ -634,7 +633,7 @@
         (
             pltpu.VMEM((128, GROUPS, 128), f32), icols_buffer, pltpu.VMEM((2, ROWS, 128), bf16),
             pltpu.VMEM((C, ROWS, COLS), f32), pltpu.VMEM((C, ROWS, COLS), bf16),
-            pltpu.VMEM((4, 320, 2 * COLS), f32), dma((2,)), dma((2,)), dma((3,)),
+            pltpu.VMEM((4, 320, 2 * COLS), f32), dma((2,)), dma((2,)), dma((5,)),
         ),
         out_specs=hbm,
         name="last",

time: 102 us -> 100 us (0.980)
  transfers between devices with their start and end apart: 10 -> 10, of which waited for: 4 -> 4; matrix products, arithmetic and copies ran while one was open for 0% -> 0% of each run, Pallas kernels for 27% -> 28%
where the time goes in v4:
time: 100 us; the launch traced here: 98.6 us
  Pallas kernels  44.5 us (44%)
  starting transfers between devices  40.9 us (41%)
  waiting for transfers between devices  12.7 us (13%)
    pallas_call x10, Pallas kernels, call(): pl.pallas_call(kernel, out_shape=outs, in_specs=specs, out_specs=out_spec...  44.5 us
    all_to_all x4, starting transfers between devices, exchange(): return lax.all_to_all(value, both, split_axis=0, concat_axis=0, tiled=True)  27.1 us
    all_to_all x4, waiting for transfers between devices, exchange(): return lax.all_to_all(value, both, split_axis=0, concat_axis=0, tiled=True)  10.6 us
    ppermute x2, starting transfers between devices, sides(): right = lax.ppermute(first, 'gy', ring('gy', -1))  6.23 us
    ppermute x1, starting transfers between devices, on_device(): bottom = lax.ppermute(upper, 'gx', ring('gx', -1)).reshape(BLOCK, COLS)  5.35 us
    ppermute x2, starting transfers between devices, sides(): left = lax.ppermute(last, 'gy', ring('gy', 1))  2.15 us
    ppermute x1, waiting for transfers between devices, on_device(): top = lax.ppermute(lower, 'gx', ring('gx', 1)).reshape(BLOCK, COLS)  2.13 us
  transfers between devices with their start and end apart: 10, of which 4 were waited for; matrix products, arithmetic and copies ran while one was open for 0% of the time, Pallas kernels for 28%

profile of v4, /device:TPU:0, one launch (start us, length us, event | category | flops | bytes accessed | tf_op | source)
XLA Modules:
  0.0 98.6 jit_solution(18404832920576413630)
XLA Ops:
  0.0 0.0 copy-start.7
  0.0 0.0 copy-start.6
  0.0 0.0 copy-start.3
  0.0 0.0 copy-start.4
  0.0 0.0 copy-start.5
  0.0 3.7 %forward.1 = (f32[128,5,128]{2,1,0:T(8,128)}, bf16[20,8,256]{2,1,0:T(8,128)(2,1)S(1)}, bf16[20,8,256]{2,1,0:T(8,128)(2,1)S(1)}) custom-call(bf16[20,128,256]{2,1,0:T(8,128)(2,1)} %bitcast.12, bf16[2,2048,256]{2,1,0:T(8,128)(2,1)} %constant.16.clone.cols_all.fcols_all, bf16[2,16,2,64,288]{4,3,2,1,0:T(8,128)(2,1)} %constant.17.clone.rows_all.frows_all), custom_call_target="tpu_custom_call" | custom-call | flops 1000000000 | bytes 4000000 | tf_op jit(solution)/shard_map/forward/pallas_call | solution.py:497
  3.7 11.2 %all-to-all-start = ((f32[128,5,128]{2,1,0:T(8,128)}), f32[128,5,128]{2,1,0:T(8,128)S(1)}, u32[]{:S(2)}, u32[]{:S(2)}) async-start(f32[128,5,128]{2,1,0:T(8,128)} %get-tuple-element.27), calls=%async_computation | async-start | bytes 1048576 | tf_op jit(solution)/shard_map/all_to_all | solution.py:514
  14.9 0.1 collective-permute-start
  15.0 5.3 %collective-permute-start.1 = (bf16[20,8,256]{2,1,0:T(8,128)(2,1)S(1)}, bf16[20,8,256]{2,1,0:T(8,128)(2,1)S(1)}, u32[]{:S(2)}, u32[]{:S(2)}) collective-permute-start(bf16[20,8,256]{2,1,0:T(8,128)(2,1)S(1)} %get-tuple-element.29.order_ref), channel_id=1, source_target_pairs={{0,120},{8,0},{16,8},{24,16},{32,24},{40,32},{48,40},{56,48},{64,5... | collective-permute-start | bytes 245768 | tf_op jit(solution)/shard_map/ppermute | solution.py:558
  20.3 0.0 copy-done.7
  20.3 0.0 copy-done.6
  20.4 0.0 copy-done.3
  20.4 0.0 copy-done.4
  20.4 0.0 copy-done.5
  20.4 4.9 %own.1 = (bf16[2560,256]{1,0:T(8,128)(2,1)}, bf16[8,2560]{1,0:T(8,128)(2,1)S(1)}, bf16[8,2560]{1,0:T(8,128)(2,1)S(1)}, bf16[160,960]{1,0:T(8,128)(2,1)}, bf16[160,1600]{1,0:T(8,128)(2,1)}) custom-call(bf16[20,128,256]{2,1,0:T(8,128)(2,1)} %bitcast.13, bf16[2,20,180]{2,1,0:T(8,128)(2,1)S(1)} %copy.15.near_ref.refs_3_, ...), custom_call_target="tpu_custom_call" | custom-call | flops 1000000000 | bytes 4000000 | tf_op jit(solution)/shard_map/own/pallas_call | solution.py:497
  25.3 2.1 %collective-permute-done = bf16[20,8,256]{2,1,0:T(8,128)(2,1)S(1)} collective-permute-done((bf16[20,8,256]{2,1,0:T(8,128)(2,1)S(1)}, bf16[20,8,256]{2,1,0:T(8,128)(2,1)S(1)}, u32[]{:S(2)}, u32[]{:S(2)}) %collective-permute-start) | collective-permute-done | bytes 81952 | tf_op jit(solution)/shard_map/ppermute | solution.py:557
  27.4 0.0 collective-permute-done.1
  27.4 0.0 copy-start
  27.4 0.0 copy-start.1
  27.4 0.1 edges.1
  27.5 1.6 %collective-permute-start.2 = (bf16[8,2880]{1,0:T(8,128)(2,1)S(1)}, bf16[8,2880]{1,0:T(8,128)(2,1)S(1)}, u32[]{:S(2)}, u32[]{:S(2)}) collective-permute-start(bf16[8,2880]{1,0:T(8,128)(2,1)S(1)} %get-tuple-element.34), channel_id=1, source_target_pairs={{0,1},{1,2},{2,3},{3,4},{4,5},{5,6},{6,7},{7,0},{8,9},{9,10},{10,1... | collective-permute-start | bytes 138248 | tf_op jit(solution)/shard_map/ppermute | solution.py:523
  29.1 2.6 %collective-permute-start.3 = (bf16[8,2880]{1,0:T(8,128)(2,1)S(1)}, bf16[8,2880]{1,0:T(8,128)(2,1)S(1)}, u32[]{:S(2)}, u32[]{:S(2)}) collective-permute-start(bf16[8,2880]{1,0:T(8,128)(2,1)S(1)} %get-tuple-element.35), channel_id=1, source_target_pairs={{0,7},{1,0},{2,1},{3,2},{4,3},{5,4},{6,5},{7,6},{8,15},{9,8},{10,9... | collective-permute-start | bytes 138248 | tf_op jit(solution)/shard_map/ppermute | solution.py:524
  31.7 0.0 all-to-all-done.received_ref
  31.7 0.0 copy-done
  31.7 0.0 copy-done.1
  31.7 1.4 %mix.2 = (bf16[128,5,128]{2,1,0:T(8,128)(2,1)}, f32[8,128]{1,0:T(8,128)S(1)}) custom-call(f32[2,3]{1,0:T(2,128)S(1)} %copy-done.1, f32[128,5,128]{2,1,0:T(8,128)S(1)} %all-to-all-done.received_ref, f32[2,2,20,16,20]{4,3,2,1,0:T(8,128)S(1)} %bitcast.6, f32[2,3]{1,0:T(2,128)S(1)} %copy-done.1), custom_call_target="tpu_custom_call" | custom-call | flops 1000000 | bytes 4000000 | tf_op jit(solution)/shard_map/mix/pallas_call | solution.py:497
  33.2 4.8 %all-to-all-start.1 = ((bf16[128,5,128]{2,1,0:T(8,128)(2,1)}), bf16[128,5,128]{2,1,0:T(8,128)(2,1)S(1)}, u32[]{:S(2)}, u32[]{:S(2)}) async-start(bf16[128,5,128]{2,1,0:T(8,128)(2,1)} %get-tuple-element.28), calls=%async_computation.1 | async-start | bytes 524288 | tf_op jit(solution)/shard_map/all_to_all | solution.py:514
  38.0 0.0 collective-permute-done.2.refs_3_
  38.0 0.0 collective-permute-done.3.refs_4_
  38.0 0.0 copy-start.2
  38.0 8.1 %conv.3 = (f32[20,136,256]{2,1,0:T(8,128)}, f32[8,128]{1,0:T(8,128)}) custom-call(f32[2,3]{1,0:T(2,128)S(1)} %copy-done.1, bf16[2560,256]{1,0:T(8,128)(2,1)} %get-tuple-element.30.refs_0_, bf16[160,256]{1,0:T(8,128)(2,1)S(1)} %bitcast.9, bf16[160,256]{1,0:T(8,128)(2,1)S(1)} %bitcast.11, bf16[8,2880]{1,0:T(8,128)(2,1)S(1)} %collective-permute-done.2.refs_3_, ...), custom_call_target="tpu_custom_call" | custom-call | flops 20000000000 | bytes 4000000 | tf_op jit(solution)/shard_map/conv/pallas_call | solution.py:497
  46.1 2.4 %all-to-all-done.1.gathered_ref = bf16[128,5,128]{2,1,0:T(8,128)(2,1)S(1)} async-done(((bf16[128,5,128]{2,1,0:T(8,128)(2,1)}), bf16[128,5,128]{2,1,0:T(8,128)(2,1)S(1)}, u32[]{:S(2)}, u32[]{:S(2)}) %all-to-all-start.1) | async-done | bytes 163872 | tf_op jit(solution)/shard_map/all_to_all | solution.py:514
  48.5 0.0 copy-done.2
  48.5 6.9 %middle.1 = (bf16[17,160,256]{2,1,0:T(8,128)(2,1)}, bf16[8,2720]{1,0:T(8,128)(2,1)S(1)}, bf16[8,2720]{1,0:T(8,128)(2,1)S(1)}, bf16[128,5,128]{2,1,0:T(8,128)(2,1)}) custom-call(f32[2,20]{1,0:T(2,128)S(1)} %copy-done.2, bf16[128,5,128]{2,1,0:T(8,128)(2,1)S(1)} %all-to-all-done.1.gathered_ref, bf16[2,8,2,64,512]{4,3,2,1,0:T(8,128)(2,1)} %constant.19.clone.icols_all, ...), custom_call_target="tpu_custom_call" | custom-call | flops 1000000000 | bytes 4000000 | tf_op jit(solution)/shard_map/middle/pallas_call | solution.py:497
  55.4 0.6 collective-permute-start.4
  56.0 3.6 %collective-permute-start.5 = (bf16[8,2720]{1,0:T(8,128)(2,1)S(1)}, bf16[8,2720]{1,0:T(8,128)(2,1)S(1)}, u32[]{:S(2)}, u32[]{:S(2)}) collective-permute-start(bf16[8,2720]{1,0:T(8,128)(2,1)S(1)} %get-tuple-element.43), channel_id=1, source_target_pairs={{0,7},{1,0},{2,1},{3,2},{4,3},{5,4},{6,5},{7,6},{8,15},{9,8},{10,9... | collective-permute-start | bytes 130568 | tf_op jit(solution)/shard_map/ppermute | solution.py:524
  59.6 5.4 %all-to-all-start.2 = ((bf16[128,5,128]{2,1,0:T(8,128)(2,1)}), bf16[128,5,128]{2,1,0:T(8,128)(2,1)S(1)}, u32[]{:S(2)}, u32[]{:S(2)}) async-start(bf16[128,5,128]{2,1,0:T(8,128)(2,1)} %get-tuple-element.40), calls=%async_computation.2 | async-start | bytes 524288 | tf_op jit(solution)/shard_map/all_to_all | solution.py:514
  65.0 0.0 collective-permute-done.4.refs_1_
  65.0 0.0 collective-permute-done.5.refs_2_
  65.0 6.6 %conv.4 = (f32[20,64,256]{2,1,0:T(8,128)}, f32[8,128]{1,0:T(8,128)S(1)}) custom-call(f32[2,3]{1,0:T(2,128)S(1)} %copy-done.1, bf16[2720,256]{1,0:T(8,128)(2,1)} %bitcast.14, bf16[8,2720]{1,0:T(8,128)(2,1)S(1)} %collective-permute-done.4.refs_1_, bf16[8,2720]{1,0:T(8,128)(2,1)S(1)} %collective-permute-done.5.refs_2_, ...), custom_call_target="tpu_custom_call" | custom-call | flops 20000000000 | bytes 4000000 | tf_op jit(solution)/shard_map/conv/pallas_call | solution.py:497
  71.6 3.8 %all-to-all-done.2.received_ref = bf16[128,5,128]{2,1,0:T(8,128)(2,1)S(1)} async-done(((bf16[128,5,128]{2,1,0:T(8,128)(2,1)}), bf16[128,5,128]{2,1,0:T(8,128)(2,1)S(1)}, u32[]{:S(2)}, u32[]{:S(2)}) %all-to-all-start.2) | async-done | bytes 163872 | tf_op jit(solution)/shard_map/all_to_all | solution.py:514
  75.4 1.5 %mix.3 = (bf16[128,5,128]{2,1,0:T(8,128)(2,1)}, f32[8,128]{1,0:T(8,128)S(1)}) custom-call(f32[2,3]{1,0:T(2,128)S(1)} %copy-done.1, bf16[128,5,128]{2,1,0:T(8,128)(2,1)S(1)} %all-to-all-done.2.received_ref, f32[2,2,20,16,20]{4,3,2,1,0:T(8,128)S(1)} %bitcast.7, f32[8,128]{1,0:T(8,128)S(1)} %get-tuple-element.44.order_ref), custom_call_target="tpu_custom_call" | custom-call | flops 1000000 | bytes 4000000 | tf_op jit(solution)/shard_map/mix/pallas_call | solution.py:497
  76.9 5.8 %all-to-all-start.3 = ((bf16[128,5,128]{2,1,0:T(8,128)(2,1)}), bf16[128,5,128]{2,1,0:T(8,128)(2,1)S(1)}, u32[]{:S(2)}, u32[]{:S(2)}) async-start(bf16[128,5,128]{2,1,0:T(8,128)(2,1)} %get-tuple-element.45), calls=%async_computation.3 | async-start | bytes 524288 | tf_op jit(solution)/shard_map/all_to_all | solution.py:514
  82.6 6.3 %conv.5 = (f32[20,64,256]{2,1,0:T(8,128)}, f32[8,128]{1,0:T(8,128)}) custom-call(f32[2,3]{1,0:T(2,128)S(1)} %copy-done.1, bf16[2720,256]{1,0:T(8,128)(2,1)} %bitcast.15, bf16[8,2720]{1,0:T(8,128)(2,1)S(1)} %collective-permute-done.4.refs_1_, bf16[8,2720]{1,0:T(8,128)(2,1)S(1)} %collective-permute-done.5.refs_2_, ...), custom_call_target="tpu_custom_call" | custom-call | flops 20000000000 | bytes 4000000 | tf_op jit(solution)/shard_map/conv/pallas_call | solution.py:497
  88.9 4.4 %all-to-all-done.3.gathered_ref = bf16[128,5,128]{2,1,0:T(8,128)(2,1)S(1)} async-done(((bf16[128,5,128]{2,1,0:T(8,128)(2,1)}), bf16[128,5,128]{2,1,0:T(8,128)(2,1)S(1)}, u32[]{:S(2)}, u32[]{:S(2)}) %all-to-all-start.3) | async-done | bytes 163872 | tf_op jit(solution)/shard_map/all_to_all | solution.py:514
  93.3 5.1 %last.1 = bf16[20,128,256]{2,1,0:T(8,128)(2,1)} custom-call(f32[2,20]{1,0:T(2,128)S(1)} %copy-done.2, bf16[128,5,128]{2,1,0:T(8,128)(2,1)S(1)} %all-to-all-done.3.gathered_ref, bf16[2,8,2,64,512]{4,3,2,1,0:T(8,128)(2,1)} %constant.19.clone.icols_all, bf16[2,16,2,136,128]{4,3,2,1,0:T(8,128)(2,1)} %constant.18.clone.irows_all, ...), custom_call_target="tpu_custom_call" | custom-call | flops 1000000000 | bytes 4000000 | tf_op jit(solution)/shard_map/last/pallas_call | solution.py:497
  (2 shorter events, 0.0 us)
Async XLA Ops:
  0.0 20.3 %copy-start.7 = (bf16[2,20,180]{2,0,1:T(2,128)(2,1)S(1)}, bf16[2,20,180]{2,0,1:T(2,128)(2,1)}, u32[]{:S(2)}) copy-start(bf16[2,20,180]{2,0,1:T(2,128)(2,1)} %param.16) | copy-start | bytes 43204
  0.0 20.3 %copy-start.6 = (bf16[2,20,500]{2,0,1:T(2,128)(2,1)S(1)}, bf16[2,20,500]{2,0,1:T(2,128)(2,1)}, u32[]{:S(2)}) copy-start(bf16[2,20,500]{2,0,1:T(2,128)(2,1)} %param.17) | copy-start | bytes 120004
  0.0 20.3 %copy-start.3 = (bf16[60,960]{1,0:T(8,128)(2,1)S(1)}, bf16[60,960]{1,0:T(8,128)(2,1)}, u32[]{:S(2)}) copy-start(bf16[60,960]{1,0:T(8,128)(2,1)} %constant.20.clone.near_spread.refs_5_) | copy-start | bytes 345604
  0.0 20.4 %copy-start.4 = (s32[8,1600]{1,0:T(8,128)S(1)}, s32[8,1600]{1,0:T(8,128)}, u32[]{:S(2)}) copy-start(s32[8,1600]{1,0:T(8,128)} %constant.23.clone.far_offsets.refs_8_) | copy-start | bytes 153604
  0.0 20.4 %copy-start.5 = (s32[8,960]{1,0:T(8,128)S(1)}, s32[8,960]{1,0:T(8,128)}, u32[]{:S(2)}) copy-start(s32[8,960]{1,0:T(8,128)} %constant.22.clone.near_offsets.refs_7_) | copy-start | bytes 92164
  3.7 28.0 %all-to-all-start = ((f32[128,5,128]{2,1,0:T(8,128)}), f32[128,5,128]{2,1,0:T(8,128)S(1)}, u32[]{:S(2)}, u32[]{:S(2)}) async-start(f32[128,5,128]{2,1,0:T(8,128)} %get-tuple-element.27), calls=%async_computation | async-start | bytes 1048576 | tf_op jit(solution)/shard_map/all_to_all | solution.py:514
  14.9 12.5 %collective-permute-start = (bf16[20,8,256]{2,1,0:T(8,128)(2,1)S(1)}, bf16[20,8,256]{2,1,0:T(8,128)(2,1)S(1)}, u32[]{:S(2)}, u32[]{:S(2)}) collective-permute-start(bf16[20,8,256]{2,1,0:T(8,128)(2,1)S(1)} %get-tuple-element.31), channel_id=1, source_target_pairs={{0,8},{8,16},{16,24},{24,32},{32,40},{40,48},{48,56},{56,64},{64,7... | collective-permute-start | bytes 245768 | tf_op jit(solution)/shard_map/ppermute | solution.py:557
  15.0 12.4 %collective-permute-start.1 = (bf16[20,8,256]{2,1,0:T(8,128)(2,1)S(1)}, bf16[20,8,256]{2,1,0:T(8,128)(2,1)S(1)}, u32[]{:S(2)}, u32[]{:S(2)}) collective-permute-start(bf16[20,8,256]{2,1,0:T(8,128)(2,1)S(1)} %get-tuple-element.29.order_ref), channel_id=1, source_target_pairs={{0,120},{8,0},{16,8},{24,16},{32,24},{40,32},{48,40},{56,48},{64,5... | collective-permute-start | bytes 245768 | tf_op jit(solution)/shard_map/ppermute | solution.py:558
  27.4 4.3 %copy-start = (f32[2,2,20,20,16]{3,4,2,1,0:T(8,128)S(1)}, f32[2,2,20,20,16]{3,4,2,1,0:T(8,128)}, u32[]{:S(2)}) copy-start(f32[2,2,20,20,16]{3,4,2,1,0:T(8,128)} %param.15) | copy-start | bytes 307204
  27.4 4.3 %copy-start.1 = (f32[2,3]{1,0:T(2,128)S(1)}, f32[2,3]{1,0:T(2,128)}, u32[]{:S(2)}) copy-start(f32[2,3]{1,0:T(2,128)} %logits_ref.9) | copy-start | bytes 76
  27.5 10.4 %collective-permute-start.2 = (bf16[8,2880]{1,0:T(8,128)(2,1)S(1)}, bf16[8,2880]{1,0:T(8,128)(2,1)S(1)}, u32[]{:S(2)}, u32[]{:S(2)}) collective-permute-start(bf16[8,2880]{1,0:T(8,128)(2,1)S(1)} %get-tuple-element.34), channel_id=1, source_target_pairs={{0,1},{1,2},{2,3},{3,4},{4,5},{5,6},{6,7},{7,0},{8,9},{9,10},{10,1... | collective-permute-start | bytes 138248 | tf_op jit(solution)/shard_map/ppermute | solution.py:523
  29.1 8.9 %collective-permute-start.3 = (bf16[8,2880]{1,0:T(8,128)(2,1)S(1)}, bf16[8,2880]{1,0:T(8,128)(2,1)S(1)}, u32[]{:S(2)}, u32[]{:S(2)}) collective-permute-start(bf16[8,2880]{1,0:T(8,128)(2,1)S(1)} %get-tuple-element.35), channel_id=1, source_target_pairs={{0,7},{1,0},{2,1},{3,2},{4,3},{5,4},{6,5},{7,6},{8,15},{9,8},{10,9... | collective-permute-start | bytes 138248 | tf_op jit(solution)/shard_map/ppermute | solution.py:524
  33.2 15.3 %all-to-all-start.1 = ((bf16[128,5,128]{2,1,0:T(8,128)(2,1)}), bf16[128,5,128]{2,1,0:T(8,128)(2,1)S(1)}, u32[]{:S(2)}, u32[]{:S(2)}) async-start(bf16[128,5,128]{2,1,0:T(8,128)(2,1)} %get-tuple-element.28), calls=%async_computation.1 | async-start | bytes 524288 | tf_op jit(solution)/shard_map/all_to_all | solution.py:514
  38.0 10.5 %copy-start.2 = (f32[2,20]{1,0:T(2,128)S(1)}, f32[2,20]{1,0:T(2,128)}, u32[]{:S(2)}) copy-start(f32[2,20]{1,0:T(2,128)} %bias_ref.3) | copy-start | bytes 484
  55.4 9.6 %collective-permute-start.4 = (bf16[8,2720]{1,0:T(8,128)(2,1)S(1)}, bf16[8,2720]{1,0:T(8,128)(2,1)S(1)}, u32[]{:S(2)}, u32[]{:S(2)}) collective-permute-start(bf16[8,2720]{1,0:T(8,128)(2,1)S(1)} %get-tuple-element.42), channel_id=1, source_target_pairs={{0,1},{1,2},{2,3},{3,4},{4,5},{5,6},{6,7},{7,0},{8,9},{9,10},{10,1... | collective-permute-start | bytes 130568 | tf_op jit(solution)/shard_map/ppermute | solution.py:523
  56.0 9.0 %collective-permute-start.5 = (bf16[8,2720]{1,0:T(8,128)(2,1)S(1)}, bf16[8,2720]{1,0:T(8,128)(2,1)S(1)}, u32[]{:S(2)}, u32[]{:S(2)}) collective-permute-start(bf16[8,2720]{1,0:T(8,128)(2,1)S(1)} %get-tuple-element.43), channel_id=1, source_target_pairs={{0,7},{1,0},{2,1},{3,2},{4,3},{5,4},{6,5},{7,6},{8,15},{9,8},{10,9... | collective-permute-start | bytes 130568 | tf_op jit(solution)/shard_map/ppermute | solution.py:524
  59.6 15.8 %all-to-all-start.2 = ((bf16[128,5,128]{2,1,0:T(8,128)(2,1)}), bf16[128,5,128]{2,1,0:T(8,128)(2,1)S(1)}, u32[]{:S(2)}, u32[]{:S(2)}) async-start(bf16[128,5,128]{2,1,0:T(8,128)(2,1)} %get-tuple-element.40), calls=%async_computation.2 | async-start | bytes 524288 | tf_op jit(solution)/shard_map/all_to_all | solution.py:514
  76.9 16.4 %all-to-all-start.3 = ((bf16[128,5,128]{2,1,0:T(8,128)(2,1)}), bf16[128,5,128]{2,1,0:T(8,128)(2,1)S(1)}, u32[]{:S(2)}, u32[]{:S(2)}) async-start(bf16[128,5,128]{2,1,0:T(8,128)(2,1)} %get-tuple-element.45), calls=%async_computation.3 | async-start | bytes 524288 | tf_op jit(solution)/shard_map/all_to_all | solution.py:514

commit v5 on v4

--- a/solution.py
+++ b/solution.py
@@ -203,11 +203,8 @@
     lane = lax.broadcasted_iota(jnp.int32, (C, 128), 1)
     row = lax.broadcasted_iota(jnp.int32, (C, 128), 0)
     lines = jnp.where((lane >> 5) == (row & 3), lines, 0.0)
-    group = lax.broadcasted_iota(jnp.int32, (8, C), 0)
-    member = lax.broadcasted_iota(jnp.int32, (8, C), 1)
-    gather = jnp.where((member >> 2) == group, 1.0, 0.0)
-    mixed = jnp.dot(gather, lines, precision=lax.Precision.HIGHEST, preferred_element_type=f32)
-    mixed = mixed[:GROUPS].astype(out_ref.dtype)
+    rows = [jnp.sum(lines[4 * g : 4 * g + 4], axis=0, keepdims=True) for g in range(GROUPS)]
+    mixed = jnp.concatenate(rows, axis=0).astype(out_ref.dtype)
     out_ref[...] = jnp.broadcast_to(mixed[None], out_ref.shape)
     marker_ref[...] = lines[:8]
 
@@ -488,6 +485,7 @@
 LIMIT = 56 * 10**6
 SMALL = 4 * 10**6
 MIDDLE = 55 * 10**6
+FORWARD = 55 * 10**6
 
 
 def call(kernel, outs, args, specs, scratch=(), out_specs=None, flops=10**9, limit=LIMIT, name=None):
@@ -552,7 +550,7 @@
             pltpu.VMEM((C, ROWS, COLS), bf16), fcols_buffer, pltpu.VMEM((2, 64, 2 * ROWS), bf16),
             dma((4 + GROUPS,)),
         ),
-        name="forward",
+        limit=FORWARD, name="forward",
     )
     top = lax.ppermute(lower, "gx", ring("gx", 1)).reshape(BLOCK, COLS)
     bottom = lax.ppermute(upper, "gx", ring("gx", -1)).reshape(BLOCK, COLS)

time: 100 us -> 99.8 us (level)
  no operation moved by 1% of the time
where the time goes in v5:
time: 99.8 us; the launch traced here: 98.3 us
  Pallas kernels  44.3 us (44%)
  starting transfers between devices  40.9 us (41%)
  waiting for transfers between devices  12.7 us (13%)
    pallas_call x10, Pallas kernels, call(): pl.pallas_call(kernel, out_shape=outs, in_specs=specs, out_specs=out_spec...  44.3 us
    all_to_all x4, starting transfers between devices, exchange(): return lax.all_to_all(value, both, split_axis=0, concat_axis=0, tiled=True)  27.1 us
    all_to_all x4, waiting for transfers between devices, exchange(): return lax.all_to_all(value, both, split_axis=0, concat_axis=0, tiled=True)  10.6 us
    ppermute x2, starting transfers between devices, sides(): right = lax.ppermute(first, 'gy', ring('gy', -1))  6.22 us
    ppermute x1, starting transfers between devices, on_device(): bottom = lax.ppermute(upper, 'gx', ring('gx', -1)).reshape(BLOCK, COLS)  5.35 us
    ppermute x2, starting transfers between devices, sides(): left = lax.ppermute(last, 'gy', ring('gy', 1))  2.16 us
    ppermute x1, waiting for transfers between devices, on_device(): top = lax.ppermute(lower, 'gx', ring('gx', 1)).reshape(BLOCK, COLS)  2.13 us
  transfers between devices with their start and end apart: 10, of which 4 were waited for; matrix products, arithmetic and copies ran while one was open for 0% of the time, Pallas kernels for 28%

profile of v5, /device:TPU:0, one launch (start us, length us, event | category | flops | bytes accessed | tf_op | source)
XLA Modules:
  0.0 98.3 jit_solution(811559830551188941)
XLA Ops:
  0.0 0.0 copy-start.7
  0.0 0.0 copy-start.6
  0.0 0.0 copy-start.3
  0.0 0.0 copy-start.4
  0.0 0.0 copy-start.5
  0.0 3.7 %forward.1 = (f32[128,5,128]{2,1,0:T(8,128)}, bf16[20,8,256]{2,1,0:T(8,128)(2,1)S(1)}, bf16[20,8,256]{2,1,0:T(8,128)(2,1)S(1)}) custom-call(bf16[20,128,256]{2,1,0:T(8,128)(2,1)} %bitcast.12, bf16[2,2048,256]{2,1,0:T(8,128)(2,1)} %constant.16.clone.cols_all.fcols_all, bf16[2,16,2,64,288]{4,3,2,1,0:T(8,128)(2,1)} %constant.17.clone.rows_all.frows_all), custom_call_target="tpu_custom_call" | custom-call | flops 1000000000 | bytes 4000000 | tf_op jit(solution)/shard_map/forward/pallas_call | solution.py:495
  3.7 11.2 %all-to-all-start = ((f32[128,5,128]{2,1,0:T(8,128)}), f32[128,5,128]{2,1,0:T(8,128)S(1)}, u32[]{:S(2)}, u32[]{:S(2)}) async-start(f32[128,5,128]{2,1,0:T(8,128)} %get-tuple-element.27), calls=%async_computation | async-start | bytes 1048576 | tf_op jit(solution)/shard_map/all_to_all | solution.py:512
  14.9 0.1 collective-permute-start
  15.0 5.3 %collective-permute-start.1 = (bf16[20,8,256]{2,1,0:T(8,128)(2,1)S(1)}, bf16[20,8,256]{2,1,0:T(8,128)(2,1)S(1)}, u32[]{:S(2)}, u32[]{:S(2)}) collective-permute-start(bf16[20,8,256]{2,1,0:T(8,128)(2,1)S(1)} %get-tuple-element.29.order_ref), channel_id=1, source_target_pairs={{0,120},{8,0},{16,8},{24,16},{32,24},{40,32},{48,40},{56,48},{64,5... | collective-permute-start | bytes 245768 | tf_op jit(solution)/shard_map/ppermute | solution.py:556
  20.3 0.0 copy-done.7
  20.3 0.0 copy-done.6
  20.4 0.0 copy-done.3
  20.4 0.0 copy-done.4
  20.4 0.0 copy-done.5
  20.4 4.9 %own.1 = (bf16[2560,256]{1,0:T(8,128)(2,1)}, bf16[8,2560]{1,0:T(8,128)(2,1)S(1)}, bf16[8,2560]{1,0:T(8,128)(2,1)S(1)}, bf16[160,960]{1,0:T(8,128)(2,1)}, bf16[160,1600]{1,0:T(8,128)(2,1)}) custom-call(bf16[20,128,256]{2,1,0:T(8,128)(2,1)} %bitcast.13, bf16[2,20,180]{2,1,0:T(8,128)(2,1)S(1)} %copy.15.near_ref.refs_3_, ...), custom_call_target="tpu_custom_call" | custom-call | flops 1000000000 | bytes 4000000 | tf_op jit(solution)/shard_map/own/pallas_call | solution.py:495
  25.3 2.1 %collective-permute-done = bf16[20,8,256]{2,1,0:T(8,128)(2,1)S(1)} collective-permute-done((bf16[20,8,256]{2,1,0:T(8,128)(2,1)S(1)}, bf16[20,8,256]{2,1,0:T(8,128)(2,1)S(1)}, u32[]{:S(2)}, u32[]{:S(2)}) %collective-permute-start) | collective-permute-done | bytes 81952 | tf_op jit(solution)/shard_map/ppermute | solution.py:555
  27.4 0.0 collective-permute-done.1
  27.4 0.0 copy-start
  27.4 0.0 copy-start.1
  27.4 0.1 edges.1
  27.5 1.6 %collective-permute-start.2 = (bf16[8,2880]{1,0:T(8,128)(2,1)S(1)}, bf16[8,2880]{1,0:T(8,128)(2,1)S(1)}, u32[]{:S(2)}, u32[]{:S(2)}) collective-permute-start(bf16[8,2880]{1,0:T(8,128)(2,1)S(1)} %get-tuple-element.34), channel_id=1, source_target_pairs={{0,1},{1,2},{2,3},{3,4},{4,5},{5,6},{6,7},{7,0},{8,9},{9,10},{10,1... | collective-permute-start | bytes 138248 | tf_op jit(solution)/shard_map/ppermute | solution.py:521
  29.1 2.6 %collective-permute-start.3 = (bf16[8,2880]{1,0:T(8,128)(2,1)S(1)}, bf16[8,2880]{1,0:T(8,128)(2,1)S(1)}, u32[]{:S(2)}, u32[]{:S(2)}) collective-permute-start(bf16[8,2880]{1,0:T(8,128)(2,1)S(1)} %get-tuple-element.35), channel_id=1, source_target_pairs={{0,7},{1,0},{2,1},{3,2},{4,3},{5,4},{6,5},{7,6},{8,15},{9,8},{10,9... | collective-permute-start | bytes 138248 | tf_op jit(solution)/shard_map/ppermute | solution.py:522
  31.7 0.0 all-to-all-done.received_ref
  31.7 0.0 copy-done
  31.7 0.0 copy-done.1
  31.7 1.3 %mix.2 = (bf16[128,5,128]{2,1,0:T(8,128)(2,1)}, f32[8,128]{1,0:T(8,128)S(1)}) custom-call(f32[2,3]{1,0:T(2,128)S(1)} %copy-done.1, f32[128,5,128]{2,1,0:T(8,128)S(1)} %all-to-all-done.received_ref, f32[2,2,20,16,20]{4,3,2,1,0:T(8,128)S(1)} %bitcast.6, f32[2,3]{1,0:T(2,128)S(1)} %copy-done.1), custom_call_target="tpu_custom_call" | custom-call | flops 1000000 | bytes 4000000 | tf_op jit(solution)/shard_map/mix/pallas_call | solution.py:495
  33.1 4.8 %all-to-all-start.1 = ((bf16[128,5,128]{2,1,0:T(8,128)(2,1)}), bf16[128,5,128]{2,1,0:T(8,128)(2,1)S(1)}, u32[]{:S(2)}, u32[]{:S(2)}) async-start(bf16[128,5,128]{2,1,0:T(8,128)(2,1)} %get-tuple-element.28), calls=%async_computation.1 | async-start | bytes 524288 | tf_op jit(solution)/shard_map/all_to_all | solution.py:512
  37.9 0.0 collective-permute-done.2.refs_3_
  37.9 0.0 collective-permute-done.3.refs_4_
  37.9 0.0 copy-start.2
  37.9 8.1 %conv.3 = (f32[20,136,256]{2,1,0:T(8,128)}, f32[8,128]{1,0:T(8,128)}) custom-call(f32[2,3]{1,0:T(2,128)S(1)} %copy-done.1, bf16[2560,256]{1,0:T(8,128)(2,1)} %get-tuple-element.30.refs_0_, bf16[160,256]{1,0:T(8,128)(2,1)S(1)} %bitcast.9, bf16[160,256]{1,0:T(8,128)(2,1)S(1)} %bitcast.11, bf16[8,2880]{1,0:T(8,128)(2,1)S(1)} %collective-permute-done.2.refs_3_, ...), custom_call_target="tpu_custom_call" | custom-call | flops 20000000000 | bytes 4000000 | tf_op jit(solution)/shard_map/conv/pallas_call | solution.py:495
  46.0 2.4 %all-to-all-done.1.gathered_ref = bf16[128,5,128]{2,1,0:T(8,128)(2,1)S(1)} async-done(((bf16[128,5,128]{2,1,0:T(8,128)(2,1)}), bf16[128,5,128]{2,1,0:T(8,128)(2,1)S(1)}, u32[]{:S(2)}, u32[]{:S(2)}) %all-to-all-start.1) | async-done | bytes 163872 | tf_op jit(solution)/shard_map/all_to_all | solution.py:512
  48.3 0.0 copy-done.2
  48.3 6.9 %middle.1 = (bf16[17,160,256]{2,1,0:T(8,128)(2,1)}, bf16[8,2720]{1,0:T(8,128)(2,1)S(1)}, bf16[8,2720]{1,0:T(8,128)(2,1)S(1)}, bf16[128,5,128]{2,1,0:T(8,128)(2,1)}) custom-call(f32[2,20]{1,0:T(2,128)S(1)} %copy-done.2, bf16[128,5,128]{2,1,0:T(8,128)(2,1)S(1)} %all-to-all-done.1.gathered_ref, bf16[2,8,2,64,512]{4,3,2,1,0:T(8,128)(2,1)} %constant.19.clone.icols_all, ...), custom_call_target="tpu_custom_call" | custom-call | flops 1000000000 | bytes 4000000 | tf_op jit(solution)/shard_map/middle/pallas_call | solution.py:495
  55.3 0.6 collective-permute-start.4
  55.9 3.6 %collective-permute-start.5 = (bf16[8,2720]{1,0:T(8,128)(2,1)S(1)}, bf16[8,2720]{1,0:T(8,128)(2,1)S(1)}, u32[]{:S(2)}, u32[]{:S(2)}) collective-permute-start(bf16[8,2720]{1,0:T(8,128)(2,1)S(1)} %get-tuple-element.43), channel_id=1, source_target_pairs={{0,7},{1,0},{2,1},{3,2},{4,3},{5,4},{6,5},{7,6},{8,15},{9,8},{10,9... | collective-permute-start | bytes 130568 | tf_op jit(solution)/shard_map/ppermute | solution.py:522
  59.5 5.3 %all-to-all-start.2 = ((bf16[128,5,128]{2,1,0:T(8,128)(2,1)}), bf16[128,5,128]{2,1,0:T(8,128)(2,1)S(1)}, u32[]{:S(2)}, u32[]{:S(2)}) async-start(bf16[128,5,128]{2,1,0:T(8,128)(2,1)} %get-tuple-element.40), calls=%async_computation.2 | async-start | bytes 524288 | tf_op jit(solution)/shard_map/all_to_all | solution.py:512
  64.8 0.0 collective-permute-done.4.refs_1_
  64.8 0.0 collective-permute-done.5.refs_2_
  64.9 6.6 %conv.4 = (f32[20,64,256]{2,1,0:T(8,128)}, f32[8,128]{1,0:T(8,128)S(1)}) custom-call(f32[2,3]{1,0:T(2,128)S(1)} %copy-done.1, bf16[2720,256]{1,0:T(8,128)(2,1)} %bitcast.14, bf16[8,2720]{1,0:T(8,128)(2,1)S(1)} %collective-permute-done.4.refs_1_, bf16[8,2720]{1,0:T(8,128)(2,1)S(1)} %collective-permute-done.5.refs_2_, ...), custom_call_target="tpu_custom_call" | custom-call | flops 20000000000 | bytes 4000000 | tf_op jit(solution)/shard_map/conv/pallas_call | solution.py:495
  71.5 3.8 %all-to-all-done.2.received_ref = bf16[128,5,128]{2,1,0:T(8,128)(2,1)S(1)} async-done(((bf16[128,5,128]{2,1,0:T(8,128)(2,1)}), bf16[128,5,128]{2,1,0:T(8,128)(2,1)S(1)}, u32[]{:S(2)}, u32[]{:S(2)}) %all-to-all-start.2) | async-done | bytes 163872 | tf_op jit(solution)/shard_map/all_to_all | solution.py:512
  75.3 1.3 %mix.3 = (bf16[128,5,128]{2,1,0:T(8,128)(2,1)}, f32[8,128]{1,0:T(8,128)S(1)}) custom-call(f32[2,3]{1,0:T(2,128)S(1)} %copy-done.1, bf16[128,5,128]{2,1,0:T(8,128)(2,1)S(1)} %all-to-all-done.2.received_ref, f32[2,2,20,16,20]{4,3,2,1,0:T(8,128)S(1)} %bitcast.7, f32[8,128]{1,0:T(8,128)S(1)} %get-tuple-element.44.order_ref), custom_call_target="tpu_custom_call" | custom-call | flops 1000000 | bytes 4000000 | tf_op jit(solution)/shard_map/mix/pallas_call | solution.py:495
  76.6 5.8 %all-to-all-start.3 = ((bf16[128,5,128]{2,1,0:T(8,128)(2,1)}), bf16[128,5,128]{2,1,0:T(8,128)(2,1)S(1)}, u32[]{:S(2)}, u32[]{:S(2)}) async-start(bf16[128,5,128]{2,1,0:T(8,128)(2,1)} %get-tuple-element.45), calls=%async_computation.3 | async-start | bytes 524288 | tf_op jit(solution)/shard_map/all_to_all | solution.py:512
  82.4 6.3 %conv.5 = (f32[20,64,256]{2,1,0:T(8,128)}, f32[8,128]{1,0:T(8,128)}) custom-call(f32[2,3]{1,0:T(2,128)S(1)} %copy-done.1, bf16[2720,256]{1,0:T(8,128)(2,1)} %bitcast.15, bf16[8,2720]{1,0:T(8,128)(2,1)S(1)} %collective-permute-done.4.refs_1_, bf16[8,2720]{1,0:T(8,128)(2,1)S(1)} %collective-permute-done.5.refs_2_, ...), custom_call_target="tpu_custom_call" | custom-call | flops 20000000000 | bytes 4000000 | tf_op jit(solution)/shard_map/conv/pallas_call | solution.py:495
  88.7 4.4 %all-to-all-done.3.gathered_ref = bf16[128,5,128]{2,1,0:T(8,128)(2,1)S(1)} async-done(((bf16[128,5,128]{2,1,0:T(8,128)(2,1)}), bf16[128,5,128]{2,1,0:T(8,128)(2,1)S(1)}, u32[]{:S(2)}, u32[]{:S(2)}) %all-to-all-start.3) | async-done | bytes 163872 | tf_op jit(solution)/shard_map/all_to_all | solution.py:512
  93.1 5.1 %last.1 = bf16[20,128,256]{2,1,0:T(8,128)(2,1)} custom-call(f32[2,20]{1,0:T(2,128)S(1)} %copy-done.2, bf16[128,5,128]{2,1,0:T(8,128)(2,1)S(1)} %all-to-all-done.3.gathered_ref, bf16[2,8,2,64,512]{4,3,2,1,0:T(8,128)(2,1)} %constant.19.clone.icols_all, bf16[2,16,2,136,128]{4,3,2,1,0:T(8,128)(2,1)} %constant.18.clone.irows_all, ...), custom_call_target="tpu_custom_call" | custom-call | flops 1000000000 | bytes 4000000 | tf_op jit(solution)/shard_map/last/pallas_call | solution.py:495
  (2 shorter events, 0.0 us)
Async XLA Ops:
  0.0 20.3 %copy-start.7 = (bf16[2,20,180]{2,0,1:T(2,128)(2,1)S(1)}, bf16[2,20,180]{2,0,1:T(2,128)(2,1)}, u32[]{:S(2)}) copy-start(bf16[2,20,180]{2,0,1:T(2,128)(2,1)} %param.16) | copy-start | bytes 43204
  0.0 20.3 %copy-start.6 = (bf16[2,20,500]{2,0,1:T(2,128)(2,1)S(1)}, bf16[2,20,500]{2,0,1:T(2,128)(2,1)}, u32[]{:S(2)}) copy-start(bf16[2,20,500]{2,0,1:T(2,128)(2,1)} %param.17) | copy-start | bytes 120004
  0.0 20.3 %copy-start.3 = (bf16[60,960]{1,0:T(8,128)(2,1)S(1)}, bf16[60,960]{1,0:T(8,128)(2,1)}, u32[]{:S(2)}) copy-start(bf16[60,960]{1,0:T(8,128)(2,1)} %constant.20.clone.near_spread.refs_5_) | copy-start | bytes 345604
  0.0 20.4 %copy-start.4 = (s32[8,1600]{1,0:T(8,128)S(1)}, s32[8,1600]{1,0:T(8,128)}, u32[]{:S(2)}) copy-start(s32[8,1600]{1,0:T(8,128)} %constant.23.clone.far_offsets.refs_8_) | copy-start | bytes 153604
  0.0 20.4 %copy-start.5 = (s32[8,960]{1,0:T(8,128)S(1)}, s32[8,960]{1,0:T(8,128)}, u32[]{:S(2)}) copy-start(s32[8,960]{1,0:T(8,128)} %constant.22.clone.near_offsets.refs_7_) | copy-start | bytes 92164
  3.7 28.0 %all-to-all-start = ((f32[128,5,128]{2,1,0:T(8,128)}), f32[128,5,128]{2,1,0:T(8,128)S(1)}, u32[]{:S(2)}, u32[]{:S(2)}) async-start(f32[128,5,128]{2,1,0:T(8,128)} %get-tuple-element.27), calls=%async_computation | async-start | bytes 1048576 | tf_op jit(solution)/shard_map/all_to_all | solution.py:512
  14.9 12.5 %collective-permute-start = (bf16[20,8,256]{2,1,0:T(8,128)(2,1)S(1)}, bf16[20,8,256]{2,1,0:T(8,128)(2,1)S(1)}, u32[]{:S(2)}, u32[]{:S(2)}) collective-permute-start(bf16[20,8,256]{2,1,0:T(8,128)(2,1)S(1)} %get-tuple-element.31), channel_id=1, source_target_pairs={{0,8},{8,16},{16,24},{24,32},{32,40},{40,48},{48,56},{56,64},{64,7... | collective-permute-start | bytes 245768 | tf_op jit(solution)/shard_map/ppermute | solution.py:555
  15.0 12.4 %collective-permute-start.1 = (bf16[20,8,256]{2,1,0:T(8,128)(2,1)S(1)}, bf16[20,8,256]{2,1,0:T(8,128)(2,1)S(1)}, u32[]{:S(2)}, u32[]{:S(2)}) collective-permute-start(bf16[20,8,256]{2,1,0:T(8,128)(2,1)S(1)} %get-tuple-element.29.order_ref), channel_id=1, source_target_pairs={{0,120},{8,0},{16,8},{24,16},{32,24},{40,32},{48,40},{56,48},{64,5... | collective-permute-start | bytes 245768 | tf_op jit(solution)/shard_map/ppermute | solution.py:556
  27.4 4.3 %copy-start = (f32[2,2,20,20,16]{3,4,2,1,0:T(8,128)S(1)}, f32[2,2,20,20,16]{3,4,2,1,0:T(8,128)}, u32[]{:S(2)}) copy-start(f32[2,2,20,20,16]{3,4,2,1,0:T(8,128)} %param.15) | copy-start | bytes 307204
  27.4 4.3 %copy-start.1 = (f32[2,3]{1,0:T(2,128)S(1)}, f32[2,3]{1,0:T(2,128)}, u32[]{:S(2)}) copy-start(f32[2,3]{1,0:T(2,128)} %logits_ref.9) | copy-start | bytes 76
  27.5 10.3 %collective-permute-start.2 = (bf16[8,2880]{1,0:T(8,128)(2,1)S(1)}, bf16[8,2880]{1,0:T(8,128)(2,1)S(1)}, u32[]{:S(2)}, u32[]{:S(2)}) collective-permute-start(bf16[8,2880]{1,0:T(8,128)(2,1)S(1)} %get-tuple-element.34), channel_id=1, source_target_pairs={{0,1},{1,2},{2,3},{3,4},{4,5},{5,6},{6,7},{7,0},{8,9},{9,10},{10,1... | collective-permute-start | bytes 138248 | tf_op jit(solution)/shard_map/ppermute | solution.py:521
  29.1 8.8 %collective-permute-start.3 = (bf16[8,2880]{1,0:T(8,128)(2,1)S(1)}, bf16[8,2880]{1,0:T(8,128)(2,1)S(1)}, u32[]{:S(2)}, u32[]{:S(2)}) collective-permute-start(bf16[8,2880]{1,0:T(8,128)(2,1)S(1)} %get-tuple-element.35), channel_id=1, source_target_pairs={{0,7},{1,0},{2,1},{3,2},{4,3},{5,4},{6,5},{7,6},{8,15},{9,8},{10,9... | collective-permute-start | bytes 138248 | tf_op jit(solution)/shard_map/ppermute | solution.py:522
  33.1 15.3 %all-to-all-start.1 = ((bf16[128,5,128]{2,1,0:T(8,128)(2,1)}), bf16[128,5,128]{2,1,0:T(8,128)(2,1)S(1)}, u32[]{:S(2)}, u32[]{:S(2)}) async-start(bf16[128,5,128]{2,1,0:T(8,128)(2,1)} %get-tuple-element.28), calls=%async_computation.1 | async-start | bytes 524288 | tf_op jit(solution)/shard_map/all_to_all | solution.py:512
  37.9 10.5 %copy-start.2 = (f32[2,20]{1,0:T(2,128)S(1)}, f32[2,20]{1,0:T(2,128)}, u32[]{:S(2)}) copy-start(f32[2,20]{1,0:T(2,128)} %bias_ref.3) | copy-start | bytes 484
  55.3 9.6 %collective-permute-start.4 = (bf16[8,2720]{1,0:T(8,128)(2,1)S(1)}, bf16[8,2720]{1,0:T(8,128)(2,1)S(1)}, u32[]{:S(2)}, u32[]{:S(2)}) collective-permute-start(bf16[8,2720]{1,0:T(8,128)(2,1)S(1)} %get-tuple-element.42), channel_id=1, source_target_pairs={{0,1},{1,2},{2,3},{3,4},{4,5},{5,6},{6,7},{7,0},{8,9},{9,10},{10,1... | collective-permute-start | bytes 130568 | tf_op jit(solution)/shard_map/ppermute | solution.py:521
  55.9 9.0 %collective-permute-start.5 = (bf16[8,2720]{1,0:T(8,128)(2,1)S(1)}, bf16[8,2720]{1,0:T(8,128)(2,1)S(1)}, u32[]{:S(2)}, u32[]{:S(2)}) collective-permute-start(bf16[8,2720]{1,0:T(8,128)(2,1)S(1)} %get-tuple-element.43), channel_id=1, source_target_pairs={{0,7},{1,0},{2,1},{3,2},{4,3},{5,4},{6,5},{7,6},{8,15},{9,8},{10,9... | collective-permute-start | bytes 130568 | tf_op jit(solution)/shard_map/ppermute | solution.py:522
  59.5 15.8 %all-to-all-start.2 = ((bf16[128,5,128]{2,1,0:T(8,128)(2,1)}), bf16[128,5,128]{2,1,0:T(8,128)(2,1)S(1)}, u32[]{:S(2)}, u32[]{:S(2)}) async-start(bf16[128,5,128]{2,1,0:T(8,128)(2,1)} %get-tuple-element.40), calls=%async_computation.2 | async-start | bytes 524288 | tf_op jit(solution)/shard_map/all_to_all | solution.py:512
  76.6 16.4 %all-to-all-start.3 = ((bf16[128,5,128]{2,1,0:T(8,128)(2,1)}), bf16[128,5,128]{2,1,0:T(8,128)(2,1)S(1)}, u32[]{:S(2)}, u32[]{:S(2)}) async-start(bf16[128,5,128]{2,1,0:T(8,128)(2,1)} %get-tuple-element.45), calls=%async_computation.3 | async-start | bytes 524288 | tf_op jit(solution)/shard_map/all_to_all | solution.py:512
